TPU v7x, 32 devices: a whole 2x2x4 slice. The times are simulated.
32 devices in a mesh: dp: 4 (over y, x), ctx: 8 (over z, core).
Axes of the slice: x: 2, y: 2, z: 4, core: 2. Of those that a mesh axis runs over, the one named last changes fastest.
Arguments:
- queries: bfloat16 [2048, 2048], P(('dp', 'ctx')), parts along dimension 0, may hold values from -10 to 10
- keys: bfloat16 [2048, 512], P(('dp', 'ctx')), parts along dimension 0, may hold values from -10 to 10
- values: bfloat16 [2048, 512], P(('dp', 'ctx')), parts along dimension 0, may hold values from -6 to 6
- block_order: int32 [64], P(('dp', 'ctx')), parts along dimension 0, may hold values from 0 to 15, as said below
- doc_lengths: int32 [16], P('dp'), parts along dimension 0, may hold values from 1 to 256, 512 in all
Outputs:
- attended: bfloat16 [2048, 2048], P(('dp', 'ctx')), parts along dimension 0
There are 4 independent parts, one for each index of `dp`. A program takes and returns all parts, laid end to end along the dimension named above; each array names one. Nothing has to cross between parts.
Inputs may be any that keep to these rules, and one draw needn't show every extreme that they name: Storage block j (rows j * 32 to j * 32 + 31) holds the tokens of window block block_order[j]; storage blocks 2 i and 2 i + 1 hold window blocks p and 15 - p for some p, in either order; every block once. `doc_lengths`: the window's documents in order; they sum to 512.
All inputs are finite; a program needn't handle non-finite values.
Results may differ from a plain program's by a relative error of at most 0.0045.
Values may be sent and summed in bfloat16 or wider, within the bound.
No kernel may reach another device: no remote copies, remote signals or barrier semaphores. Data moves between devices by JAX's collectives and lax.ppermute only.
A program may use at most 64 MiB of HBM per device.

v0:
```python
from functools import partial
import math

import jax
import jax.numpy as jnp
from jax import lax
from jax.sharding import PartitionSpec as P

QH = 16
KH = 4
HD = 128
BLOCK = 32


NEGATIVE = -1e30
STEP_ROWS = 512


def document_of(doc_ends, positions):
    return jnp.sum((doc_ends[None, :] <= positions[:, None]).astype(jnp.int32), axis=1)


def lookup(small_table, wanted):
    indices = jnp.arange(small_table.shape[0], dtype=jnp.int32)
    matches = wanted[:, None] == indices[None, :]
    return jnp.sum(jnp.where(matches, small_table[None, :], 0), axis=1)


def absorb(carried, query_rows, key_rows, value_rows, allowed, score_scale):
    running_top, running_sum, weighted = carried
    scores = (
        jnp.einsum("tgjd,sgd->tgjs", query_rows, key_rows, preferred_element_type=jnp.float32)
        * score_scale
    )
    pair_mask = allowed[:, None, None, :]
    masked = jnp.where(pair_mask, scores, NEGATIVE)
    new_top = jnp.maximum(running_top, jnp.max(masked, axis=-1))
    weights = jnp.where(pair_mask, jnp.exp(masked - new_top[..., None]), 0.0)
    factor = jnp.exp(running_top - new_top)
    running_sum = running_sum * factor + jnp.sum(weights, axis=-1)
    weighted = weighted * factor[..., None] + jnp.einsum(
        "tgjs,sgd->tgjd",
        weights.astype(jnp.bfloat16),
        value_rows,
        preferred_element_type=jnp.float32,
    )
    return (new_top, running_sum, weighted)


def unchanged(carried):
    return carried


def on_device(queries, keys, values, block_order, doc_lengths):
    heads_group = QH // KH
    score_scale = 1.0 / math.sqrt(HD)
    order_all = lax.all_gather(block_order, "ctx", axis=0, tiled=True)
    doc_ends = jnp.cumsum(doc_lengths)
    offsets = jnp.arange(BLOCK, dtype=jnp.int32)
    own_rows = queries.reshape(2, BLOCK, KH, heads_group, HD)
    slot_rows = [own_rows[0], own_rows[1]]
    slot_block = [block_order[0], block_order[1]]
    slot_live = [jnp.array(True), jnp.array(True)]
    slot_count = len(slot_rows)
    slot_pos = [block_index * BLOCK + offsets for block_index in slot_block]
    slot_doc = [document_of(doc_ends, place_rows) for place_rows in slot_pos]
    empty_state = (
        jnp.full((BLOCK, KH, heads_group), NEGATIVE, jnp.float32),
        jnp.zeros((BLOCK, KH, heads_group), jnp.float32),
        jnp.zeros((BLOCK, KH, heads_group, HD), jnp.float32),
    )
    initial = tuple((empty_state for slot_index in range(slot_count)))

    def take_rows(carried_all, key_rows, value_rows, key_pos, key_doc):
        row_count = key_rows.shape[0]
        key_heads = key_rows.reshape(row_count, KH, HD)
        value_heads = value_rows.reshape(row_count, KH, HD)
        results = []
        for slot_index in range(slot_count):
            allowed = (key_doc[None, :] == slot_doc[slot_index][:, None]) & (
                key_pos[None, :] <= slot_pos[slot_index][:, None]
            )
            needed = slot_live[slot_index] & jnp.any(allowed)
            update = partial(
                absorb,
                query_rows=slot_rows[slot_index],
                key_rows=key_heads,
                value_rows=value_heads,
                allowed=allowed,
                score_scale=score_scale,
            )
            results.append(lax.cond(needed, update, unchanged, carried_all[slot_index]))
        return tuple(results)

    def fold_piece(carried_all, piece):
        key_piece, value_piece = piece
        piece_rows = key_piece.shape[0]
        row_ids = jnp.arange(piece_rows, dtype=jnp.int32)
        key_block = lookup(order_all, row_ids // BLOCK)
        key_pos = key_block * BLOCK + row_ids % BLOCK
        key_doc = document_of(doc_ends, key_pos)
        if piece_rows > STEP_ROWS and piece_rows % STEP_ROWS == 0:

            def one_step(step_index, inner):
                first = step_index * STEP_ROWS
                return take_rows(
                    inner,
                    lax.dynamic_slice_in_dim(key_piece, first, STEP_ROWS, 0),
                    lax.dynamic_slice_in_dim(value_piece, first, STEP_ROWS, 0),
                    lax.dynamic_slice_in_dim(key_pos, first, STEP_ROWS, 0),
                    lax.dynamic_slice_in_dim(key_doc, first, STEP_ROWS, 0),
                )

            return lax.fori_loop(0, piece_rows // STEP_ROWS, one_step, carried_all)
        return take_rows(carried_all, key_piece, value_piece, key_pos, key_doc)

    folded = fold_piece(
        initial,
        (
            lax.all_gather(keys, "ctx", axis=0, tiled=True),
            lax.all_gather(values, "ctx", axis=0, tiled=True),
        ),
    )
    outputs = []
    for slot_index in range(slot_count):
        running_top, running_sum, weighted = folded[slot_index]
        safe_sum = jnp.where(running_sum > 0.0, running_sum, 1.0)
        outputs.append(
            (weighted / safe_sum[..., None]).astype(jnp.bfloat16).reshape(BLOCK, QH * HD)
        )
    first_out = outputs[0]
    second_out = outputs[1]
    return jnp.concatenate([first_out, second_out], axis=0)


def solution(mesh):
    return jax.shard_map(
        on_device,
        mesh=mesh,
        in_specs=(
            P(("dp", "ctx"), None),
            P(("dp", "ctx"), None),
            P(("dp", "ctx"), None),
            P(("dp", "ctx")),
            P("dp"),
        ),
        out_specs=P(("dp", "ctx"), None),
        check_vma=False,
    )
```

profile of v0, /device:TPU:0, one launch (start us, length us, event | category | flops | bytes accessed | tf_op | source)
XLA Modules:
  0.0 54.5 jit_solution(6925227718261533068)
XLA Ops:
  0.0 0.7 %copy-done.3 = u32[32]{0:T(128)S(1)} copy-done((u32[32]{0:T(128)S(1)}, u32[32]{0:T(128)}, u32[]{:S(2)}) %copy-start.3) | copy-done | bytes 152
  0.7 0.6 %dynamic-slice = u32[1]{0:T(128)} dynamic-slice(u32[32]{0:T(128)S(1)} %copy-done.3, u32[]{:T(128)S(6)} %add.68), dynamic_slice_sizes={1} | dynamic-slice | bytes 12
  1.9 0.8 %reduce-window.8 = s32[4,1]{0,1:T(1,128)S(1)} reduce-window(s32[4,1]{0,1:T(1,128)} %bitcast.53, s32[]{:T(128)} %constant.66.clone.1), window={size=4x1 pad=3_0x0_0}, to_apply=%region_0.0 | reduce-window | flops 12 | bytes 36 | tf_op jit(solution)/shard_map/reduce-window.3
  2.7 0.8 %dynamic-update-slice = s32[16]{0:T(128)S(1)} dynamic-update-slice(s32[16]{0:T(128)S(1)} %broadcast.145, s32[2]{0:T(128)} %param.12, u32[]{:T(128)} %bitcast.10) | dynamic-update-slice | bytes 20
  3.6 10.6 %all-reduce = s32[16]{0:T(128)S(1)} all-reduce(s32[16]{0:T(128)S(1)} %dynamic-update-slice), channel_id=1, replica_groups=mesh['dp'=4,'ctx'=8] {'ctx'}, use_global_device_ids=true, to_apply=%add | all-reduce | flops 16 | bytes 128
  14.2 1.4 %fusion.40 = (s32[1]{0:T(128)}, s32[1]{0:T(128)}) fusion(s32[2]{0:T(128)} %param.12), kind=kLoop, calls=%fused_computation.66 | loop fusion | bytes 16 | tf_op jit(solution)/shard_map/slice | solution.py:62
  16.9 0.1 convert_reduce_fusion.2
  17.0 0.1 select_reduce_fusion
  17.1 0.1 convert_reduce_fusion
  17.2 0.7 %fusion.36 = (pred[]{:T(512)}, pred[32,512]{1,0:T(8,128)(4,1)S(1)}, pred[]{:T(512)}, pred[32,512]{1,0:T(8,128)(4,1)S(1)}) fusion(s32[32]{0:T(128)S(1)} %get-tuple-element.84, s32[512]{0:T(512)S(1)} %fusion.32, s32[32]{0:T(128)S(1)} %get-tuple-element.65, s32[512]{0:T(512)S(1)} %convert_reduce_fusion, s32[32]{0:T(128)S(1)} %get-tuple-element.83, ...), kind=kLoop, calls=%fused_computation.62 | loop fusion | flops 131070 | bytes 37378 | tf_op jit(solution)/shard_map/reduce_or | solution.py:83
  19.1 14.8 %all_gather.10 = bf16[512,512]{1,0:T(8,128)(2,1)S(1)} all-gather(bf16[64,512]{1,0:T(8,128)(2,1)S(1)} %copy-done.1), channel_id=1, replica_groups=mesh['dp'=4,'ctx'=8] {'ctx'}, dimensions={0}, use_global_device_ids=true | all-gather | bytes 589824 | tf_op jit(solution)/shard_map/all_gather | solution.py:120
  34.0 0.2 copy.30
  34.2 0.6 %copy-done.2 = bf16[64,512]{1,0:T(8,128)(2,1)S(1)} copy-done((bf16[64,512]{1,0:T(8,128)(2,1)S(1)}, bf16[64,512]{1,0:T(8,128)(2,1)}, u32[]{:S(2)}) %copy-start.2) | copy-done | bytes 65560
  34.8 15.0 %all_gather.11 = bf16[512,512]{1,0:T(8,128)(2,1)S(1)} all-gather(bf16[64,512]{1,0:T(8,128)(2,1)S(1)} %copy-done.2), channel_id=1, replica_groups=mesh['dp'=4,'ctx'=8] {'ctx'}, dimensions={0}, use_global_device_ids=true | all-gather | bytes 589824 | tf_op jit(solution)/shard_map/all_gather | solution.py:121
  49.8 0.2 copy.31
  50.0 0.7 %copy-done = bf16[64,2048]{1,0:T(8,128)(2,1)S(1)} copy-done((bf16[64,2048]{1,0:T(8,128)(2,1)S(1)}, bf16[64,2048]{1,0:T(8,128)(2,1)}, u32[]{:S(2)}) %copy-start) | copy-done | bytes 262168
  50.7 1.2 %conditional.2 = (f32[32,4,4]{0,2,1:T(4,128)S(1)}, f32[32,4,4,128]{3,0,2,1:T(8,128)S(1)}) conditional(s32[]{:T(128)} %convert_element_type.29, () %tuple.21, (pred[32,512]{1,0:T(8,128)(4,1)S(1)}, bf16[64,2048]{1,0:T(8,128)(2,1)S(1)}, bf16[512,4,128]{0,2,1:T(8,128)(2,1)S(1)}, bf16[512,4,128]{0,2,1:T(8,128)(2,1)S(1)}) %tuple.50), branch_computations={%region_5.6_spmd, %region_6.9_spmd} | conditional | flops 136644096 | bytes 5183504 | solution.py:92
  50.7 0.1 squeeze.8
  50.8 0.4 fusion.38
  51.2 0.3 fusion.4
  51.6 0.4 fusion.2
  52.0 0.1 divide_convert_fusion.1
  52.1 0.1 copy.34
  52.2 0.1 reshape.118
  52.3 1.2 %conditional.3 = (f32[32,4,4]{0,2,1:T(4,128)S(1)}, f32[32,4,4,128]{3,0,2,1:T(8,128)S(1)}) conditional(s32[]{:T(128)} %convert_element_type.32, () %tuple.23, (pred[32,512]{1,0:T(8,128)(4,1)S(1)}, bf16[64,2048]{1,0:T(8,128)(2,1)S(1)}, bf16[512,4,128]{0,2,1:T(8,128)(2,1)S(1)}, bf16[512,4,128]{0,2,1:T(8,128)(2,1)S(1)}) %tuple.51), branch_computations={%region_11.12_spmd, %region_12.15_spmd} | conditional | flops 136644096 | bytes 5183504 | solution.py:92
  52.3 0.1 squeeze.9
  52.4 0.4 fusion.39
  52.8 0.3 fusion.18
  53.1 0.4 fusion.16
  53.5 0.1 divide_convert_fusion
  53.7 0.1 reshape.119
  53.8 0.7 %pad_maximum_fusion = bf16[64,2048]{1,0:T(8,128)(2,1)} fusion(bf16[32,2048]{1,0:T(8,128)(2,1)S(1)} %reshape.119, bf16[32,2048]{1,0:T(8,128)(2,1)S(1)} %reshape.118), kind=kLoop, calls=%fused_computation.36 | loop fusion | flops 524288 | bytes 524288 | tf_op jit(solution)/shard_map/concatenate | solution.py:133
  (18 shorter events, 0.2 us)
Async XLA Ops:
  0.0 0.7 %copy-start.3 = (u32[32]{0:T(128)S(1)}, u32[32]{0:T(128)}, u32[]{:S(2)}) copy-start(u32[32]{0:T(128)} %constant.79) | copy-start | bytes 388
  0.0 19.1 %copy-start.1 = (bf16[64,512]{1,0:T(8,128)(2,1)S(1)}, bf16[64,512]{1,0:T(8,128)(2,1)}, u32[]{:S(2)}) copy-start(bf16[64,512]{1,0:T(8,128)(2,1)} %param.10) | copy-start | bytes 196612
  34.0 0.8 %copy-start.2 = (bf16[64,512]{1,0:T(8,128)(2,1)S(1)}, bf16[64,512]{1,0:T(8,128)(2,1)}, u32[]{:S(2)}) copy-start(bf16[64,512]{1,0:T(8,128)(2,1)} %param.11) | copy-start | bytes 196612
  49.8 0.9 %copy-start = (bf16[64,2048]{1,0:T(8,128)(2,1)S(1)}, bf16[64,2048]{1,0:T(8,128)(2,1)}, u32[]{:S(2)}) copy-start(bf16[64,2048]{1,0:T(8,128)(2,1)} %param.9) | copy-start | bytes 786436
where the time goes:
time: 54.9 us; the launch traced here: 54.5 us
  blocking collectives  40.4 us (74%)
  local copies, waits for them, and re-layouts  5.71 us (10%)
  other arithmetic  3.58 us (7%)
  between operations  3.31 us (6%)
  matrix products  1.47 us (3%)
    all_gather x1, blocking collectives, on_device(): lax.all_gather(values, 'ctx', axis=0, tiled=True)  15 us
    all_gather x1, blocking collectives, on_device(): lax.all_gather(keys, 'ctx', axis=0, tiled=True)  14.8 us
    unnamed x1, blocking collectives  10.6 us
    unnamed x11, local copies, waits for them, and re-layouts  3.44 us
    slice x1, local copies, waits for them, and re-layouts, on_device(): slot_block = [block_order[0], block_order[1]]  1.39 us

commit v1 on v0

v1 whole, which is shorter than its diff:
```python
import math
from functools import partial

import jax
import jax.numpy as jnp
from jax import lax
from jax.experimental import pallas as pl
from jax.experimental.pallas import tpu as pltpu
from jax.sharding import PartitionSpec as P

QH = 16
KH = 4
HD = 128
BLOCK = 32
GROUP = QH // KH
TAG = 8
NEGATIVE = -1e30
VMEM = pl.BlockSpec(memory_space=pltpu.VMEM)
SMEM = pl.BlockSpec(memory_space=pltpu.SMEM)


def tag_kernel(order_ref, keys_ref, out_ref):
    rows, width = keys_ref.shape
    out_ref[:rows, :] = keys_ref[...]
    lane = lax.broadcasted_iota(jnp.int32, (TAG, width), 1)
    block = jnp.where((lane // BLOCK) % 2 == 0, order_ref[0], order_ref[1])
    out_ref[rows:, :] = block.astype(jnp.float32).astype(jnp.bfloat16)


def tag_keys(block_order, keys):
    rows, width = keys.shape
    return pl.pallas_call(
        tag_kernel,
        out_shape=jax.ShapeDtypeStruct((rows + TAG, width), keys.dtype),
        in_specs=[SMEM, VMEM],
        out_specs=VMEM,
        name="tag",
    )(block_order, keys)


def weights_kernel(count, order_ref, lengths_ref, queries_ref, *refs):
    key_refs = refs[:count]
    weights_ref, total_ref, keys_all, allowed_ref = refs[count:]
    rows = queries_ref.shape[0]
    tokens = count * rows
    for index in range(count):
        keys_all[index * rows : (index + 1) * rows, :] = key_refs[index][:rows, :]

    row = lax.broadcasted_iota(jnp.int32, (rows, 128), 0)
    query_pos = jnp.where(row < BLOCK, order_ref[0], order_ref[1]) * BLOCK + row % BLOCK
    first_pos = jnp.zeros_like(query_pos)
    end = 0
    for doc in range(lengths_ref.shape[0]):
        end = end + lengths_ref[doc]
        first_pos = jnp.where(query_pos >= end, end, first_pos)
    lane = lax.broadcasted_iota(jnp.int32, (TAG, 128), 1)
    for pair in range(count // 2):
        early = key_refs[2 * pair][rows:, :128].astype(jnp.float32)
        late = key_refs[2 * pair + 1][rows:, :128].astype(jnp.float32)
        block = jnp.where(lane < rows, early, late).astype(jnp.int32)
        key_pos = (block * BLOCK + lane % BLOCK)[:1, :]
        allowed = (key_pos >= first_pos) & (key_pos <= query_pos)
        allowed_ref[:, pair * 128 : (pair + 1) * 128] = jnp.where(allowed, 0.0, NEGATIVE)

    scale = math.log2(math.e) / math.sqrt(HD)
    for head in range(KH):
        keys_head = keys_all[:, head * HD : (head + 1) * HD]
        for inner in range(GROUP):
            at = (head * GROUP + inner) * HD
            scores = lax.dot_general(
                queries_ref[:, at : at + HD],
                keys_head,
                (((1,), (1,)), ((), ())),
                preferred_element_type=jnp.float32,
            )
            masked = jnp.where(allowed_ref[...] == 0.0, scores, NEGATIVE)
            top = jnp.max(masked, axis=1, keepdims=True)
            weights = jnp.exp2((masked - top) * scale)
            rows_at = slice(inner * rows, (inner + 1) * rows)
            total_ref[head, rows_at, :] = jnp.sum(weights, axis=1, keepdims=True)
            weights_ref[head, rows_at, :] = weights.astype(jnp.bfloat16)


def attention_weights(block_order, doc_lengths, queries, key_parts):
    count = len(key_parts)
    rows = queries.shape[0]
    tokens = count * rows
    work = KH * GROUP * rows * tokens
    return pl.pallas_call(
        partial(weights_kernel, count),
        out_shape=(
            jax.ShapeDtypeStruct((KH, GROUP * rows, tokens), jnp.bfloat16),
            jax.ShapeDtypeStruct((KH, GROUP * rows, 1), jnp.float32),
        ),
        in_specs=[SMEM, SMEM, VMEM] + [VMEM] * count,
        out_specs=(VMEM, VMEM),
        scratch_shapes=[
            pltpu.VMEM((tokens, KH * HD), jnp.bfloat16),
            pltpu.VMEM((rows, tokens), jnp.float32),
        ],
        compiler_params=pltpu.CompilerParams(vmem_limit_bytes=48 << 20),
        cost_estimate=pl.CostEstimate(
            flops=2 * work * HD, transcendentals=work, bytes_accessed=2 * work
        ),
        name="weights",
    )(block_order, doc_lengths, queries, *key_parts)


def mix_kernel(count, weights_ref, total_ref, *refs):
    value_refs = refs[:count]
    out_ref, values_all = refs[count:]
    rows = value_refs[0].shape[0]
    for index in range(count):
        values_all[index * rows : (index + 1) * rows, :] = value_refs[index][...]
    for head in range(KH):
        mixed = jnp.dot(
            weights_ref[head],
            values_all[:, head * HD : (head + 1) * HD],
            preferred_element_type=jnp.float32,
        )
        mixed = (mixed / total_ref[head]).astype(jnp.bfloat16)
        for inner in range(GROUP):
            at = (head * GROUP + inner) * HD
            out_ref[:, at : at + HD] = mixed[inner * rows : (inner + 1) * rows, :]


def mix_values(weights, total, value_parts):
    count = len(value_parts)
    rows = value_parts[0].shape[0]
    tokens = count * rows
    work = KH * GROUP * rows * tokens
    return pl.pallas_call(
        partial(mix_kernel, count),
        out_shape=jax.ShapeDtypeStruct((rows, QH * HD), jnp.bfloat16),
        in_specs=[VMEM, VMEM] + [VMEM] * count,
        out_specs=VMEM,
        scratch_shapes=[pltpu.VMEM((tokens, KH * HD), jnp.bfloat16)],
        compiler_params=pltpu.CompilerParams(vmem_limit_bytes=48 << 20),
        cost_estimate=pl.CostEstimate(
            flops=2 * work * HD, transcendentals=0, bytes_accessed=2 * work
        ),
        name="mix",
    )(weights, total, *value_parts)


def on_device(devices, queries, keys, values, block_order, doc_lengths):
    chips = devices // 2
    other_core = [(i, i ^ 1) for i in range(devices)]

    def from_chip(array, step):
        pairs = [
            (2 * chip + core, 2 * ((chip + step) % chips) + core)
            for chip in range(chips)
            for core in range(2)
        ]
        return lax.ppermute(array, "ctx", pairs)

    def across(array):
        return lax.ppermute(array, "ctx", other_core)

    tagged = tag_keys(block_order, keys)
    key_parts = [tagged] + [from_chip(tagged, step) for step in range(1, chips)]
    value_parts = [values] + [from_chip(values, step) for step in range(1, chips)]
    key_parts = key_parts + [across(part) for part in key_parts]
    value_parts = value_parts + [across(part) for part in value_parts]
    weights, total = attention_weights(block_order, doc_lengths, queries, key_parts)
    return mix_values(weights, total, value_parts)


def solution(mesh):
    return jax.shard_map(
        partial(on_device, mesh.shape["ctx"]),
        mesh=mesh,
        in_specs=(
            P(("dp", "ctx"), None),
            P(("dp", "ctx"), None),
            P(("dp", "ctx"), None),
            P(("dp", "ctx")),
            P("dp"),
        ),
        out_specs=P(("dp", "ctx"), None),
        check_vma=False,
    )
```

time: 54.9 us -> 27.7 us (0.50)
  blocking collectives: 40.4 us -> 0 us
  starting transfers between devices: 0 us -> 14.2 us
  waiting for transfers between devices: 0 us -> 7.03 us
  Pallas kernels: 0 us -> 4.3 us
  local copies, waits for them, and re-layouts: 5.71 us -> 1.84 us
  other arithmetic: 3.58 us -> 0 us
  between operations: 3.31 us -> 0.06 us
  matrix products: 1.47 us -> 0 us
    all_gather x2 -> x0, blocking collectives: 29.8 us -> none  [the longest x1 15 us: on_device(): lax.all_gather(values, 'ctx', axis=0, tiled=True)]
    ppermute x0 -> x14, starting transfers between devices: none -> 14.2 us  [the longest x6 12.7 us: from_chip(): return lax.ppermute(array, 'ctx', pairs)]
    unnamed x1 -> x0, blocking collectives: 10.6 us -> none
    ppermute x0 -> x14, waiting for transfers between devices: none -> 7.03 us  [the longest x6 7.01 us: from_chip(): return lax.ppermute(array, 'ctx', pairs)]
    pallas_call x0 -> x3, Pallas kernels: none -> 4.3 us  [the longest x1 1.59 us: attention_weights(): pl.pallas_call(partial(weights_kernel, count), out_shape=(jax.ShapeDtypeS...]
    unnamed x11 -> x10, local copies, waits for them, and re-layouts: 3.44 us -> 1.84 us
    dot_general x4 -> x0, matrix products: 1.47 us -> none  [the longest x2 0.76 us: absorb(): jnp.einsum('tgjd,sgd->tgjs', query_rows, key_rows, preferred_element_type...]
    slice x3 -> x0, local copies, waits for them, and re-layouts: 1.41 us -> none  [the longest x1 1.39 us: on_device(): slot_block = [block_order[0], block_order[1]]]
  transfers between devices with their start and end apart: 0 -> 14, of which waited for: 0 -> 4; matrix products, arithmetic and copies ran while one was open for 0% -> 0% of each run, Pallas kernels for 0% -> 6%
where the time goes in v1:
time: 27.7 us; the launch traced here: 27.5 us
  starting transfers between devices  14.2 us (51%)
  waiting for transfers between devices  7.03 us (25%)
  Pallas kernels  4.3 us (16%)
  local copies, waits for them, and re-layouts  1.84 us (7%)
    ppermute x6, starting transfers between devices, from_chip(): return lax.ppermute(array, 'ctx', pairs)  12.7 us
    ppermute x6, waiting for transfers between devices, from_chip(): return lax.ppermute(array, 'ctx', pairs)  7.01 us
    unnamed x10, local copies, waits for them, and re-layouts  1.84 us
    pallas_call x1, Pallas kernels, attention_weights(): pl.pallas_call(partial(weights_kernel, count), out_shape=(jax.ShapeDtypeS...  1.59 us
    ppermute x8, starting transfers between devices, across(): return lax.ppermute(array, 'ctx', other_core)  1.54 us
    pallas_call x1, Pallas kernels, tag_keys(): pl.pallas_call(tag_kernel, out_shape=jax.ShapeDtypeStruct((rows + TAG, wi...  1.53 us
    pallas_call x1, Pallas kernels, mix_values(): pl.pallas_call(partial(mix_kernel, count), out_shape=jax.ShapeDtypeStruct...  1.18 us
  transfers between devices with their start and end apart: 14, of which 4 were waited for; matrix products, arithmetic and copies ran while one was open for 0% of the time, Pallas kernels for 6%

profile of v1, /device:TPU:0, one launch (start us, length us, event | category | flops | bytes accessed | tf_op | source)
XLA Modules:
  0.0 27.5 jit_solution(8417114785578560242)
XLA Ops:
  0.0 1.5 %tag.1.refs_0_ = bf16[72,512]{1,0:T(8,128)(2,1)} custom-call(s32[2]{0:T(128)} %order_ref.3, bf16[64,512]{1,0:T(8,128)(2,1)} %keys_ref.1), custom_call_target="tpu_custom_call" | custom-call | tf_op jit(solution)/shard_map/tag/pallas_call | solution.py:32
  1.5 3.0 %collective-permute-start = (bf16[72,512]{1,0:T(8,128)(2,1)}, bf16[72,512]{1,0:T(8,128)(2,1)S(1)}, u32[]{:S(2)}, u32[]{:S(2)}) collective-permute-start(bf16[72,512]{1,0:T(8,128)(2,1)} %tag.1.refs_0_), channel_id=1, source_target_pairs={{0,2},{1,3},{2,4},{3,5},{4,6},{5,7},{6,0},{7,1},{8,10},{9,11},{10,... | collective-permute-start | bytes 221192 | tf_op jit(solution)/shard_map/ppermute | solution.py:156
  4.6 2.6 %collective-permute-start.1 = (bf16[72,512]{1,0:T(8,128)(2,1)}, bf16[72,512]{1,0:T(8,128)(2,1)S(1)}, u32[]{:S(2)}, u32[]{:S(2)}) collective-permute-start(bf16[72,512]{1,0:T(8,128)(2,1)} %tag.1.refs_0_), channel_id=1, source_target_pairs={{0,4},{1,5},{2,6},{3,7},{4,0},{5,1},{6,2},{7,3},{8,12},{9,13},{10,... | collective-permute-start | bytes 221192 | tf_op jit(solution)/shard_map/ppermute | solution.py:156
  7.2 0.0 collective-permute-start.7
  7.2 1.9 %collective-permute-start.8 = (bf16[64,512]{1,0:T(8,128)(2,1)S(1)}, bf16[64,512]{1,0:T(8,128)(2,1)S(1)}, u32[]{:S(2)}, u32[]{:S(2)}) collective-permute-start(bf16[64,512]{1,0:T(8,128)(2,1)S(1)} %copy-done.1), channel_id=1, source_target_pairs={{0,4},{1,5},{2,6},{3,7},{4,0},{5,1},{6,2},{7,3},{8,12},{9,13},{10,... | collective-permute-start | bytes 196616 | tf_op jit(solution)/shard_map/ppermute | solution.py:156
  9.1 1.9 %collective-permute-start.2 = (bf16[72,512]{1,0:T(8,128)(2,1)}, bf16[72,512]{1,0:T(8,128)(2,1)S(1)}, u32[]{:S(2)}, u32[]{:S(2)}) collective-permute-start(bf16[72,512]{1,0:T(8,128)(2,1)} %tag.1.refs_0_), channel_id=1, source_target_pairs={{0,6},{1,7},{2,0},{3,1},{4,2},{5,3},{6,4},{7,5},{8,14},{9,15},{10,... | collective-permute-start | bytes 221192 | tf_op jit(solution)/shard_map/ppermute | solution.py:156
  11.0 3.0 %collective-permute-done.7.refs_1_ = bf16[64,512]{1,0:T(8,128)(2,1)S(1)} collective-permute-done((bf16[64,512]{1,0:T(8,128)(2,1)S(1)}, bf16[64,512]{1,0:T(8,128)(2,1)S(1)}, u32[]{:S(2)}, u32[]{:S(2)}) %collective-permute-start.7) | collective-permute-done | bytes 65568 | tf_op jit(solution)/shard_map/ppermute | solution.py:156
  14.0 0.0 collective-permute-start.3
  14.0 0.0 collective-permute-done.refs_1_
  14.0 0.5 %collective-permute-start.4 = (bf16[72,512]{1,0:T(8,128)(2,1)S(1)}, bf16[72,512]{1,0:T(8,128)(2,1)S(1)}, u32[]{:S(2)}, u32[]{:S(2)}) collective-permute-start(bf16[72,512]{1,0:T(8,128)(2,1)S(1)} %collective-permute-done.refs_1_), channel_id=1, source_target_pairs={{0,1},{1,0},{2,3},{3,2},{4,5},{5,4},{6,7},{7,6},{8,9},{9,8},{10,11... | collective-permute-start | bytes 221192 | tf_op jit(solution)/shard_map/ppermute | solution.py:159
  14.5 0.7 %collective-permute-done.1.refs_2_ = bf16[72,512]{1,0:T(8,128)(2,1)S(1)} collective-permute-done((bf16[72,512]{1,0:T(8,128)(2,1)}, bf16[72,512]{1,0:T(8,128)(2,1)S(1)}, u32[]{:S(2)}, u32[]{:S(2)}) %collective-permute-start.1) | collective-permute-done | bytes 73760 | tf_op jit(solution)/shard_map/ppermute | solution.py:156
  15.3 0.0 collective-permute-start.5
  15.3 1.3 %collective-permute-done.8.refs_2_ = bf16[64,512]{1,0:T(8,128)(2,1)S(1)} collective-permute-done((bf16[64,512]{1,0:T(8,128)(2,1)S(1)}, bf16[64,512]{1,0:T(8,128)(2,1)S(1)}, u32[]{:S(2)}, u32[]{:S(2)}) %collective-permute-start.8) | collective-permute-done | bytes 65568 | tf_op jit(solution)/shard_map/ppermute | solution.py:156
  16.6 3.3 %collective-permute-start.9 = (bf16[64,512]{1,0:T(8,128)(2,1)S(1)}, bf16[64,512]{1,0:T(8,128)(2,1)S(1)}, u32[]{:S(2)}, u32[]{:S(2)}) collective-permute-start(bf16[64,512]{1,0:T(8,128)(2,1)S(1)} %copy-done.1), channel_id=1, source_target_pairs={{0,6},{1,7},{2,0},{3,1},{4,2},{5,3},{6,4},{7,5},{8,14},{9,15},{10,... | collective-permute-start | bytes 196616 | tf_op jit(solution)/shard_map/ppermute | solution.py:156
  19.9 0.0 collective-permute-done.2.refs_3_
  19.9 0.0 collective-permute-start.6
  19.9 1.9 %collective-permute-done.9.refs_3_ = bf16[64,512]{1,0:T(8,128)(2,1)S(1)} collective-permute-done((bf16[64,512]{1,0:T(8,128)(2,1)S(1)}, bf16[64,512]{1,0:T(8,128)(2,1)S(1)}, u32[]{:S(2)}, u32[]{:S(2)}) %collective-permute-start.9) | collective-permute-done | bytes 65568 | tf_op jit(solution)/shard_map/ppermute | solution.py:156
  21.8 0.0 collective-permute-start.10
  21.8 0.0 collective-permute-done.3.refs_4_
  21.8 0.5 %collective-permute-start.11 = (bf16[64,512]{1,0:T(8,128)(2,1)S(1)}, bf16[64,512]{1,0:T(8,128)(2,1)S(1)}, u32[]{:S(2)}, u32[]{:S(2)}) collective-permute-start(bf16[64,512]{1,0:T(8,128)(2,1)S(1)} %collective-permute-done.7.refs_1_), channel_id=1, source_target_pairs={{0,1},{1,0},{2,3},{3,2},{4,5},{5,4},{6,7},{7,6},{8,9},{9,8},{10,11... | collective-permute-start | bytes 196616 | tf_op jit(solution)/shard_map/ppermute | solution.py:159
  22.3 0.0 collective-permute-done.4.refs_5_
  22.3 0.1 collective-permute-start.12
  22.4 0.0 collective-permute-done.5.refs_6_
  22.4 0.4 %collective-permute-start.13 = (bf16[64,512]{1,0:T(8,128)(2,1)S(1)}, bf16[64,512]{1,0:T(8,128)(2,1)S(1)}, u32[]{:S(2)}, u32[]{:S(2)}) collective-permute-start(bf16[64,512]{1,0:T(8,128)(2,1)S(1)} %collective-permute-done.9.refs_3_), channel_id=1, source_target_pairs={{0,1},{1,0},{2,3},{3,2},{4,5},{5,4},{6,7},{7,6},{8,9},{9,8},{10,11... | collective-permute-start | bytes 196616 | tf_op jit(solution)/shard_map/ppermute | solution.py:159
  22.8 0.0 collective-permute-done.6.refs_7_
  22.8 0.0 copy-start
  22.8 0.9 %copy-done = bf16[72,512]{1,0:T(8,128)(2,1)S(1)} copy-done((bf16[72,512]{1,0:T(8,128)(2,1)S(1)}, bf16[72,512]{1,0:T(8,128)(2,1)}, u32[]{:S(2)}) %copy-start) | copy-done | bytes 73752
  23.7 0.9 %copy-done.3 = bf16[64,2048]{1,0:T(8,128)(2,1)S(1)} copy-done((bf16[64,2048]{1,0:T(8,128)(2,1)S(1)}, bf16[64,2048]{1,0:T(8,128)(2,1)}, u32[]{:S(2)}) %copy-start.3) | copy-done | bytes 262168
  24.7 1.6 %weights.1 = (bf16[4,256,512]{2,1,0:T(8,128)(2,1)S(1)}, f32[4,256,1]{2,1,0:T(8,128)S(1)}) custom-call(s32[2]{0:T(128)S(1)} %copy-done.2, s32[4]{0:T(128)S(1)} %copy-done.4, bf16[64,2048]{1,0:T(8,128)(2,1)S(1)} %copy-done.3, bf16[72,512]{1,0:T(8,128)(2,1)S(1)} %copy-done, bf16[72,512]{1,0:T(8,128)(2,1)S(1)} %collective-permute-done.refs_1_, ...), custom_call_target="tpu_custom_call" | custom-call | flops 134217728 | bytes 1048576 | tf_op jit(solution)/shard_map/weights/pallas_call | solution.py:89
  26.3 0.0 collective-permute-done.10.refs_4_
  26.3 0.0 collective-permute-done.13.refs_7_
  26.3 1.2 %mix.1 = bf16[64,2048]{1,0:T(8,128)(2,1)} custom-call(bf16[4,256,512]{2,1,0:T(8,128)(2,1)S(1)} %get-tuple-element.7.weights_ref, f32[4,256,1]{2,1,0:T(8,128)S(1)} %get-tuple-element.8.total_ref, bf16[64,512]{1,0:T(8,128)(2,1)S(1)} %copy-done.1, bf16[64,512]{1,0:T(8,128)(2,1)S(1)} %collective-permute-done.7.refs_1_, ...), custom_call_target="tpu_custom_call" | custom-call | flops 134217728 | bytes 1048576 | tf_op jit(solution)/shard_map/mix/pallas_call | solution.py:132
  (9 shorter events, 0.0 us)
Async XLA Ops:
  0.0 22.8 %copy-start.2 = (s32[2]{0:T(128)S(1)}, s32[2]{0:T(128)}, u32[]{:S(2)}) copy-start(s32[2]{0:T(128)} %order_ref.3) | copy-start | bytes 28
  0.0 7.2 %copy-start.1 = (bf16[64,512]{1,0:T(8,128)(2,1)S(1)}, bf16[64,512]{1,0:T(8,128)(2,1)}, u32[]{:S(2)}) copy-start(bf16[64,512]{1,0:T(8,128)(2,1)} %refs_0_.1) | copy-start | bytes 196612
  0.0 22.8 %copy-start.4 = (s32[4]{0:T(128)S(1)}, s32[4]{0:T(128)}, u32[]{:S(2)}) copy-start(s32[4]{0:T(128)} %lengths_ref.1) | copy-start | bytes 52
  1.5 12.5 %collective-permute-start = (bf16[72,512]{1,0:T(8,128)(2,1)}, bf16[72,512]{1,0:T(8,128)(2,1)S(1)}, u32[]{:S(2)}, u32[]{:S(2)}) collective-permute-start(bf16[72,512]{1,0:T(8,128)(2,1)} %tag.1.refs_0_), channel_id=1, source_target_pairs={{0,2},{1,3},{2,4},{3,5},{4,6},{5,7},{6,0},{7,1},{8,10},{9,11},{10,... | collective-permute-start | bytes 221192 | tf_op jit(solution)/shard_map/ppermute | solution.py:156
  4.6 10.7 %collective-permute-start.1 = (bf16[72,512]{1,0:T(8,128)(2,1)}, bf16[72,512]{1,0:T(8,128)(2,1)S(1)}, u32[]{:S(2)}, u32[]{:S(2)}) collective-permute-start(bf16[72,512]{1,0:T(8,128)(2,1)} %tag.1.refs_0_), channel_id=1, source_target_pairs={{0,4},{1,5},{2,6},{3,7},{4,0},{5,1},{6,2},{7,3},{8,12},{9,13},{10,... | collective-permute-start | bytes 221192 | tf_op jit(solution)/shard_map/ppermute | solution.py:156
  7.2 6.9 %collective-permute-start.7 = (bf16[64,512]{1,0:T(8,128)(2,1)S(1)}, bf16[64,512]{1,0:T(8,128)(2,1)S(1)}, u32[]{:S(2)}, u32[]{:S(2)}) collective-permute-start(bf16[64,512]{1,0:T(8,128)(2,1)S(1)} %copy-done.1), channel_id=1, source_target_pairs={{0,2},{1,3},{2,4},{3,5},{4,6},{5,7},{6,0},{7,1},{8,10},{9,11},{10,... | collective-permute-start | bytes 196616 | tf_op jit(solution)/shard_map/ppermute | solution.py:156
  7.2 9.4 %collective-permute-start.8 = (bf16[64,512]{1,0:T(8,128)(2,1)S(1)}, bf16[64,512]{1,0:T(8,128)(2,1)S(1)}, u32[]{:S(2)}, u32[]{:S(2)}) collective-permute-start(bf16[64,512]{1,0:T(8,128)(2,1)S(1)} %copy-done.1), channel_id=1, source_target_pairs={{0,4},{1,5},{2,6},{3,7},{4,0},{5,1},{6,2},{7,3},{8,12},{9,13},{10,... | collective-permute-start | bytes 196616 | tf_op jit(solution)/shard_map/ppermute | solution.py:156
  9.1 10.8 %collective-permute-start.2 = (bf16[72,512]{1,0:T(8,128)(2,1)}, bf16[72,512]{1,0:T(8,128)(2,1)S(1)}, u32[]{:S(2)}, u32[]{:S(2)}) collective-permute-start(bf16[72,512]{1,0:T(8,128)(2,1)} %tag.1.refs_0_), channel_id=1, source_target_pairs={{0,6},{1,7},{2,0},{3,1},{4,2},{5,3},{6,4},{7,5},{8,14},{9,15},{10,... | collective-permute-start | bytes 221192 | tf_op jit(solution)/shard_map/ppermute | solution.py:156
  14.0 7.8 %collective-permute-start.3 = (bf16[72,512]{1,0:T(8,128)(2,1)}, bf16[72,512]{1,0:T(8,128)(2,1)S(1)}, u32[]{:S(2)}, u32[]{:S(2)}) collective-permute-start(bf16[72,512]{1,0:T(8,128)(2,1)} %tag.1.refs_0_), channel_id=1, source_target_pairs={{0,1},{1,0},{2,3},{3,2},{4,5},{5,4},{6,7},{7,6},{8,9},{9,8},{10,11... | collective-permute-start | bytes 221192 | tf_op jit(solution)/shard_map/ppermute | solution.py:159
  14.0 8.3 %collective-permute-start.4 = (bf16[72,512]{1,0:T(8,128)(2,1)S(1)}, bf16[72,512]{1,0:T(8,128)(2,1)S(1)}, u32[]{:S(2)}, u32[]{:S(2)}) collective-permute-start(bf16[72,512]{1,0:T(8,128)(2,1)S(1)} %collective-permute-done.refs_1_), channel_id=1, source_target_pairs={{0,1},{1,0},{2,3},{3,2},{4,5},{5,4},{6,7},{7,6},{8,9},{9,8},{10,11... | collective-permute-start | bytes 221192 | tf_op jit(solution)/shard_map/ppermute | solution.py:159
  15.3 7.1 %collective-permute-start.5 = (bf16[72,512]{1,0:T(8,128)(2,1)S(1)}, bf16[72,512]{1,0:T(8,128)(2,1)S(1)}, u32[]{:S(2)}, u32[]{:S(2)}) collective-permute-start(bf16[72,512]{1,0:T(8,128)(2,1)S(1)} %collective-permute-done.1.refs_2_), channel_id=1, source_target_pairs={{0,1},{1,0},{2,3},{3,2},{4,5},{5,4},{6,7},{7,6},{8,9},{9,8},{10,11... | collective-permute-start | bytes 221192 | tf_op jit(solution)/shard_map/ppermute | solution.py:159
  16.6 5.2 %collective-permute-start.9 = (bf16[64,512]{1,0:T(8,128)(2,1)S(1)}, bf16[64,512]{1,0:T(8,128)(2,1)S(1)}, u32[]{:S(2)}, u32[]{:S(2)}) collective-permute-start(bf16[64,512]{1,0:T(8,128)(2,1)S(1)} %copy-done.1), channel_id=1, source_target_pairs={{0,6},{1,7},{2,0},{3,1},{4,2},{5,3},{6,4},{7,5},{8,14},{9,15},{10,... | collective-permute-start | bytes 196616 | tf_op jit(solution)/shard_map/ppermute | solution.py:156
  19.9 2.9 %collective-permute-start.6 = (bf16[72,512]{1,0:T(8,128)(2,1)S(1)}, bf16[72,512]{1,0:T(8,128)(2,1)S(1)}, u32[]{:S(2)}, u32[]{:S(2)}) collective-permute-start(bf16[72,512]{1,0:T(8,128)(2,1)S(1)} %collective-permute-done.2.refs_3_), channel_id=1, source_target_pairs={{0,1},{1,0},{2,3},{3,2},{4,5},{5,4},{6,7},{7,6},{8,9},{9,8},{10,11... | collective-permute-start | bytes 221192 | tf_op jit(solution)/shard_map/ppermute | solution.py:159
  21.8 4.5 %collective-permute-start.10 = (bf16[64,512]{1,0:T(8,128)(2,1)S(1)}, bf16[64,512]{1,0:T(8,128)(2,1)S(1)}, u32[]{:S(2)}, u32[]{:S(2)}) collective-permute-start(bf16[64,512]{1,0:T(8,128)(2,1)S(1)} %copy-done.1), channel_id=1, source_target_pairs={{0,1},{1,0},{2,3},{3,2},{4,5},{5,4},{6,7},{7,6},{8,9},{9,8},{10,11... | collective-permute-start | bytes 196616 | tf_op jit(solution)/shard_map/ppermute | solution.py:159
  21.8 4.5 %collective-permute-start.11 = (bf16[64,512]{1,0:T(8,128)(2,1)S(1)}, bf16[64,512]{1,0:T(8,128)(2,1)S(1)}, u32[]{:S(2)}, u32[]{:S(2)}) collective-permute-start(bf16[64,512]{1,0:T(8,128)(2,1)S(1)} %collective-permute-done.7.refs_1_), channel_id=1, source_target_pairs={{0,1},{1,0},{2,3},{3,2},{4,5},{5,4},{6,7},{7,6},{8,9},{9,8},{10,11... | collective-permute-start | bytes 196616 | tf_op jit(solution)/shard_map/ppermute | solution.py:159
  22.3 4.0 %collective-permute-start.12 = (bf16[64,512]{1,0:T(8,128)(2,1)S(1)}, bf16[64,512]{1,0:T(8,128)(2,1)S(1)}, u32[]{:S(2)}, u32[]{:S(2)}) collective-permute-start(bf16[64,512]{1,0:T(8,128)(2,1)S(1)} %collective-permute-done.8.refs_2_), channel_id=1, source_target_pairs={{0,1},{1,0},{2,3},{3,2},{4,5},{5,4},{6,7},{7,6},{8,9},{9,8},{10,11... | collective-permute-start | bytes 196616 | tf_op jit(solution)/shard_map/ppermute | solution.py:159
  22.4 3.9 %collective-permute-start.13 = (bf16[64,512]{1,0:T(8,128)(2,1)S(1)}, bf16[64,512]{1,0:T(8,128)(2,1)S(1)}, u32[]{:S(2)}, u32[]{:S(2)}) collective-permute-start(bf16[64,512]{1,0:T(8,128)(2,1)S(1)} %collective-permute-done.9.refs_3_), channel_id=1, source_target_pairs={{0,1},{1,0},{2,3},{3,2},{4,5},{5,4},{6,7},{7,6},{8,9},{9,8},{10,11... | collective-permute-start | bytes 196616 | tf_op jit(solution)/shard_map/ppermute | solution.py:159
  22.8 0.9 %copy-start = (bf16[72,512]{1,0:T(8,128)(2,1)S(1)}, bf16[72,512]{1,0:T(8,128)(2,1)}, u32[]{:S(2)}) copy-start(bf16[72,512]{1,0:T(8,128)(2,1)} %tag.1.refs_0_) | copy-start | bytes 221188
  23.7 0.9 %copy-start.3 = (bf16[64,2048]{1,0:T(8,128)(2,1)S(1)}, bf16[64,2048]{1,0:T(8,128)(2,1)}, u32[]{:S(2)}) copy-start(bf16[64,2048]{1,0:T(8,128)(2,1)} %queries_ref.1) | copy-start | bytes 786436

commit v2 on v1

v2 whole, which is shorter than its diff:
```python
import math
from functools import partial

import jax
import jax.numpy as jnp
from jax import lax
from jax.experimental import pallas as pl
from jax.experimental.pallas import tpu as pltpu
from jax.sharding import PartitionSpec as P

QH = 16
KH = 4
HD = 128
BLOCK = 32
GROUP = QH // KH
TAG = 8
NEGATIVE = -1e30
SCALE = math.log2(math.e) / math.sqrt(HD)
VMEM = pl.BlockSpec(memory_space=pltpu.VMEM)
SMEM = pl.BlockSpec(memory_space=pltpu.SMEM)
ANY = pl.BlockSpec(memory_space=pl.ANY)


def pack_kernel(order_ref, keys_ref, values_ref, out_ref, order, sems):
    rows, width = keys_ref.shape
    copies = (
        pltpu.make_async_copy(order_ref, order, sems.at[0]),
        pltpu.make_async_copy(keys_ref, out_ref.at[pl.ds(0, rows), pl.ds(0, width)], sems.at[1]),
        pltpu.make_async_copy(values_ref, out_ref.at[pl.ds(0, rows), pl.ds(width, width)], sems.at[2]),
    )
    for copy in copies:
        copy.start()
    copies[0].wait()
    lane = lax.broadcasted_iota(jnp.int32, (TAG, 2 * width), 1)
    block = jnp.where((lane // BLOCK) % 2 == 0, order[0], order[1])
    out_ref[rows:, :] = block.astype(jnp.float32).astype(jnp.bfloat16)
    copies[1].wait()
    copies[2].wait()


def pack(block_order, keys, values):
    rows, width = keys.shape
    return pl.pallas_call(
        pack_kernel,
        out_shape=pltpu.VMEM((rows + TAG, 2 * width), keys.dtype),
        in_specs=[ANY, ANY, ANY],
        out_specs=VMEM,
        scratch_shapes=[
            pltpu.SMEM(block_order.shape, jnp.int32),
            pltpu.SemaphoreType.DMA((3,)),
        ],
        name="pack",
    )(block_order, keys, values)


def stage_kernel(count, first, last, order_ref, lengths_ref, queries_ref, *refs):
    part_refs, refs = refs[:count], refs[count:]
    if not first:
        (top_in, total_in, mixed_in), refs = refs[:3], refs[3:]
    if last:
        out_ref, staged, sems = refs
    else:
        top_out, total_out, mixed_out = refs
    rows = queries_ref.shape[0]
    width = KH * HD

    row = lax.broadcasted_iota(jnp.int32, (rows, 128), 0)
    query_pos = jnp.where(row < BLOCK, order_ref[0], order_ref[1]) * BLOCK + row % BLOCK
    first_pos = jnp.zeros_like(query_pos)
    end = 0
    for doc in range(lengths_ref.shape[0]):
        end = end + lengths_ref[doc]
        first_pos = jnp.where(query_pos >= end, end, first_pos)
    lane = lax.broadcasted_iota(jnp.int32, (TAG, 128), 1)
    masks = []
    for pair in range(count // 2):
        early = part_refs[2 * pair][rows:, :128].astype(jnp.float32)
        late = part_refs[2 * pair + 1][rows:, :128].astype(jnp.float32)
        block = jnp.where(lane < rows, early, late).astype(jnp.int32)
        key_pos = (block * BLOCK + lane % BLOCK)[:1, :]
        allowed = (key_pos >= first_pos) & (key_pos <= query_pos)
        masks.append(jnp.where(allowed, 0.0, NEGATIVE))
    mask = jnp.concatenate(masks, axis=1)
    mask = jnp.concatenate([mask] * GROUP, axis=0)

    copies = []
    for head in range(KH):
        at = head * GROUP * HD
        queries = jnp.concatenate(
            [queries_ref[:, at + g * HD : at + (g + 1) * HD] for g in range(GROUP)], axis=0
        )
        keys = jnp.concatenate(
            [part[:rows, head * HD : (head + 1) * HD] for part in part_refs], axis=0
        )
        values = jnp.concatenate(
            [part[:rows, width + head * HD : width + (head + 1) * HD] for part in part_refs],
            axis=0,
        )
        scores = lax.dot_general(
            queries, keys, (((1,), (1,)), ((), ())), preferred_element_type=jnp.float32
        )
        scores = scores + mask
        top = jnp.max(scores, axis=1, keepdims=True)
        if not first:
            before = top_in[head]
            top = jnp.maximum(top, before[:, :1])
        weights = jnp.exp2((scores - top) * SCALE)
        total = jnp.broadcast_to(jnp.sum(weights, axis=1, keepdims=True), (GROUP * rows, HD))
        mixed = jnp.dot(weights.astype(jnp.bfloat16), values, preferred_element_type=jnp.float32)
        if not first:
            factor = jnp.exp2((before - top) * SCALE)
            total = total + total_in[head] * factor
            mixed = mixed + mixed_in[head] * factor
        if last:
            mixed = (mixed * (1.0 / total)).astype(jnp.bfloat16)
            for g in range(GROUP):
                staged[:, at + g * HD : at + (g + 1) * HD] = mixed[g * rows : (g + 1) * rows, :]
            columns = pl.ds(at, GROUP * HD)
            copy = pltpu.make_async_copy(staged.at[:, columns], out_ref.at[:, columns], sems.at[head])
            copy.start()
            copies.append(copy)
        else:
            top_out[head] = jnp.broadcast_to(top, (GROUP * rows, HD))
            total_out[head] = total
            mixed_out[head] = mixed
    for copy in copies:
        copy.wait()


def attend(block_order, doc_lengths, queries, parts, state, last):
    count = len(parts)
    rows = queries.shape[0]
    work = KH * GROUP * rows * count * rows
    out_shape = (jax.ShapeDtypeStruct((KH, GROUP * rows, HD), jnp.float32),) * 3
    if last:
        out_shape = jax.ShapeDtypeStruct(queries.shape, jnp.bfloat16)
    return pl.pallas_call(
        partial(stage_kernel, count, not state, last),
        out_shape=out_shape,
        in_specs=[SMEM, SMEM, VMEM] + [VMEM] * (count + len(state)),
        out_specs=ANY if last else (VMEM, VMEM, VMEM),
        scratch_shapes=[
            pltpu.VMEM(queries.shape, jnp.bfloat16),
            pltpu.SemaphoreType.DMA((KH,)),
        ]
        if last
        else [],
        compiler_params=pltpu.CompilerParams(vmem_limit_bytes=40 << 20),
        cost_estimate=pl.CostEstimate(
            flops=4 * work * HD, transcendentals=work, bytes_accessed=4 * work
        ),
        name="last_stage" if last else "stage",
    )(block_order, doc_lengths, queries, *parts, *state)


def on_device(devices, queries, keys, values, block_order, doc_lengths):
    chips = devices // 2
    other_core = [(i, i ^ 1) for i in range(devices)]
    paired = chips & (chips - 1) == 0

    def from_chip(array, step):
        pairs = []
        for chip in range(chips):
            other = chip ^ step if paired else (chip + step) % chips
            pairs += [(2 * chip + core, 2 * other + core) for core in range(2)]
        return lax.ppermute(array, "ctx", pairs)

    def across(array):
        return lax.ppermute(array, "ctx", other_core)

    own = pack(block_order, keys, values)
    steps = STEPS if chips == 4 else range(1, chips)
    arrived = [own] + [from_chip(own, step) for step in steps]
    state = ()
    groups = GROUPS if chips == 4 else [range(at, min(at + 4, chips)) for at in range(0, chips, 4)]
    for group in groups:
        parts = [half for index in group for half in (arrived[index], across(arrived[index]))]
        state = attend(block_order, doc_lengths, queries, parts, state, group is groups[-1])
    return state


STEPS = (2, 3, 1)
GROUPS = ((0, 3), (1, 2))


def solution(mesh):
    return jax.shard_map(
        partial(on_device, mesh.shape["ctx"]),
        mesh=mesh,
        in_specs=(
            P(("dp", "ctx"), None),
            P(("dp", "ctx"), None),
            P(("dp", "ctx"), None),
            P(("dp", "ctx")),
            P("dp"),
        ),
        out_specs=P(("dp", "ctx"), None),
        check_vma=False,
    )
```

time: 27.7 us -> 22.7 us (0.82)
  starting transfers between devices: 14.2 us -> 6.2 us
  waiting for transfers between devices: 7.03 us -> 11.4 us
  local copies, waits for them, and re-layouts: 1.84 us -> 0.01 us
  Pallas kernels: 4.3 us -> 4.88 us
    ppermute x6 -> x3, starting transfers between devices: 12.7 us -> 5.69 us  [from_chip(): return lax.ppermute(array, 'ctx', pairs)]
    ppermute x6 -> x3, waiting for transfers between devices: 7.01 us -> 11.4 us  [from_chip(): return lax.ppermute(array, 'ctx', pairs)]
    unnamed x10 -> x6, local copies, waits for them, and re-layouts: 1.84 us -> 0.01 us
    ppermute x8 -> x4, starting transfers between devices: 1.54 us -> 0.52 us  [across(): return lax.ppermute(array, 'ctx', other_core)]
    pallas_call x3, Pallas kernels: 4.3 us -> 4.88 us  [the longest x2 3.94 us: attend(): pl.pallas_call(partial(stage_kernel, count, not state, last), out_shape=o...]
  transfers between devices with their start and end apart: 14 -> 7, of which waited for: 4 -> 2; matrix products, arithmetic and copies ran while one was open for 0% -> 0% of each run, Pallas kernels for 6% -> 6%
where the time goes in v2:
time: 22.7 us; the launch traced here: 22.6 us
  waiting for transfers between devices  11.4 us (50%)
  starting transfers between devices  6.2 us (27%)
  Pallas kernels  4.88 us (21%)
    ppermute x3, waiting for transfers between devices, from_chip(): return lax.ppermute(array, 'ctx', pairs)  11.4 us
    ppermute x3, starting transfers between devices, from_chip(): return lax.ppermute(array, 'ctx', pairs)  5.69 us
    pallas_call x2, Pallas kernels, attend(): pl.pallas_call(partial(stage_kernel, count, not state, last), out_shape=o...  3.94 us
    pallas_call x1, Pallas kernels, pack(): pl.pallas_call(pack_kernel, out_shape=pltpu.VMEM((rows + TAG, 2 * width),...  0.94 us
    ppermute x4, starting transfers between devices, across(): return lax.ppermute(array, 'ctx', other_core)  0.52 us
  transfers between devices with their start and end apart: 7, of which 2 were waited for; matrix products, arithmetic and copies ran while one was open for 0% of the time, Pallas kernels for 6%

profile of v2, /device:TPU:0, one launch (start us, length us, event | category | flops | bytes accessed | tf_op | source)
XLA Modules:
  0.0 22.6 jit_solution(17862202491721047413)
XLA Ops:
  0.0 0.0 copy-start.1
  0.0 0.0 copy-start
  0.0 0.0 copy-start.2
  0.0 0.9 %pack.1.refs_0_ = bf16[72,1024]{1,0:T(8,128)(2,1)S(1)} custom-call(s32[2]{0:T(128)} %order_ref.5, bf16[64,512]{1,0:T(8,128)(2,1)} %keys_ref.1, bf16[64,512]{1,0:T(8,128)(2,1)} %values_ref.1), custom_call_target="tpu_custom_call" | custom-call | tf_op jit(solution)/shard_map/pack/pallas_call | solution.py:43
  1.0 3.1 %collective-permute-start.5 = (bf16[72,1024]{1,0:T(8,128)(2,1)S(1)}, bf16[72,1024]{1,0:T(8,128)(2,1)S(1)}, u32[]{:S(2)}, u32[]{:S(2)}) collective-permute-start(bf16[72,1024]{1,0:T(8,128)(2,1)S(1)} %pack.1.refs_0_), channel_id=1, source_target_pairs={{0,2},{1,3},{2,0},{3,1},{4,6},{5,7},{6,4},{7,5},{8,10},{9,11},{10,... | collective-permute-start | bytes 442376 | tf_op jit(solution)/shard_map/ppermute | solution.py:166
  4.0 2.6 %collective-permute-start = (bf16[72,1024]{1,0:T(8,128)(2,1)S(1)}, bf16[72,1024]{1,0:T(8,128)(2,1)S(1)}, u32[]{:S(2)}, u32[]{:S(2)}) collective-permute-start(bf16[72,1024]{1,0:T(8,128)(2,1)S(1)} %pack.1.refs_0_), channel_id=1, source_target_pairs={{0,4},{1,5},{2,6},{3,7},{4,0},{5,1},{6,2},{7,3},{8,12},{9,13},{10,... | collective-permute-start | bytes 442376 | tf_op jit(solution)/shard_map/ppermute | solution.py:166
  6.6 0.0 collective-permute-start.2
  6.6 0.0 collective-permute-start.4
  6.6 3.3 %collective-permute-done.5.refs_2_ = bf16[72,1024]{1,0:T(8,128)(2,1)S(1)} collective-permute-done((bf16[72,1024]{1,0:T(8,128)(2,1)S(1)}, bf16[72,1024]{1,0:T(8,128)(2,1)S(1)}, u32[]{:S(2)}, u32[]{:S(2)}) %collective-permute-start.5) | collective-permute-done | bytes 147488 | tf_op jit(solution)/shard_map/ppermute | solution.py:166
  9.9 0.0 collective-permute-start.6
  9.9 8.1 %collective-permute-done.refs_0_ = bf16[72,1024]{1,0:T(8,128)(2,1)S(1)} collective-permute-done((bf16[72,1024]{1,0:T(8,128)(2,1)S(1)}, bf16[72,1024]{1,0:T(8,128)(2,1)S(1)}, u32[]{:S(2)}, u32[]{:S(2)}) %collective-permute-start) | collective-permute-done | bytes 147488 | tf_op jit(solution)/shard_map/ppermute | solution.py:166
  18.0 0.0 collective-permute-start.1
  18.0 0.0 collective-permute-done.2.refs_2_
  18.1 0.5 %collective-permute-start.3 = (bf16[72,1024]{1,0:T(8,128)(2,1)S(1)}, bf16[72,1024]{1,0:T(8,128)(2,1)S(1)}, u32[]{:S(2)}, u32[]{:S(2)}) collective-permute-start(bf16[72,1024]{1,0:T(8,128)(2,1)S(1)} %collective-permute-done.2.refs_2_), channel_id=1, source_target_pairs={{0,1},{1,0},{2,3},{3,2},{4,5},{5,4},{6,7},{7,6},{8,9},{9,8},{10,11... | collective-permute-start | bytes 442376 | tf_op jit(solution)/shard_map/ppermute | solution.py:169
  18.6 0.0 collective-permute-done.4.refs_1_
  18.6 0.0 collective-permute-done.6.refs_3_
  18.6 0.0 copy-done.1
  18.6 0.0 copy-done
  18.6 0.0 copy-done.2
  18.6 1.4 %stage.1 = (f32[4,256,128]{2,1,0:T(8,128)S(1)}, f32[4,256,128]{2,1,0:T(8,128)S(1)}, f32[4,256,128]{2,1,0:T(8,128)S(1)}) custom-call(s32[2]{0:T(128)S(1)} %copy-done.1, s32[4]{0:T(128)S(1)} %copy-done.2, bf16[64,2048]{1,0:T(8,128)(2,1)S(1)} %copy-done, bf16[72,1024]{1,0:T(8,128)(2,1)S(1)} %pack.1.refs_0_, ...), custom_call_target="tpu_custom_call" | custom-call | flops 134217728 | bytes 1048576 | tf_op jit(solution)/shard_map/stage/pallas_call | solution.py:137
  20.0 0.0 collective-permute-done.1.refs_1_
  20.0 0.0 collective-permute-done.3.refs_3_
  20.0 2.6 %last_stage.1 = bf16[64,2048]{1,0:T(8,128)(2,1)} custom-call(s32[2]{0:T(128)S(1)} %copy-done.1, s32[4]{0:T(128)S(1)} %copy-done.2, bf16[64,2048]{1,0:T(8,128)(2,1)S(1)} %copy-done, bf16[72,1024]{1,0:T(8,128)(2,1)S(1)} %collective-permute-done.refs_0_, bf16[72,1024]{1,0:T(8,128)(2,1)S(1)} %collective-permute-done.1.refs_1_, ...), custom_call_target="tpu_custom_call" | custom-call | flops 134217728 | bytes 1048576 | tf_op jit(solution)/shard_map/last_stage/pallas_call | solution.py:137
Async XLA Ops:
  0.0 18.6 %copy-start.1 = (s32[2]{0:T(128)S(1)}, s32[2]{0:T(128)}, u32[]{:S(2)}) copy-start(s32[2]{0:T(128)} %order_ref.5) | copy-start | bytes 28
  0.0 18.6 %copy-start = (bf16[64,2048]{1,0:T(8,128)(2,1)S(1)}, bf16[64,2048]{1,0:T(8,128)(2,1)}, u32[]{:S(2)}) copy-start(bf16[64,2048]{1,0:T(8,128)(2,1)} %queries_ref.3) | copy-start | bytes 786436
  0.0 18.6 %copy-start.2 = (s32[4]{0:T(128)S(1)}, s32[4]{0:T(128)}, u32[]{:S(2)}) copy-start(s32[4]{0:T(128)} %lengths_ref.3) | copy-start | bytes 52
  1.0 8.9 %collective-permute-start.5 = (bf16[72,1024]{1,0:T(8,128)(2,1)S(1)}, bf16[72,1024]{1,0:T(8,128)(2,1)S(1)}, u32[]{:S(2)}, u32[]{:S(2)}) collective-permute-start(bf16[72,1024]{1,0:T(8,128)(2,1)S(1)} %pack.1.refs_0_), channel_id=1, source_target_pairs={{0,2},{1,3},{2,0},{3,1},{4,6},{5,7},{6,4},{7,5},{8,10},{9,11},{10,... | collective-permute-start | bytes 442376 | tf_op jit(solution)/shard_map/ppermute | solution.py:166
  4.0 14.0 %collective-permute-start = (bf16[72,1024]{1,0:T(8,128)(2,1)S(1)}, bf16[72,1024]{1,0:T(8,128)(2,1)S(1)}, u32[]{:S(2)}, u32[]{:S(2)}) collective-permute-start(bf16[72,1024]{1,0:T(8,128)(2,1)S(1)} %pack.1.refs_0_), channel_id=1, source_target_pairs={{0,4},{1,5},{2,6},{3,7},{4,0},{5,1},{6,2},{7,3},{8,12},{9,13},{10,... | collective-permute-start | bytes 442376 | tf_op jit(solution)/shard_map/ppermute | solution.py:166
  6.6 11.4 %collective-permute-start.2 = (bf16[72,1024]{1,0:T(8,128)(2,1)S(1)}, bf16[72,1024]{1,0:T(8,128)(2,1)S(1)}, u32[]{:S(2)}, u32[]{:S(2)}) collective-permute-start(bf16[72,1024]{1,0:T(8,128)(2,1)S(1)} %pack.1.refs_0_), channel_id=1, source_target_pairs={{0,6},{1,7},{2,4},{3,5},{4,2},{5,3},{6,0},{7,1},{8,14},{9,15},{10,... | collective-permute-start | bytes 442376 | tf_op jit(solution)/shard_map/ppermute | solution.py:166
  6.6 11.9 %collective-permute-start.4 = (bf16[72,1024]{1,0:T(8,128)(2,1)S(1)}, bf16[72,1024]{1,0:T(8,128)(2,1)S(1)}, u32[]{:S(2)}, u32[]{:S(2)}) collective-permute-start(bf16[72,1024]{1,0:T(8,128)(2,1)S(1)} %pack.1.refs_0_), channel_id=1, source_target_pairs={{0,1},{1,0},{2,3},{3,2},{4,5},{5,4},{6,7},{7,6},{8,9},{9,8},{10,11... | collective-permute-start | bytes 442376 | tf_op jit(solution)/shard_map/ppermute | solution.py:169
  9.9 8.7 %collective-permute-start.6 = (bf16[72,1024]{1,0:T(8,128)(2,1)S(1)}, bf16[72,1024]{1,0:T(8,128)(2,1)S(1)}, u32[]{:S(2)}, u32[]{:S(2)}) collective-permute-start(bf16[72,1024]{1,0:T(8,128)(2,1)S(1)} %collective-permute-done.5.refs_2_), channel_id=1, source_target_pairs={{0,1},{1,0},{2,3},{3,2},{4,5},{5,4},{6,7},{7,6},{8,9},{9,8},{10,11... | collective-permute-start | bytes 442376 | tf_op jit(solution)/shard_map/ppermute | solution.py:169
  18.0 1.9 %collective-permute-start.1 = (bf16[72,1024]{1,0:T(8,128)(2,1)S(1)}, bf16[72,1024]{1,0:T(8,128)(2,1)S(1)}, u32[]{:S(2)}, u32[]{:S(2)}) collective-permute-start(bf16[72,1024]{1,0:T(8,128)(2,1)S(1)} %collective-permute-done.refs_0_), channel_id=1, source_target_pairs={{0,1},{1,0},{2,3},{3,2},{4,5},{5,4},{6,7},{7,6},{8,9},{9,8},{10,11... | collective-permute-start | bytes 442376 | tf_op jit(solution)/shard_map/ppermute | solution.py:169
  18.1 1.9 %collective-permute-start.3 = (bf16[72,1024]{1,0:T(8,128)(2,1)S(1)}, bf16[72,1024]{1,0:T(8,128)(2,1)S(1)}, u32[]{:S(2)}, u32[]{:S(2)}) collective-permute-start(bf16[72,1024]{1,0:T(8,128)(2,1)S(1)} %collective-permute-done.2.refs_2_), channel_id=1, source_target_pairs={{0,1},{1,0},{2,3},{3,2},{4,5},{5,4},{6,7},{7,6},{8,9},{9,8},{10,11... | collective-permute-start | bytes 442376 | tf_op jit(solution)/shard_map/ppermute | solution.py:169

commit v3 on v2

v3 whole, which is shorter than its diff:
```python
import math
from functools import partial

import jax
import jax.numpy as jnp
from jax import lax
from jax.experimental import pallas as pl
from jax.experimental.pallas import tpu as pltpu
from jax.sharding import PartitionSpec as P

QH = 16
KH = 4
HD = 128
BLOCK = 32
GROUP = QH // KH
TAG = 8
NEGATIVE = -1e30
SCALE = math.log2(math.e) / math.sqrt(HD)
VMEM = pl.BlockSpec(memory_space=pltpu.VMEM)
ANY = pl.BlockSpec(memory_space=pl.ANY)


def pack_kernel(
    order_ref, lengths_ref, keys_ref, values_ref, packed_ref, span_ref, order, lengths, sems
):
    rows = keys_ref.shape[0]
    copies = [
        pltpu.make_async_copy(order_ref, order, sems.at[0]),
        pltpu.make_async_copy(lengths_ref, lengths, sems.at[1]),
    ]
    for index in range(2 * KH):
        source = keys_ref if index < KH else values_ref
        copies.append(
            pltpu.make_async_copy(
                source.at[:, pl.ds(index % KH * HD, HD)],
                packed_ref.at[pl.ds(index * rows, rows), :],
                sems.at[2 + index],
            )
        )
    for copy in copies:
        copy.start()
    copies[0].wait()
    copies[1].wait()
    lane = lax.broadcasted_iota(jnp.int32, (TAG, HD), 1)
    block = jnp.where((lane // BLOCK) % 2 == 0, order[0], order[1])
    packed_ref[2 * KH * rows :, :] = block.astype(jnp.float32).astype(jnp.bfloat16)
    row = lax.broadcasted_iota(jnp.int32, (rows, 128), 0)
    position = jnp.where(row < BLOCK, order[0], order[1]) * BLOCK + row % BLOCK
    first = jnp.zeros_like(position)
    end = 0
    for doc in range(lengths.shape[0]):
        end = end + lengths[doc]
        first = jnp.where(position >= end, end, first)
    span_ref[0] = first
    span_ref[1] = position
    for copy in copies[2:]:
        copy.wait()


def pack(block_order, doc_lengths, keys, values):
    rows = keys.shape[0]
    return pl.pallas_call(
        pack_kernel,
        out_shape=(
            pltpu.VMEM((2 * KH * rows + TAG, HD), keys.dtype),
            pltpu.VMEM((2, rows, 128), jnp.int32),
        ),
        in_specs=[ANY, ANY, ANY, ANY],
        out_specs=(VMEM, VMEM),
        scratch_shapes=[
            pltpu.SMEM(block_order.shape, jnp.int32),
            pltpu.SMEM(doc_lengths.shape, jnp.int32),
            pltpu.SemaphoreType.DMA((2 + 2 * KH,)),
        ],
        name="pack",
    )(block_order, doc_lengths, keys, values)


def fetch_kernel(queries_ref, out_ref, sem):
    copy = pltpu.make_async_copy(queries_ref, out_ref, sem)
    copy.start()
    copy.wait()


def fetch(queries):
    return pl.pallas_call(
        fetch_kernel,
        out_shape=pltpu.VMEM(queries.shape, queries.dtype),
        in_specs=[ANY],
        out_specs=VMEM,
        scratch_shapes=[pltpu.SemaphoreType.DMA],
        cost_estimate=pl.CostEstimate(
            flops=0, transcendentals=0, bytes_accessed=16 * queries.size
        ),
        name="fetch",
    )(queries)


def attend_kernel(count, span_ref, queries_ref, *refs):
    part_refs = refs[:count]
    out_ref, staged, sems = refs[count:]
    rows = queries_ref.shape[0]
    columns = GROUP * HD

    lane = lax.broadcasted_iota(jnp.int32, (TAG, 128), 1)
    masks = []
    for pair in range(count // 2):
        early = part_refs[2 * pair][2 * KH * rows :, :].astype(jnp.float32)
        late = part_refs[2 * pair + 1][2 * KH * rows :, :].astype(jnp.float32)
        block = jnp.where(lane < rows, early, late).astype(jnp.int32)
        position = (block * BLOCK + lane % BLOCK)[:1, :]
        allowed = (position >= span_ref[0]) & (position <= span_ref[1])
        masks.append(jnp.where(allowed, 0.0, NEGATIVE))
    mask = jnp.concatenate([jnp.concatenate(masks, axis=1)] * GROUP, axis=0)

    scores = []
    for head in range(KH):
        at = head * columns
        queries = jnp.concatenate(
            [queries_ref[:, at + g * HD : at + (g + 1) * HD] for g in range(GROUP)], axis=0
        )
        keys = jnp.concatenate(
            [part[head * rows : (head + 1) * rows, :] for part in part_refs], axis=0
        )
        scores.append(
            lax.dot_general(
                queries, keys, (((1,), (1,)), ((), ())), preferred_element_type=jnp.float32
            )
            + mask
        )
    weights, totals = [], []
    for head in range(KH):
        top = jnp.max(scores[head], axis=1, keepdims=True)
        weight = jnp.exp2((scores[head] - top) * SCALE)
        totals.append(jnp.sum(weight, axis=1, keepdims=True))
        weights.append(weight.astype(jnp.bfloat16))
    copies = []
    for head in range(KH):
        values = jnp.concatenate(
            [part[(KH + head) * rows : (KH + head + 1) * rows, :] for part in part_refs],
            axis=0,
        )
        mixed = jnp.dot(weights[head], values, preferred_element_type=jnp.float32)
        mixed = (mixed * (1.0 / totals[head])).astype(jnp.bfloat16)
        at = head * columns
        for g in range(GROUP):
            staged[:, at + g * HD : at + (g + 1) * HD] = mixed[g * rows : (g + 1) * rows, :]
        here = pl.ds(at, columns)
        copies.append(
            pltpu.make_async_copy(staged.at[:, here], out_ref.at[:, here], sems.at[head])
        )
        copies[head].start()
    for copy in copies:
        copy.wait()


def attend(span, queries, parts):
    count = len(parts)
    rows = queries.shape[0]
    work = KH * GROUP * rows * count * rows
    return pl.pallas_call(
        partial(attend_kernel, count),
        out_shape=jax.ShapeDtypeStruct(queries.shape, jnp.bfloat16),
        in_specs=[VMEM, VMEM] + [VMEM] * count,
        out_specs=ANY,
        scratch_shapes=[
            pltpu.VMEM(queries.shape, jnp.bfloat16),
            pltpu.SemaphoreType.DMA((KH,)),
        ],
        compiler_params=pltpu.CompilerParams(vmem_limit_bytes=40 << 20),
        cost_estimate=pl.CostEstimate(
            flops=4 * work * HD, transcendentals=work, bytes_accessed=4 * work
        ),
        name="attend",
    )(span, queries, *parts)


def on_device(devices, queries, keys, values, block_order, doc_lengths):
    chips = devices // 2
    other_core = [(i, i ^ 1) for i in range(devices)]
    paired = chips & (chips - 1) == 0

    def from_chip(array, step):
        pairs = []
        for chip in range(chips):
            other = chip ^ step if paired else (chip + step) % chips
            pairs += [(2 * chip + core, 2 * other + core) for core in range(2)]
        return lax.ppermute(array, "ctx", pairs)

    def across(array):
        return lax.ppermute(array, "ctx", other_core)

    own, span = pack(block_order, doc_lengths, keys, values)
    steps = STEPS if chips == 4 else range(1, chips)
    parts = []
    for part in [own] + [from_chip(own, step) for step in steps]:
        parts += [part, across(part)]
    return attend(span, fetch(queries), parts)


STEPS = (1, 3, 2)


def solution(mesh):
    return jax.shard_map(
        partial(on_device, mesh.shape["ctx"]),
        mesh=mesh,
        in_specs=(
            P(("dp", "ctx"), None),
            P(("dp", "ctx"), None),
            P(("dp", "ctx"), None),
            P(("dp", "ctx")),
            P("dp"),
        ),
        out_specs=P(("dp", "ctx"), None),
        check_vma=False,
    )
```

time: 22.7 us -> 19.6 us (0.86)
  the two profiles are of different devices: /device:TPU:0 before, /device:TPU:17 now
where the time goes in v3:
time: 19.6 us; the launch traced here: 19.4 us
  starting transfers between devices  8 us (41%)
  waiting for transfers between devices  7.88 us (40%)
  Pallas kernels  3.52 us (18%)
    ppermute x3, waiting for transfers between devices, from_chip(): return lax.ppermute(array, 'ctx', pairs)  7.53 us
    ppermute x4, starting transfers between devices, across(): return lax.ppermute(array, 'ctx', other_core)  4.39 us
    ppermute x3, starting transfers between devices, from_chip(): return lax.ppermute(array, 'ctx', pairs)  3.61 us
    pallas_call x1, Pallas kernels, attend(): pl.pallas_call(partial(attend_kernel, count), out_shape=jax.ShapeDtypeStr...  1.64 us
    pallas_call x1, Pallas kernels, fetch(): pl.pallas_call(fetch_kernel, out_shape=pltpu.VMEM(queries.shape, queries....  0.96 us
    pallas_call x1, Pallas kernels, pack(): pl.pallas_call(pack_kernel, out_shape=(pltpu.VMEM((2 * KH * rows + TAG, H...  0.92 us
  transfers between devices with their start and end apart: 7, of which 3 were waited for; matrix products, arithmetic and copies ran while one was open for 0% of the time, Pallas kernels for 5%

profile of v3, /device:TPU:17, one launch (start us, length us, event | category | flops | bytes accessed | tf_op | source)
XLA Modules:
  0.0 19.4 jit_solution(17471301759504760475)
XLA Ops:
  0.0 0.9 %pack.1 = (bf16[520,128]{1,0:T(8,128)(2,1)S(1)}, s32[2,64,128]{2,1,0:T(8,128)S(1)}) custom-call(s32[2]{0:T(128)} %order_ref.1, s32[4]{0:T(128)} %lengths_ref.1, bf16[64,512]{1,0:T(8,128)(2,1)} %keys_ref.1, bf16[64,512]{1,0:T(8,128)(2,1)} %values_ref.1), custom_call_target="tpu_custom_call" | custom-call | tf_op jit(solution)/shard_map/pack/pallas_call | solution.py:62
  0.9 0.1 collective-permute-start.5
  1.0 2.5 %collective-permute-start.3 = (bf16[520,128]{1,0:T(8,128)(2,1)S(1)}, bf16[520,128]{1,0:T(8,128)(2,1)S(1)}, u32[]{:S(2)}, u32[]{:S(2)}) collective-permute-start(bf16[520,128]{1,0:T(8,128)(2,1)S(1)} %get-tuple-element.8.refs_0_), channel_id=1, source_target_pairs={{0,6},{1,7},{2,4},{3,5},{4,2},{5,3},{6,0},{7,1},{8,14},{9,15},{10,... | collective-permute-start | bytes 399368 | tf_op jit(solution)/shard_map/ppermute | solution.py:188
  3.5 1.1 %collective-permute-start.1 = (bf16[520,128]{1,0:T(8,128)(2,1)S(1)}, bf16[520,128]{1,0:T(8,128)(2,1)S(1)}, u32[]{:S(2)}, u32[]{:S(2)}) collective-permute-start(bf16[520,128]{1,0:T(8,128)(2,1)S(1)} %get-tuple-element.8.refs_0_), channel_id=1, source_target_pairs={{0,2},{1,3},{2,0},{3,1},{4,6},{5,7},{6,4},{7,5},{8,10},{9,11},{10,... | collective-permute-start | bytes 399368 | tf_op jit(solution)/shard_map/ppermute | solution.py:188
  4.5 1.5 %collective-permute-start = (bf16[520,128]{1,0:T(8,128)(2,1)S(1)}, bf16[520,128]{1,0:T(8,128)(2,1)S(1)}, u32[]{:S(2)}, u32[]{:S(2)}) collective-permute-start(bf16[520,128]{1,0:T(8,128)(2,1)S(1)} %get-tuple-element.8.refs_0_), channel_id=1, source_target_pairs={{0,1},{1,0},{2,3},{3,2},{4,5},{5,4},{6,7},{7,6},{8,9},{9,8},{10,11... | collective-permute-start | bytes 399368 | tf_op jit(solution)/shard_map/ppermute | solution.py:191
  6.1 2.9 %collective-permute-done.5.refs_6_ = bf16[520,128]{1,0:T(8,128)(2,1)S(1)} collective-permute-done((bf16[520,128]{1,0:T(8,128)(2,1)S(1)}, bf16[520,128]{1,0:T(8,128)(2,1)S(1)}, u32[]{:S(2)}, u32[]{:S(2)}) %collective-permute-start.5) | collective-permute-done | bytes 133152 | tf_op jit(solution)/shard_map/ppermute | solution.py:188
  9.0 2.4 %collective-permute-start.6 = (bf16[520,128]{1,0:T(8,128)(2,1)S(1)}, bf16[520,128]{1,0:T(8,128)(2,1)S(1)}, u32[]{:S(2)}, u32[]{:S(2)}) collective-permute-start(bf16[520,128]{1,0:T(8,128)(2,1)S(1)} %collective-permute-done.5.refs_6_), channel_id=1, source_target_pairs={{0,1},{1,0},{2,3},{3,2},{4,5},{5,4},{6,7},{7,6},{8,9},{9,8},{10,11... | collective-permute-start | bytes 399368 | tf_op jit(solution)/shard_map/ppermute | solution.py:191
  11.3 4.6 %collective-permute-done.3.refs_4_ = bf16[520,128]{1,0:T(8,128)(2,1)S(1)} collective-permute-done((bf16[520,128]{1,0:T(8,128)(2,1)S(1)}, bf16[520,128]{1,0:T(8,128)(2,1)S(1)}, u32[]{:S(2)}, u32[]{:S(2)}) %collective-permute-start.3) | collective-permute-done | bytes 133152 | tf_op jit(solution)/shard_map/ppermute | solution.py:188
  16.0 0.5 %collective-permute-start.4 = (bf16[520,128]{1,0:T(8,128)(2,1)S(1)}, bf16[520,128]{1,0:T(8,128)(2,1)S(1)}, u32[]{:S(2)}, u32[]{:S(2)}) collective-permute-start(bf16[520,128]{1,0:T(8,128)(2,1)S(1)} %collective-permute-done.3.refs_4_), channel_id=1, source_target_pairs={{0,1},{1,0},{2,3},{3,2},{4,5},{5,4},{6,7},{7,6},{8,9},{9,8},{10,11... | collective-permute-start | bytes 399368 | tf_op jit(solution)/shard_map/ppermute | solution.py:191
  16.5 0.0 collective-permute-done.1.refs_2_
  16.5 0.0 collective-permute-start.2
  16.5 1.0 %fetch.1.queries_ref = bf16[64,2048]{1,0:T(8,128)(2,1)S(1)} custom-call(bf16[64,2048]{1,0:T(8,128)(2,1)} %queries_ref.1), custom_call_target="tpu_custom_call" | custom-call | bytes 2097152 | tf_op jit(solution)/shard_map/fetch/pallas_call | solution.py:86
  17.4 0.0 collective-permute-done.refs_1_
  17.5 0.0 collective-permute-done.6.refs_7_
  17.5 0.0 collective-permute-done.4.refs_5_
  17.5 0.3 %collective-permute-done.2.refs_3_ = bf16[520,128]{1,0:T(8,128)(2,1)S(1)} collective-permute-done((bf16[520,128]{1,0:T(8,128)(2,1)S(1)}, bf16[520,128]{1,0:T(8,128)(2,1)S(1)}, u32[]{:S(2)}, u32[]{:S(2)}) %collective-permute-start.2) | collective-permute-done | bytes 133152 | tf_op jit(solution)/shard_map/ppermute | solution.py:191
  17.8 1.6 %attend.1 = bf16[64,2048]{1,0:T(8,128)(2,1)} custom-call(s32[2,64,128]{2,1,0:T(8,128)S(1)} %get-tuple-element.7.span_ref, bf16[64,2048]{1,0:T(8,128)(2,1)S(1)} %fetch.1.queries_ref, bf16[520,128]{1,0:T(8,128)(2,1)S(1)} %get-tuple-element.8.refs_0_, bf16[520,128]{1,0:T(8,128)(2,1)S(1)} %collective-permute-done.refs_1_, ...), custom_call_target="tpu_custom_call" | custom-call | flops 268435456 | bytes 2097152 | tf_op jit(solution)/shard_map/attend/pallas_call | solution.py:161
Async XLA Ops:
  0.9 8.0 %collective-permute-start.5 = (bf16[520,128]{1,0:T(8,128)(2,1)S(1)}, bf16[520,128]{1,0:T(8,128)(2,1)S(1)}, u32[]{:S(2)}, u32[]{:S(2)}) collective-permute-start(bf16[520,128]{1,0:T(8,128)(2,1)S(1)} %get-tuple-element.8.refs_0_), channel_id=1, source_target_pairs={{0,4},{1,5},{2,6},{3,7},{4,0},{5,1},{6,2},{7,3},{8,12},{9,13},{10,... | collective-permute-start | bytes 399368 | tf_op jit(solution)/shard_map/ppermute | solution.py:188
  1.0 15.0 %collective-permute-start.3 = (bf16[520,128]{1,0:T(8,128)(2,1)S(1)}, bf16[520,128]{1,0:T(8,128)(2,1)S(1)}, u32[]{:S(2)}, u32[]{:S(2)}) collective-permute-start(bf16[520,128]{1,0:T(8,128)(2,1)S(1)} %get-tuple-element.8.refs_0_), channel_id=1, source_target_pairs={{0,6},{1,7},{2,4},{3,5},{4,2},{5,3},{6,0},{7,1},{8,14},{9,15},{10,... | collective-permute-start | bytes 399368 | tf_op jit(solution)/shard_map/ppermute | solution.py:188
  3.5 13.0 %collective-permute-start.1 = (bf16[520,128]{1,0:T(8,128)(2,1)S(1)}, bf16[520,128]{1,0:T(8,128)(2,1)S(1)}, u32[]{:S(2)}, u32[]{:S(2)}) collective-permute-start(bf16[520,128]{1,0:T(8,128)(2,1)S(1)} %get-tuple-element.8.refs_0_), channel_id=1, source_target_pairs={{0,2},{1,3},{2,0},{3,1},{4,6},{5,7},{6,4},{7,5},{8,10},{9,11},{10,... | collective-permute-start | bytes 399368 | tf_op jit(solution)/shard_map/ppermute | solution.py:188
  4.5 12.9 %collective-permute-start = (bf16[520,128]{1,0:T(8,128)(2,1)S(1)}, bf16[520,128]{1,0:T(8,128)(2,1)S(1)}, u32[]{:S(2)}, u32[]{:S(2)}) collective-permute-start(bf16[520,128]{1,0:T(8,128)(2,1)S(1)} %get-tuple-element.8.refs_0_), channel_id=1, source_target_pairs={{0,1},{1,0},{2,3},{3,2},{4,5},{5,4},{6,7},{7,6},{8,9},{9,8},{10,11... | collective-permute-start | bytes 399368 | tf_op jit(solution)/shard_map/ppermute | solution.py:191
  9.0 8.5 %collective-permute-start.6 = (bf16[520,128]{1,0:T(8,128)(2,1)S(1)}, bf16[520,128]{1,0:T(8,128)(2,1)S(1)}, u32[]{:S(2)}, u32[]{:S(2)}) collective-permute-start(bf16[520,128]{1,0:T(8,128)(2,1)S(1)} %collective-permute-done.5.refs_6_), channel_id=1, source_target_pairs={{0,1},{1,0},{2,3},{3,2},{4,5},{5,4},{6,7},{7,6},{8,9},{9,8},{10,11... | collective-permute-start | bytes 399368 | tf_op jit(solution)/shard_map/ppermute | solution.py:191
  16.0 1.5 %collective-permute-start.4 = (bf16[520,128]{1,0:T(8,128)(2,1)S(1)}, bf16[520,128]{1,0:T(8,128)(2,1)S(1)}, u32[]{:S(2)}, u32[]{:S(2)}) collective-permute-start(bf16[520,128]{1,0:T(8,128)(2,1)S(1)} %collective-permute-done.3.refs_4_), channel_id=1, source_target_pairs={{0,1},{1,0},{2,3},{3,2},{4,5},{5,4},{6,7},{7,6},{8,9},{9,8},{10,11... | collective-permute-start | bytes 399368 | tf_op jit(solution)/shard_map/ppermute | solution.py:191
  16.5 1.4 %collective-permute-start.2 = (bf16[520,128]{1,0:T(8,128)(2,1)S(1)}, bf16[520,128]{1,0:T(8,128)(2,1)S(1)}, u32[]{:S(2)}, u32[]{:S(2)}) collective-permute-start(bf16[520,128]{1,0:T(8,128)(2,1)S(1)} %collective-permute-done.1.refs_2_), channel_id=1, source_target_pairs={{0,1},{1,0},{2,3},{3,2},{4,5},{5,4},{6,7},{7,6},{8,9},{9,8},{10,11... | collective-permute-start | bytes 399368 | tf_op jit(solution)/shard_map/ppermute | solution.py:191

commit v4 on v3

--- a/solution.py
+++ b/solution.py
@@ -178,27 +178,30 @@
 def on_device(devices, queries, keys, values, block_order, doc_lengths):
     chips = devices // 2
     other_core = [(i, i ^ 1) for i in range(devices)]
-    paired = chips & (chips - 1) == 0
-
-    def from_chip(array, step):
-        pairs = []
-        for chip in range(chips):
-            other = chip ^ step if paired else (chip + step) % chips
-            pairs += [(2 * chip + core, 2 * other + core) for core in range(2)]
+    if chips == 4:
+        routes = ROUTES
+    elif chips & (chips - 1) == 0:
+        routes = [[chip ^ step for chip in range(chips)] for step in range(1, chips)]
+    else:
+        routes = [[(chip + step) % chips for chip in range(chips)] for step in range(1, chips)]
+
+    def along(array, route):
+        pairs = [
+            (2 * chip + core, 2 * route[chip] + core) for chip in range(chips) for core in range(2)
+        ]
         return lax.ppermute(array, "ctx", pairs)
 
     def across(array):
         return lax.ppermute(array, "ctx", other_core)
 
     own, span = pack(block_order, doc_lengths, keys, values)
-    steps = STEPS if chips == 4 else range(1, chips)
     parts = []
-    for part in [own] + [from_chip(own, step) for step in steps]:
+    for part in [own] + [along(own, route) for route in routes]:
         parts += [part, across(part)]
     return attend(span, fetch(queries), parts)
 
 
-STEPS = (1, 3, 2)
+ROUTES = ((1, 0, 3, 2), (2, 3, 1, 0), (3, 2, 0, 1))
 
 
 def solution(mesh):

time: 19.6 us -> 18.9 us (0.964)
  the two profiles are of different devices: /device:TPU:17 before, /device:TPU:0 now
where the time goes in v4:
time: 18.9 us; the launch traced here: 18.7 us
  waiting for transfers between devices  8.5 us (45%)
  starting transfers between devices  6.58 us (35%)
  Pallas kernels  3.52 us (19%)
    ppermute x3, waiting for transfers between devices, along(): return lax.ppermute(array, 'ctx', pairs)  8.21 us
    ppermute x3, starting transfers between devices, along(): return lax.ppermute(array, 'ctx', pairs)  6 us
    pallas_call x1, Pallas kernels, attend(): pl.pallas_call(partial(attend_kernel, count), out_shape=jax.ShapeDtypeStr...  1.64 us
    pallas_call x1, Pallas kernels, fetch(): pl.pallas_call(fetch_kernel, out_shape=pltpu.VMEM(queries.shape, queries....  0.96 us
    pallas_call x1, Pallas kernels, pack(): pl.pallas_call(pack_kernel, out_shape=(pltpu.VMEM((2 * KH * rows + TAG, H...  0.92 us
    ppermute x4, starting transfers between devices, across(): return lax.ppermute(array, 'ctx', other_core)  0.58 us
  transfers between devices with their start and end apart: 7, of which 2 were waited for; matrix products, arithmetic and copies ran while one was open for 0% of the time, Pallas kernels for 5%

profile of v4, /device:TPU:0, one launch (start us, length us, event | category | flops | bytes accessed | tf_op | source)
XLA Modules:
  0.0 18.7 jit_solution(1521227487070385141)
XLA Ops:
  0.0 0.9 %pack.1 = (bf16[520,128]{1,0:T(8,128)(2,1)S(1)}, s32[2,64,128]{2,1,0:T(8,128)S(1)}) custom-call(s32[2]{0:T(128)} %order_ref.1, s32[4]{0:T(128)} %lengths_ref.1, bf16[64,512]{1,0:T(8,128)(2,1)} %keys_ref.1, bf16[64,512]{1,0:T(8,128)(2,1)} %values_ref.1), custom_call_target="tpu_custom_call" | custom-call | tf_op jit(solution)/shard_map/pack/pallas_call | solution.py:62
  0.9 5.1 %collective-permute-start.5 = (bf16[520,128]{1,0:T(8,128)(2,1)S(1)}, bf16[520,128]{1,0:T(8,128)(2,1)S(1)}, u32[]{:S(2)}, u32[]{:S(2)}) collective-permute-start(bf16[520,128]{1,0:T(8,128)(2,1)S(1)} %get-tuple-element.8.refs_0_), channel_id=1, source_target_pairs={{0,6},{1,7},{2,4},{3,5},{4,0},{5,1},{6,2},{7,3},{8,14},{9,15},{10,... | collective-permute-start | bytes 399368 | tf_op jit(solution)/shard_map/ppermute | solution.py:192
  6.0 0.0 collective-permute-start.3
  6.0 0.9 %collective-permute-start.1 = (bf16[520,128]{1,0:T(8,128)(2,1)S(1)}, bf16[520,128]{1,0:T(8,128)(2,1)S(1)}, u32[]{:S(2)}, u32[]{:S(2)}) collective-permute-start(bf16[520,128]{1,0:T(8,128)(2,1)S(1)} %get-tuple-element.8.refs_0_), channel_id=1, source_target_pairs={{0,2},{1,3},{2,0},{3,1},{4,6},{5,7},{6,4},{7,5},{8,10},{9,11},{10,... | collective-permute-start | bytes 399368 | tf_op jit(solution)/shard_map/ppermute | solution.py:192
  6.9 0.0 collective-permute-start
  6.9 8.2 %collective-permute-done.5.refs_6_ = bf16[520,128]{1,0:T(8,128)(2,1)S(1)} collective-permute-done((bf16[520,128]{1,0:T(8,128)(2,1)S(1)}, bf16[520,128]{1,0:T(8,128)(2,1)S(1)}, u32[]{:S(2)}, u32[]{:S(2)}) %collective-permute-start.5) | collective-permute-done | bytes 133152 | tf_op jit(solution)/shard_map/ppermute | solution.py:192
  15.1 0.0 collective-permute-start.6
  15.1 0.0 collective-permute-done.3.refs_4_
  15.1 0.5 %collective-permute-start.4 = (bf16[520,128]{1,0:T(8,128)(2,1)S(1)}, bf16[520,128]{1,0:T(8,128)(2,1)S(1)}, u32[]{:S(2)}, u32[]{:S(2)}) collective-permute-start(bf16[520,128]{1,0:T(8,128)(2,1)S(1)} %collective-permute-done.3.refs_4_), channel_id=1, source_target_pairs={{0,1},{1,0},{2,3},{3,2},{4,5},{5,4},{6,7},{7,6},{8,9},{9,8},{10,11... | collective-permute-start | bytes 399368 | tf_op jit(solution)/shard_map/ppermute | solution.py:195
  15.7 0.0 collective-permute-done.1.refs_2_
  15.7 0.1 collective-permute-start.2
  15.7 1.0 %fetch.1.queries_ref = bf16[64,2048]{1,0:T(8,128)(2,1)S(1)} custom-call(bf16[64,2048]{1,0:T(8,128)(2,1)} %queries_ref.1), custom_call_target="tpu_custom_call" | custom-call | bytes 2097152 | tf_op jit(solution)/shard_map/fetch/pallas_call | solution.py:86
  16.7 0.0 collective-permute-done.refs_1_
  16.7 0.0 collective-permute-done.6.refs_7_
  16.7 0.0 collective-permute-done.4.refs_5_
  16.7 0.3 %collective-permute-done.2.refs_3_ = bf16[520,128]{1,0:T(8,128)(2,1)S(1)} collective-permute-done((bf16[520,128]{1,0:T(8,128)(2,1)S(1)}, bf16[520,128]{1,0:T(8,128)(2,1)S(1)}, u32[]{:S(2)}, u32[]{:S(2)}) %collective-permute-start.2) | collective-permute-done | bytes 133152 | tf_op jit(solution)/shard_map/ppermute | solution.py:195
  17.0 1.6 %attend.1 = bf16[64,2048]{1,0:T(8,128)(2,1)} custom-call(s32[2,64,128]{2,1,0:T(8,128)S(1)} %get-tuple-element.7.span_ref, bf16[64,2048]{1,0:T(8,128)(2,1)S(1)} %fetch.1.queries_ref, bf16[520,128]{1,0:T(8,128)(2,1)S(1)} %get-tuple-element.8.refs_0_, bf16[520,128]{1,0:T(8,128)(2,1)S(1)} %collective-permute-done.refs_1_, ...), custom_call_target="tpu_custom_call" | custom-call | flops 268435456 | bytes 2097152 | tf_op jit(solution)/shard_map/attend/pallas_call | solution.py:161
Async XLA Ops:
  0.9 14.2 %collective-permute-start.5 = (bf16[520,128]{1,0:T(8,128)(2,1)S(1)}, bf16[520,128]{1,0:T(8,128)(2,1)S(1)}, u32[]{:S(2)}, u32[]{:S(2)}) collective-permute-start(bf16[520,128]{1,0:T(8,128)(2,1)S(1)} %get-tuple-element.8.refs_0_), channel_id=1, source_target_pairs={{0,6},{1,7},{2,4},{3,5},{4,0},{5,1},{6,2},{7,3},{8,14},{9,15},{10,... | collective-permute-start | bytes 399368 | tf_op jit(solution)/shard_map/ppermute | solution.py:192
  6.0 9.1 %collective-permute-start.3 = (bf16[520,128]{1,0:T(8,128)(2,1)S(1)}, bf16[520,128]{1,0:T(8,128)(2,1)S(1)}, u32[]{:S(2)}, u32[]{:S(2)}) collective-permute-start(bf16[520,128]{1,0:T(8,128)(2,1)S(1)} %get-tuple-element.8.refs_0_), channel_id=1, source_target_pairs={{0,4},{1,5},{2,6},{3,7},{4,2},{5,3},{6,0},{7,1},{8,12},{9,13},{10,... | collective-permute-start | bytes 399368 | tf_op jit(solution)/shard_map/ppermute | solution.py:192
  6.0 9.6 %collective-permute-start.1 = (bf16[520,128]{1,0:T(8,128)(2,1)S(1)}, bf16[520,128]{1,0:T(8,128)(2,1)S(1)}, u32[]{:S(2)}, u32[]{:S(2)}) collective-permute-start(bf16[520,128]{1,0:T(8,128)(2,1)S(1)} %get-tuple-element.8.refs_0_), channel_id=1, source_target_pairs={{0,2},{1,3},{2,0},{3,1},{4,6},{5,7},{6,4},{7,5},{8,10},{9,11},{10,... | collective-permute-start | bytes 399368 | tf_op jit(solution)/shard_map/ppermute | solution.py:192
  6.9 9.8 %collective-permute-start = (bf16[520,128]{1,0:T(8,128)(2,1)S(1)}, bf16[520,128]{1,0:T(8,128)(2,1)S(1)}, u32[]{:S(2)}, u32[]{:S(2)}) collective-permute-start(bf16[520,128]{1,0:T(8,128)(2,1)S(1)} %get-tuple-element.8.refs_0_), channel_id=1, source_target_pairs={{0,1},{1,0},{2,3},{3,2},{4,5},{5,4},{6,7},{7,6},{8,9},{9,8},{10,11... | collective-permute-start | bytes 399368 | tf_op jit(solution)/shard_map/ppermute | solution.py:195
  15.1 1.6 %collective-permute-start.6 = (bf16[520,128]{1,0:T(8,128)(2,1)S(1)}, bf16[520,128]{1,0:T(8,128)(2,1)S(1)}, u32[]{:S(2)}, u32[]{:S(2)}) collective-permute-start(bf16[520,128]{1,0:T(8,128)(2,1)S(1)} %collective-permute-done.5.refs_6_), channel_id=1, source_target_pairs={{0,1},{1,0},{2,3},{3,2},{4,5},{5,4},{6,7},{7,6},{8,9},{9,8},{10,11... | collective-permute-start | bytes 399368 | tf_op jit(solution)/shard_map/ppermute | solution.py:195
  15.1 1.6 %collective-permute-start.4 = (bf16[520,128]{1,0:T(8,128)(2,1)S(1)}, bf16[520,128]{1,0:T(8,128)(2,1)S(1)}, u32[]{:S(2)}, u32[]{:S(2)}) collective-permute-start(bf16[520,128]{1,0:T(8,128)(2,1)S(1)} %collective-permute-done.3.refs_4_), channel_id=1, source_target_pairs={{0,1},{1,0},{2,3},{3,2},{4,5},{5,4},{6,7},{7,6},{8,9},{9,8},{10,11... | collective-permute-start | bytes 399368 | tf_op jit(solution)/shard_map/ppermute | solution.py:195
  15.7 1.4 %collective-permute-start.2 = (bf16[520,128]{1,0:T(8,128)(2,1)S(1)}, bf16[520,128]{1,0:T(8,128)(2,1)S(1)}, u32[]{:S(2)}, u32[]{:S(2)}) collective-permute-start(bf16[520,128]{1,0:T(8,128)(2,1)S(1)} %collective-permute-done.1.refs_2_), channel_id=1, source_target_pairs={{0,1},{1,0},{2,3},{3,2},{4,5},{5,4},{6,7},{7,6},{8,9},{9,8},{10,11... | collective-permute-start | bytes 399368 | tf_op jit(solution)/shard_map/ppermute | solution.py:195

commit v5 on v4

--- a/solution.py
+++ b/solution.py
@@ -21,30 +21,32 @@
 
 
 def pack_kernel(
-    order_ref, lengths_ref, keys_ref, values_ref, packed_ref, span_ref, order, lengths, sems
+    order_ref, lengths_ref, keys_ref, values_ref,
+    packed_ref, span_ref, order, lengths, sems,
 ):
     rows = keys_ref.shape[0]
+    half = KH * rows
     copies = [
         pltpu.make_async_copy(order_ref, order, sems.at[0]),
         pltpu.make_async_copy(lengths_ref, lengths, sems.at[1]),
     ]
-    for index in range(2 * KH):
-        source = keys_ref if index < KH else values_ref
-        copies.append(
-            pltpu.make_async_copy(
-                source.at[:, pl.ds(index % KH * HD, HD)],
-                packed_ref.at[pl.ds(index * rows, rows), :],
-                sems.at[2 + index],
+    for head in range(KH):
+        for source, first in ((keys_ref, 0), (values_ref, half)):
+            copies.append(
+                pltpu.make_async_copy(
+                    source.at[:, pl.ds(head * HD, HD)],
+                    packed_ref.at[pl.ds(first + head * rows, rows), :],
+                    sems.at[len(copies)],
+                )
             )
-        )
     for copy in copies:
         copy.start()
     copies[0].wait()
     copies[1].wait()
     lane = lax.broadcasted_iota(jnp.int32, (TAG, HD), 1)
     block = jnp.where((lane // BLOCK) % 2 == 0, order[0], order[1])
-    packed_ref[2 * KH * rows :, :] = block.astype(jnp.float32).astype(jnp.bfloat16)
-    row = lax.broadcasted_iota(jnp.int32, (rows, 128), 0)
+    packed_ref[2 * half :, :] = block.astype(jnp.float32).astype(jnp.bfloat16)
+    row = lax.broadcasted_iota(jnp.int32, (rows, HD), 0)
     position = jnp.where(row < BLOCK, order[0], order[1]) * BLOCK + row % BLOCK
     first = jnp.zeros_like(position)
     end = 0
@@ -59,11 +61,12 @@
 
 def pack(block_order, doc_lengths, keys, values):
     rows = keys.shape[0]
+    half = KH * rows
     return pl.pallas_call(
         pack_kernel,
         out_shape=(
-            pltpu.VMEM((2 * KH * rows + TAG, HD), keys.dtype),
-            pltpu.VMEM((2, rows, 128), jnp.int32),
+            pltpu.VMEM((2 * half + TAG, HD), keys.dtype),
+            pltpu.VMEM((2, rows, HD), jnp.int32),
         ),
         in_specs=[ANY, ANY, ANY, ANY],
         out_specs=(VMEM, VMEM),
@@ -96,18 +99,26 @@
     )(queries)
 
 
-def attend_kernel(count, span_ref, queries_ref, *refs):
-    part_refs = refs[:count]
-    out_ref, staged, sems = refs[count:]
+def attend_kernel(count, first, last, span_ref, queries_ref, *refs):
     rows = queries_ref.shape[0]
+    half = KH * rows
     columns = GROUP * HD
-
-    lane = lax.broadcasted_iota(jnp.int32, (TAG, 128), 1)
+    part_refs, refs = refs[:count], refs[count:]
+    if not first:
+        (top_in, total_in, mixed_in), refs = refs[:3], refs[3:]
+    if last:
+        out_ref, staged, sems = refs
+    else:
+        top_out, total_out, mixed_out = refs
+
+    lane = lax.broadcasted_iota(jnp.int32, (TAG, HD), 1)
     masks = []
-    for pair in range(count // 2):
-        early = part_refs[2 * pair][2 * KH * rows :, :].astype(jnp.float32)
-        late = part_refs[2 * pair + 1][2 * KH * rows :, :].astype(jnp.float32)
-        block = jnp.where(lane < rows, early, late).astype(jnp.int32)
+    for early, late in zip(part_refs[::2], part_refs[1::2]):
+        block = jnp.where(
+            lane < rows,
+            early[2 * half :, :].astype(jnp.float32),
+            late[2 * half :, :].astype(jnp.float32),
+        ).astype(jnp.int32)
         position = (block * BLOCK + lane % BLOCK)[:1, :]
         allowed = (position >= span_ref[0]) & (position <= span_ref[1])
         masks.append(jnp.where(allowed, 0.0, NEGATIVE))
@@ -128,20 +139,36 @@
             )
             + mask
         )
-    weights, totals = [], []
+    tops, weights, totals = [], [], []
     for head in range(KH):
         top = jnp.max(scores[head], axis=1, keepdims=True)
-        weight = jnp.exp2((scores[head] - top) * SCALE)
+        if not first:
+            top = jnp.maximum(top, top_in[head])
+            wide = jnp.concatenate([top] * len(masks), axis=1)
+            weight = jnp.exp2((scores[head] - wide) * SCALE)
+        else:
+            weight = jnp.exp2((scores[head] - top) * SCALE)
+        tops.append(top)
         totals.append(jnp.sum(weight, axis=1, keepdims=True))
         weights.append(weight.astype(jnp.bfloat16))
     copies = []
     for head in range(KH):
         values = jnp.concatenate(
-            [part[(KH + head) * rows : (KH + head + 1) * rows, :] for part in part_refs],
+            [part[half + head * rows : half + (head + 1) * rows, :] for part in part_refs],
             axis=0,
         )
         mixed = jnp.dot(weights[head], values, preferred_element_type=jnp.float32)
-        mixed = (mixed * (1.0 / totals[head])).astype(jnp.bfloat16)
+        total = totals[head]
+        if not first:
+            factor = jnp.exp2((top_in[head] - tops[head]) * SCALE)
+            total = total + total_in[head] * factor
+            mixed = mixed + mixed_in[head] * factor
+        if not last:
+            top_out[head] = jnp.broadcast_to(tops[head], (GROUP * rows, HD))
+            total_out[head] = jnp.broadcast_to(total, (GROUP * rows, HD))
+            mixed_out[head] = mixed
+            continue
+        mixed = (mixed * (1.0 / total)).astype(jnp.bfloat16)
         at = head * columns
         for g in range(GROUP):
             staged[:, at + g * HD : at + (g + 1) * HD] = mixed[g * rows : (g + 1) * rows, :]
@@ -154,25 +181,26 @@
         copy.wait()
 
 
-def attend(span, queries, parts):
-    count = len(parts)
+def attend(span, queries, parts, state, last):
     rows = queries.shape[0]
-    work = KH * GROUP * rows * count * rows
+    work = KH * GROUP * rows * len(parts) * rows
+    out_shape = (pltpu.VMEM((KH, GROUP * rows, HD), jnp.float32),) * 3
+    scratch = []
+    if last:
+        out_shape = jax.ShapeDtypeStruct(queries.shape, jnp.bfloat16)
+        scratch = [pltpu.VMEM(queries.shape, jnp.bfloat16), pltpu.SemaphoreType.DMA((KH,))]
     return pl.pallas_call(
-        partial(attend_kernel, count),
-        out_shape=jax.ShapeDtypeStruct(queries.shape, jnp.bfloat16),
-        in_specs=[VMEM, VMEM] + [VMEM] * count,
-        out_specs=ANY,
-        scratch_shapes=[
-            pltpu.VMEM(queries.shape, jnp.bfloat16),
-            pltpu.SemaphoreType.DMA((KH,)),
-        ],
+        partial(attend_kernel, len(parts), not state, last),
+        out_shape=out_shape,
+        in_specs=[VMEM] * (2 + len(parts) + len(state)),
+        out_specs=ANY if last else (VMEM, VMEM, VMEM),
+        scratch_shapes=scratch,
         compiler_params=pltpu.CompilerParams(vmem_limit_bytes=40 << 20),
         cost_estimate=pl.CostEstimate(
             flops=4 * work * HD, transcendentals=work, bytes_accessed=4 * work
         ),
-        name="attend",
-    )(span, queries, *parts)
+        name="finish" if last else "begin",
+    )(span, queries, *parts, *state)
 
 
 def on_device(devices, queries, keys, values, block_order, doc_lengths):
@@ -195,10 +223,17 @@
         return lax.ppermute(array, "ctx", other_core)
 
     own, span = pack(block_order, doc_lengths, keys, values)
-    parts = []
-    for part in [own] + [along(own, route) for route in routes]:
-        parts += [part, across(part)]
-    return attend(span, fetch(queries), parts)
+    rows = fetch(queries)
+    early = [own, across(own)]
+    late = []
+    for index, route in enumerate(reversed(routes)):
+        part = along(own, route)
+        if index == 0:
+            rows, part = lax.optimization_barrier((rows, part))
+        early.append(part)
+        late.append(across(part))
+    state = attend(span, rows, early + late[: len(late) % 2], (), False)
+    return attend(span, rows, late[len(late) % 2 :], state, True)
 
 
 ROUTES = ((1, 0, 3, 2), (2, 3, 1, 0), (3, 2, 0, 1))

time: 18.9 us -> 18.7 us (0.989)
  waiting for transfers between devices: 8.5 us -> 8.01 us
  Pallas kernels: 3.52 us -> 3.88 us
    ppermute x3, waiting for transfers between devices: 8.21 us -> 7.24 us  [along(): return lax.ppermute(array, 'ctx', pairs)]
    ppermute x4, waiting for transfers between devices: 0.29 us -> 0.77 us  [across(): return lax.ppermute(array, 'ctx', other_core)]
    pallas_call x2 -> x3, Pallas kernels: 2.56 us -> 2.92 us  [the longest x2 2 us: attend(): pl.pallas_call(partial(attend_kernel, len(parts), not state, last), out_s...]
  transfers between devices with their start and end apart: 7 -> 7, of which waited for: 2 -> 2; matrix products, arithmetic and copies ran while one was open for 0% -> 0% of each run, Pallas kernels for 5% -> 9%
where the time goes in v5:
time: 18.7 us; the launch traced here: 18.5 us
  waiting for transfers between devices  8.01 us (43%)
  starting transfers between devices  6.58 us (35%)
  Pallas kernels  3.88 us (21%)
    ppermute x3, waiting for transfers between devices, along(): return lax.ppermute(array, 'ctx', pairs)  7.24 us
    ppermute x3, starting transfers between devices, along(): return lax.ppermute(array, 'ctx', pairs)  6 us
    pallas_call x2, Pallas kernels, attend(): pl.pallas_call(partial(attend_kernel, len(parts), not state, last), out_s...  2 us
    pallas_call x1, Pallas kernels, fetch(): pl.pallas_call(fetch_kernel, out_shape=pltpu.VMEM(queries.shape, queries....  0.96 us
    pallas_call x1, Pallas kernels, pack(): pl.pallas_call(pack_kernel, out_shape=(pltpu.VMEM((2 * half + TAG, HD), k...  0.92 us
    ppermute x4, waiting for transfers between devices, across(): return lax.ppermute(array, 'ctx', other_core)  0.77 us
    ppermute x4, starting transfers between devices, across(): return lax.ppermute(array, 'ctx', other_core)  0.58 us
  transfers between devices with their start and end apart: 7, of which 2 were waited for; matrix products, arithmetic and copies ran while one was open for 0% of the time, Pallas kernels for 9%

profile of v5, /device:TPU:0, one launch (start us, length us, event | category | flops | bytes accessed | tf_op | source)
XLA Modules:
  0.0 18.5 jit_solution(527687964549258699)
XLA Ops:
  0.0 0.9 %pack.1 = (bf16[520,128]{1,0:T(8,128)(2,1)S(1)}, s32[2,64,128]{2,1,0:T(8,128)S(1)}) custom-call(s32[2]{0:T(128)} %order_ref.1, s32[4]{0:T(128)} %lengths_ref.1, bf16[64,512]{1,0:T(8,128)(2,1)} %keys_ref.1, bf16[64,512]{1,0:T(8,128)(2,1)} %values_ref.1), custom_call_target="tpu_custom_call" | custom-call | tf_op jit(solution)/shard_map/pack/pallas_call | solution.py:65
  0.9 5.1 %collective-permute-start = (bf16[520,128]{1,0:T(8,128)(2,1)S(1)}, bf16[520,128]{1,0:T(8,128)(2,1)S(1)}, u32[]{:S(2)}, u32[]{:S(2)}) collective-permute-start(bf16[520,128]{1,0:T(8,128)(2,1)S(1)} %get-tuple-element.13.refs_0_), channel_id=1, source_target_pairs={{0,6},{1,7},{2,4},{3,5},{4,0},{5,1},{6,2},{7,3},{8,14},{9,15},{10,... | collective-permute-start | bytes 399368 | tf_op jit(solution)/shard_map/ppermute | solution.py:220
  6.0 0.0 collective-permute-start.1
  6.0 0.9 %collective-permute-start.3 = (bf16[520,128]{1,0:T(8,128)(2,1)S(1)}, bf16[520,128]{1,0:T(8,128)(2,1)S(1)}, u32[]{:S(2)}, u32[]{:S(2)}) collective-permute-start(bf16[520,128]{1,0:T(8,128)(2,1)S(1)} %get-tuple-element.13.refs_0_), channel_id=1, source_target_pairs={{0,2},{1,3},{2,0},{3,1},{4,6},{5,7},{6,4},{7,5},{8,10},{9,11},{10,... | collective-permute-start | bytes 399368 | tf_op jit(solution)/shard_map/ppermute | solution.py:220
  6.9 0.0 collective-permute-start.5
  6.9 1.0 %fetch.1.queries_ref = bf16[64,2048]{1,0:T(8,128)(2,1)S(1)} custom-call(bf16[64,2048]{1,0:T(8,128)(2,1)} %queries_ref.1), custom_call_target="tpu_custom_call" | custom-call | bytes 2097152 | tf_op jit(solution)/shard_map/fetch/pallas_call | solution.py:89
  7.9 7.2 %collective-permute-done.refs_2_ = bf16[520,128]{1,0:T(8,128)(2,1)S(1)} collective-permute-done((bf16[520,128]{1,0:T(8,128)(2,1)S(1)}, bf16[520,128]{1,0:T(8,128)(2,1)S(1)}, u32[]{:S(2)}, u32[]{:S(2)}) %collective-permute-start) | collective-permute-done | bytes 133152 | tf_op jit(solution)/shard_map/ppermute | solution.py:220
  15.1 0.0 collective-permute-start.6
  15.1 0.0 collective-permute-done.1.refs_3_
  15.1 0.5 %collective-permute-start.2 = (bf16[520,128]{1,0:T(8,128)(2,1)S(1)}, bf16[520,128]{1,0:T(8,128)(2,1)S(1)}, u32[]{:S(2)}, u32[]{:S(2)}) collective-permute-start(bf16[520,128]{1,0:T(8,128)(2,1)S(1)} %collective-permute-done.1.refs_3_), channel_id=1, source_target_pairs={{0,1},{1,0},{2,3},{3,2},{4,5},{5,4},{6,7},{7,6},{8,9},{9,8},{10,11... | collective-permute-start | bytes 399368 | tf_op jit(solution)/shard_map/ppermute | solution.py:223
  15.7 0.0 collective-permute-done.3.refs_4_
  15.7 0.1 collective-permute-start.4
  15.7 0.0 collective-permute-done.5.refs_1_
  15.7 0.8 %collective-permute-done.6.refs_5_ = bf16[520,128]{1,0:T(8,128)(2,1)S(1)} collective-permute-done((bf16[520,128]{1,0:T(8,128)(2,1)S(1)}, bf16[520,128]{1,0:T(8,128)(2,1)S(1)}, u32[]{:S(2)}, u32[]{:S(2)}) %collective-permute-start.6) | collective-permute-done | bytes 133152 | tf_op jit(solution)/shard_map/ppermute | solution.py:223
  16.5 0.7 %begin.1 = (f32[4,256,128]{2,1,0:T(8,128)S(1)}, f32[4,256,128]{2,1,0:T(8,128)S(1)}, f32[4,256,128]{2,1,0:T(8,128)S(1)}) custom-call(s32[2,64,128]{2,1,0:T(8,128)S(1)} %get-tuple-element.12.span_ref, bf16[64,2048]{1,0:T(8,128)(2,1)S(1)} %fetch.1.queries_ref, bf16[520,128]{1,0:T(8,128)(2,1)S(1)} %get-tuple-element.13.refs_0_, ...), custom_call_target="tpu_custom_call" | custom-call | flops 201326592 | bytes 1572864 | tf_op jit(solution)/shard_map/begin/pallas_call | solution.py:192
  17.2 0.0 collective-permute-done.2.refs_0_
  17.2 0.0 collective-permute-done.4.refs_1_
  17.3 1.3 %finish.1 = bf16[64,2048]{1,0:T(8,128)(2,1)} custom-call(s32[2,64,128]{2,1,0:T(8,128)S(1)} %get-tuple-element.12.span_ref, bf16[64,2048]{1,0:T(8,128)(2,1)S(1)} %fetch.1.queries_ref, bf16[520,128]{1,0:T(8,128)(2,1)S(1)} %collective-permute-done.2.refs_0_, bf16[520,128]{1,0:T(8,128)(2,1)S(1)} %collective-permute-done.4.refs_1_, ...), custom_call_target="tpu_custom_call" | custom-call | flops 67108864 | bytes 524288 | tf_op jit(solution)/shard_map/finish/pallas_call | solution.py:192
Async XLA Ops:
  0.9 14.2 %collective-permute-start = (bf16[520,128]{1,0:T(8,128)(2,1)S(1)}, bf16[520,128]{1,0:T(8,128)(2,1)S(1)}, u32[]{:S(2)}, u32[]{:S(2)}) collective-permute-start(bf16[520,128]{1,0:T(8,128)(2,1)S(1)} %get-tuple-element.13.refs_0_), channel_id=1, source_target_pairs={{0,6},{1,7},{2,4},{3,5},{4,0},{5,1},{6,2},{7,3},{8,14},{9,15},{10,... | collective-permute-start | bytes 399368 | tf_op jit(solution)/shard_map/ppermute | solution.py:220
  6.0 9.1 %collective-permute-start.1 = (bf16[520,128]{1,0:T(8,128)(2,1)S(1)}, bf16[520,128]{1,0:T(8,128)(2,1)S(1)}, u32[]{:S(2)}, u32[]{:S(2)}) collective-permute-start(bf16[520,128]{1,0:T(8,128)(2,1)S(1)} %get-tuple-element.13.refs_0_), channel_id=1, source_target_pairs={{0,4},{1,5},{2,6},{3,7},{4,2},{5,3},{6,0},{7,1},{8,12},{9,13},{10,... | collective-permute-start | bytes 399368 | tf_op jit(solution)/shard_map/ppermute | solution.py:220
  6.0 9.6 %collective-permute-start.3 = (bf16[520,128]{1,0:T(8,128)(2,1)S(1)}, bf16[520,128]{1,0:T(8,128)(2,1)S(1)}, u32[]{:S(2)}, u32[]{:S(2)}) collective-permute-start(bf16[520,128]{1,0:T(8,128)(2,1)S(1)} %get-tuple-element.13.refs_0_), channel_id=1, source_target_pairs={{0,2},{1,3},{2,0},{3,1},{4,6},{5,7},{6,4},{7,5},{8,10},{9,11},{10,... | collective-permute-start | bytes 399368 | tf_op jit(solution)/shard_map/ppermute | solution.py:220
  6.9 8.8 %collective-permute-start.5 = (bf16[520,128]{1,0:T(8,128)(2,1)S(1)}, bf16[520,128]{1,0:T(8,128)(2,1)S(1)}, u32[]{:S(2)}, u32[]{:S(2)}) collective-permute-start(bf16[520,128]{1,0:T(8,128)(2,1)S(1)} %get-tuple-element.13.refs_0_), channel_id=1, source_target_pairs={{0,1},{1,0},{2,3},{3,2},{4,5},{5,4},{6,7},{7,6},{8,9},{9,8},{10,11... | collective-permute-start | bytes 399368 | tf_op jit(solution)/shard_map/ppermute | solution.py:223
  15.1 1.4 %collective-permute-start.6 = (bf16[520,128]{1,0:T(8,128)(2,1)S(1)}, bf16[520,128]{1,0:T(8,128)(2,1)S(1)}, u32[]{:S(2)}, u32[]{:S(2)}) collective-permute-start(bf16[520,128]{1,0:T(8,128)(2,1)S(1)} %collective-permute-done.refs_2_), channel_id=1, source_target_pairs={{0,1},{1,0},{2,3},{3,2},{4,5},{5,4},{6,7},{7,6},{8,9},{9,8},{10,11... | collective-permute-start | bytes 399368 | tf_op jit(solution)/shard_map/ppermute | solution.py:223
  15.1 2.1 %collective-permute-start.2 = (bf16[520,128]{1,0:T(8,128)(2,1)S(1)}, bf16[520,128]{1,0:T(8,128)(2,1)S(1)}, u32[]{:S(2)}, u32[]{:S(2)}) collective-permute-start(bf16[520,128]{1,0:T(8,128)(2,1)S(1)} %collective-permute-done.1.refs_3_), channel_id=1, source_target_pairs={{0,1},{1,0},{2,3},{3,2},{4,5},{5,4},{6,7},{7,6},{8,9},{9,8},{10,11... | collective-permute-start | bytes 399368 | tf_op jit(solution)/shard_map/ppermute | solution.py:223
  15.7 1.6 %collective-permute-start.4 = (bf16[520,128]{1,0:T(8,128)(2,1)S(1)}, bf16[520,128]{1,0:T(8,128)(2,1)S(1)}, u32[]{:S(2)}, u32[]{:S(2)}) collective-permute-start(bf16[520,128]{1,0:T(8,128)(2,1)S(1)} %collective-permute-done.3.refs_4_), channel_id=1, source_target_pairs={{0,1},{1,0},{2,3},{3,2},{4,5},{5,4},{6,7},{7,6},{8,9},{9,8},{10,11... | collective-permute-start | bytes 399368 | tf_op jit(solution)/shard_map/ppermute | solution.py:223

commit v6 on v5

--- a/solution.py
+++ b/solution.py
@@ -209,13 +209,17 @@
     if chips == 4:
         routes = ROUTES
     elif chips & (chips - 1) == 0:
-        routes = [[chip ^ step for chip in range(chips)] for step in range(1, chips)]
+        routes = [[[chip ^ step for chip in range(chips)]] * 2 for step in range(1, chips)]
     else:
-        routes = [[(chip + step) % chips for chip in range(chips)] for step in range(1, chips)]
+        routes = [
+            [[(chip + step) % chips for chip in range(chips)]] * 2 for step in range(1, chips)
+        ]
 
     def along(array, route):
         pairs = [
-            (2 * chip + core, 2 * route[chip] + core) for chip in range(chips) for core in range(2)
+            (2 * chip + core, 2 * route[core][chip] + core)
+            for chip in range(chips)
+            for core in range(2)
         ]
         return lax.ppermute(array, "ctx", pairs)
 
@@ -226,7 +230,7 @@
     rows = fetch(queries)
     early = [own, across(own)]
     late = []
-    for index, route in enumerate(reversed(routes)):
+    for index, route in enumerate(routes):
         part = along(own, route)
         if index == 0:
             rows, part = lax.optimization_barrier((rows, part))
@@ -236,7 +240,7 @@
     return attend(span, rows, late[len(late) % 2 :], state, True)
 
 
-ROUTES = ((1, 0, 3, 2), (2, 3, 1, 0), (3, 2, 0, 1))
+ROUTES = (((1, 2, 3, 0), (3, 2, 0, 1)), ((2, 3, 0, 1), (2, 3, 1, 0)), ((3, 0, 1, 2), (1, 0, 3, 2)))
 
 
 def solution(mesh):

time: 18.7 us -> 18.5 us (0.989)
  waiting for transfers between devices: 8.01 us -> 3.55 us
  starting transfers between devices: 6.58 us -> 10.8 us
    ppermute x3, waiting for transfers between devices: 7.24 us -> 3.25 us  [along(): return lax.ppermute(array, 'ctx', pairs)]
    ppermute x4, starting transfers between devices: 0.58 us -> 3.84 us  [across(): return lax.ppermute(array, 'ctx', other_core)]
    ppermute x3, starting transfers between devices: 6 us -> 7.01 us  [along(): return lax.ppermute(array, 'ctx', pairs)]
    ppermute x4, waiting for transfers between devices: 0.77 us -> 0.29 us  [across(): return lax.ppermute(array, 'ctx', other_core)]
  transfers between devices with their start and end apart: 7 -> 7, of which waited for: 2 -> 4; matrix products, arithmetic and copies ran while one was open for 0% -> 0% of each run, Pallas kernels for 9% -> 9%
where the time goes in v6:
time: 18.5 us; the launch traced here: 18.3 us
  starting transfers between devices  10.8 us (58%)
  Pallas kernels  3.87 us (21%)
  waiting for transfers between devices  3.55 us (19%)
    ppermute x3, starting transfers between devices, along(): return lax.ppermute(array, 'ctx', pairs)  7.01 us
    ppermute x4, starting transfers between devices, across(): return lax.ppermute(array, 'ctx', other_core)  3.84 us
    ppermute x3, waiting for transfers between devices, along(): return lax.ppermute(array, 'ctx', pairs)  3.25 us
    pallas_call x2, Pallas kernels, attend(): pl.pallas_call(partial(attend_kernel, len(parts), not state, last), out_s...  1.99 us
    pallas_call x1, Pallas kernels, fetch(): pl.pallas_call(fetch_kernel, out_shape=pltpu.VMEM(queries.shape, queries....  0.96 us
    pallas_call x1, Pallas kernels, pack(): pl.pallas_call(pack_kernel, out_shape=(pltpu.VMEM((2 * half + TAG, HD), k...  0.92 us
  transfers between devices with their start and end apart: 7, of which 4 were waited for; matrix products, arithmetic and copies ran while one was open for 0% of the time, Pallas kernels for 9%

profile of v6, /device:TPU:0, one launch (start us, length us, event | category | flops | bytes accessed | tf_op | source)
XLA Modules:
  0.0 18.3 jit_solution(18248317963645318250)
XLA Ops:
  0.0 0.9 %pack.1 = (bf16[520,128]{1,0:T(8,128)(2,1)S(1)}, s32[2,64,128]{2,1,0:T(8,128)S(1)}) custom-call(s32[2]{0:T(128)} %order_ref.1, s32[4]{0:T(128)} %lengths_ref.1, bf16[64,512]{1,0:T(8,128)(2,1)} %keys_ref.1, bf16[64,512]{1,0:T(8,128)(2,1)} %values_ref.1), custom_call_target="tpu_custom_call" | custom-call | tf_op jit(solution)/shard_map/pack/pallas_call | solution.py:65
  0.9 3.1 %collective-permute-start = (bf16[520,128]{1,0:T(8,128)(2,1)S(1)}, bf16[520,128]{1,0:T(8,128)(2,1)S(1)}, u32[]{:S(2)}, u32[]{:S(2)}) collective-permute-start(bf16[520,128]{1,0:T(8,128)(2,1)S(1)} %get-tuple-element.13.refs_0_), channel_id=1, source_target_pairs={{0,2},{1,7},{2,4},{3,5},{4,6},{5,1},{6,0},{7,3},{8,10},{9,15},{10,... | collective-permute-start | bytes 399368 | tf_op jit(solution)/shard_map/ppermute | solution.py:224
  4.0 2.6 %collective-permute-start.1 = (bf16[520,128]{1,0:T(8,128)(2,1)S(1)}, bf16[520,128]{1,0:T(8,128)(2,1)S(1)}, u32[]{:S(2)}, u32[]{:S(2)}) collective-permute-start(bf16[520,128]{1,0:T(8,128)(2,1)S(1)} %get-tuple-element.13.refs_0_), channel_id=1, source_target_pairs={{0,4},{1,5},{2,6},{3,7},{4,0},{5,3},{6,2},{7,1},{8,12},{9,13},{10,... | collective-permute-start | bytes 399368 | tf_op jit(solution)/shard_map/ppermute | solution.py:224
  6.6 1.3 %collective-permute-start.3 = (bf16[520,128]{1,0:T(8,128)(2,1)S(1)}, bf16[520,128]{1,0:T(8,128)(2,1)S(1)}, u32[]{:S(2)}, u32[]{:S(2)}) collective-permute-start(bf16[520,128]{1,0:T(8,128)(2,1)S(1)} %get-tuple-element.13.refs_0_), channel_id=1, source_target_pairs={{0,6},{1,3},{2,0},{3,1},{4,2},{5,7},{6,4},{7,5},{8,14},{9,11},{10,... | collective-permute-start | bytes 399368 | tf_op jit(solution)/shard_map/ppermute | solution.py:224
  7.9 0.0 collective-permute-start.5
  8.0 1.0 %fetch.1.queries_ref = bf16[64,2048]{1,0:T(8,128)(2,1)S(1)} custom-call(bf16[64,2048]{1,0:T(8,128)(2,1)} %queries_ref.1), custom_call_target="tpu_custom_call" | custom-call | bytes 2097152 | tf_op jit(solution)/shard_map/fetch/pallas_call | solution.py:89
  8.9 0.9 %collective-permute-done.refs_2_ = bf16[520,128]{1,0:T(8,128)(2,1)S(1)} collective-permute-done((bf16[520,128]{1,0:T(8,128)(2,1)S(1)}, bf16[520,128]{1,0:T(8,128)(2,1)S(1)}, u32[]{:S(2)}, u32[]{:S(2)}) %collective-permute-start) | collective-permute-done | bytes 133152 | tf_op jit(solution)/shard_map/ppermute | solution.py:224
  9.8 3.3 %collective-permute-start.6 = (bf16[520,128]{1,0:T(8,128)(2,1)S(1)}, bf16[520,128]{1,0:T(8,128)(2,1)S(1)}, u32[]{:S(2)}, u32[]{:S(2)}) collective-permute-start(bf16[520,128]{1,0:T(8,128)(2,1)S(1)} %collective-permute-done.refs_2_), channel_id=1, source_target_pairs={{0,1},{1,0},{2,3},{3,2},{4,5},{5,4},{6,7},{7,6},{8,9},{9,8},{10,11... | collective-permute-start | bytes 399368 | tf_op jit(solution)/shard_map/ppermute | solution.py:227
  13.2 2.3 %collective-permute-done.1.refs_3_ = bf16[520,128]{1,0:T(8,128)(2,1)S(1)} collective-permute-done((bf16[520,128]{1,0:T(8,128)(2,1)S(1)}, bf16[520,128]{1,0:T(8,128)(2,1)S(1)}, u32[]{:S(2)}, u32[]{:S(2)}) %collective-permute-start.1) | collective-permute-done | bytes 133152 | tf_op jit(solution)/shard_map/ppermute | solution.py:224
  15.5 0.0 collective-permute-start.2
  15.5 0.0 collective-permute-done.3.refs_4_
  15.5 0.5 %collective-permute-start.4 = (bf16[520,128]{1,0:T(8,128)(2,1)S(1)}, bf16[520,128]{1,0:T(8,128)(2,1)S(1)}, u32[]{:S(2)}, u32[]{:S(2)}) collective-permute-start(bf16[520,128]{1,0:T(8,128)(2,1)S(1)} %collective-permute-done.3.refs_4_), channel_id=1, source_target_pairs={{0,1},{1,0},{2,3},{3,2},{4,5},{5,4},{6,7},{7,6},{8,9},{9,8},{10,11... | collective-permute-start | bytes 399368 | tf_op jit(solution)/shard_map/ppermute | solution.py:227
  16.0 0.0 collective-permute-done.5.refs_1_
  16.0 0.0 collective-permute-done.6.refs_5_
  16.0 0.7 %begin.1 = (f32[4,256,128]{2,1,0:T(8,128)S(1)}, f32[4,256,128]{2,1,0:T(8,128)S(1)}, f32[4,256,128]{2,1,0:T(8,128)S(1)}) custom-call(s32[2,64,128]{2,1,0:T(8,128)S(1)} %get-tuple-element.12.span_ref, bf16[64,2048]{1,0:T(8,128)(2,1)S(1)} %fetch.1.queries_ref, bf16[520,128]{1,0:T(8,128)(2,1)S(1)} %get-tuple-element.13.refs_0_, ...), custom_call_target="tpu_custom_call" | custom-call | flops 201326592 | bytes 1572864 | tf_op jit(solution)/shard_map/begin/pallas_call | solution.py:192
  16.7 0.1 collective-permute-done.2.refs_0_
  16.8 0.2 %collective-permute-done.4.refs_1_ = bf16[520,128]{1,0:T(8,128)(2,1)S(1)} collective-permute-done((bf16[520,128]{1,0:T(8,128)(2,1)S(1)}, bf16[520,128]{1,0:T(8,128)(2,1)S(1)}, u32[]{:S(2)}, u32[]{:S(2)}) %collective-permute-start.4) | collective-permute-done | bytes 133152 | tf_op jit(solution)/shard_map/ppermute | solution.py:227
  17.0 1.3 %finish.1 = bf16[64,2048]{1,0:T(8,128)(2,1)} custom-call(s32[2,64,128]{2,1,0:T(8,128)S(1)} %get-tuple-element.12.span_ref, bf16[64,2048]{1,0:T(8,128)(2,1)S(1)} %fetch.1.queries_ref, bf16[520,128]{1,0:T(8,128)(2,1)S(1)} %collective-permute-done.2.refs_0_, bf16[520,128]{1,0:T(8,128)(2,1)S(1)} %collective-permute-done.4.refs_1_, ...), custom_call_target="tpu_custom_call" | custom-call | flops 67108864 | bytes 524288 | tf_op jit(solution)/shard_map/finish/pallas_call | solution.py:192
Async XLA Ops:
  0.9 8.9 %collective-permute-start = (bf16[520,128]{1,0:T(8,128)(2,1)S(1)}, bf16[520,128]{1,0:T(8,128)(2,1)S(1)}, u32[]{:S(2)}, u32[]{:S(2)}) collective-permute-start(bf16[520,128]{1,0:T(8,128)(2,1)S(1)} %get-tuple-element.13.refs_0_), channel_id=1, source_target_pairs={{0,2},{1,7},{2,4},{3,5},{4,6},{5,1},{6,0},{7,3},{8,10},{9,15},{10,... | collective-permute-start | bytes 399368 | tf_op jit(solution)/shard_map/ppermute | solution.py:224
  4.0 11.5 %collective-permute-start.1 = (bf16[520,128]{1,0:T(8,128)(2,1)S(1)}, bf16[520,128]{1,0:T(8,128)(2,1)S(1)}, u32[]{:S(2)}, u32[]{:S(2)}) collective-permute-start(bf16[520,128]{1,0:T(8,128)(2,1)S(1)} %get-tuple-element.13.refs_0_), channel_id=1, source_target_pairs={{0,4},{1,5},{2,6},{3,7},{4,0},{5,3},{6,2},{7,1},{8,12},{9,13},{10,... | collective-permute-start | bytes 399368 | tf_op jit(solution)/shard_map/ppermute | solution.py:224
  6.6 8.9 %collective-permute-start.3 = (bf16[520,128]{1,0:T(8,128)(2,1)S(1)}, bf16[520,128]{1,0:T(8,128)(2,1)S(1)}, u32[]{:S(2)}, u32[]{:S(2)}) collective-permute-start(bf16[520,128]{1,0:T(8,128)(2,1)S(1)} %get-tuple-element.13.refs_0_), channel_id=1, source_target_pairs={{0,6},{1,3},{2,0},{3,1},{4,2},{5,7},{6,4},{7,5},{8,14},{9,11},{10,... | collective-permute-start | bytes 399368 | tf_op jit(solution)/shard_map/ppermute | solution.py:224
  7.9 8.1 %collective-permute-start.5 = (bf16[520,128]{1,0:T(8,128)(2,1)S(1)}, bf16[520,128]{1,0:T(8,128)(2,1)S(1)}, u32[]{:S(2)}, u32[]{:S(2)}) collective-permute-start(bf16[520,128]{1,0:T(8,128)(2,1)S(1)} %get-tuple-element.13.refs_0_), channel_id=1, source_target_pairs={{0,1},{1,0},{2,3},{3,2},{4,5},{5,4},{6,7},{7,6},{8,9},{9,8},{10,11... | collective-permute-start | bytes 399368 | tf_op jit(solution)/shard_map/ppermute | solution.py:227
  9.8 6.2 %collective-permute-start.6 = (bf16[520,128]{1,0:T(8,128)(2,1)S(1)}, bf16[520,128]{1,0:T(8,128)(2,1)S(1)}, u32[]{:S(2)}, u32[]{:S(2)}) collective-permute-start(bf16[520,128]{1,0:T(8,128)(2,1)S(1)} %collective-permute-done.refs_2_), channel_id=1, source_target_pairs={{0,1},{1,0},{2,3},{3,2},{4,5},{5,4},{6,7},{7,6},{8,9},{9,8},{10,11... | collective-permute-start | bytes 399368 | tf_op jit(solution)/shard_map/ppermute | solution.py:227
  15.5 1.4 %collective-permute-start.2 = (bf16[520,128]{1,0:T(8,128)(2,1)S(1)}, bf16[520,128]{1,0:T(8,128)(2,1)S(1)}, u32[]{:S(2)}, u32[]{:S(2)}) collective-permute-start(bf16[520,128]{1,0:T(8,128)(2,1)S(1)} %collective-permute-done.1.refs_3_), channel_id=1, source_target_pairs={{0,1},{1,0},{2,3},{3,2},{4,5},{5,4},{6,7},{7,6},{8,9},{9,8},{10,11... | collective-permute-start | bytes 399368 | tf_op jit(solution)/shard_map/ppermute | solution.py:227
  15.5 1.5 %collective-permute-start.4 = (bf16[520,128]{1,0:T(8,128)(2,1)S(1)}, bf16[520,128]{1,0:T(8,128)(2,1)S(1)}, u32[]{:S(2)}, u32[]{:S(2)}) collective-permute-start(bf16[520,128]{1,0:T(8,128)(2,1)S(1)} %collective-permute-done.3.refs_4_), channel_id=1, source_target_pairs={{0,1},{1,0},{2,3},{3,2},{4,5},{5,4},{6,7},{7,6},{8,9},{9,8},{10,11... | collective-permute-start | bytes 399368 | tf_op jit(solution)/shard_map/ppermute | solution.py:227

commit v7 on v6

--- a/solution.py
+++ b/solution.py
@@ -240,7 +240,7 @@
     return attend(span, rows, late[len(late) % 2 :], state, True)
 
 
-ROUTES = (((1, 2, 3, 0), (3, 2, 0, 1)), ((2, 3, 0, 1), (2, 3, 1, 0)), ((3, 0, 1, 2), (1, 0, 3, 2)))
+ROUTES = (((2, 0, 3, 1), (3, 2, 0, 1)), ((1, 3, 0, 2), (2, 3, 1, 0)), ((3, 2, 1, 0), (1, 0, 3, 2)))
 
 
 def solution(mesh):

time: 18.5 us -> 18.5 us (level)
  waiting for transfers between devices: 3.55 us -> 5.18 us
  starting transfers between devices: 10.8 us -> 9.22 us
    ppermute x4, starting transfers between devices: 3.84 us -> 2.09 us  [across(): return lax.ppermute(array, 'ctx', other_core)]
    ppermute x3, waiting for transfers between devices: 3.25 us -> 4.88 us  [along(): return lax.ppermute(array, 'ctx', pairs)]
  transfers between devices with their start and end apart: 7 -> 7, of which waited for: 4 -> 3; matrix products, arithmetic and copies ran while one was open for 0% -> 0% of each run, Pallas kernels for 9% -> 9%
where the time goes in v7:
time: 18.5 us; the launch traced here: 18.3 us
  starting transfers between devices  9.22 us (50%)
  waiting for transfers between devices  5.18 us (28%)
  Pallas kernels  3.87 us (21%)
    ppermute x3, starting transfers between devices, along(): return lax.ppermute(array, 'ctx', pairs)  7.13 us
    ppermute x3, waiting for transfers between devices, along(): return lax.ppermute(array, 'ctx', pairs)  4.88 us
    ppermute x4, starting transfers between devices, across(): return lax.ppermute(array, 'ctx', other_core)  2.09 us
    pallas_call x2, Pallas kernels, attend(): pl.pallas_call(partial(attend_kernel, len(parts), not state, last), out_s...  1.99 us
    pallas_call x1, Pallas kernels, fetch(): pl.pallas_call(fetch_kernel, out_shape=pltpu.VMEM(queries.shape, queries....  0.96 us
    pallas_call x1, Pallas kernels, pack(): pl.pallas_call(pack_kernel, out_shape=(pltpu.VMEM((2 * half + TAG, HD), k...  0.92 us
  transfers between devices with their start and end apart: 7, of which 3 were waited for; matrix products, arithmetic and copies ran while one was open for 0% of the time, Pallas kernels for 9%

profile of v7, /device:TPU:0, one launch (start us, length us, event | category | flops | bytes accessed | tf_op | source)
XLA Modules:
  0.0 18.3 jit_solution(9236198242921509146)
XLA Ops:
  0.0 0.9 %pack.1 = (bf16[520,128]{1,0:T(8,128)(2,1)S(1)}, s32[2,64,128]{2,1,0:T(8,128)S(1)}) custom-call(s32[2]{0:T(128)} %order_ref.1, s32[4]{0:T(128)} %lengths_ref.1, bf16[64,512]{1,0:T(8,128)(2,1)} %keys_ref.1, bf16[64,512]{1,0:T(8,128)(2,1)} %values_ref.1), custom_call_target="tpu_custom_call" | custom-call | tf_op jit(solution)/shard_map/pack/pallas_call | solution.py:65
  0.9 4.1 %collective-permute-start = (bf16[520,128]{1,0:T(8,128)(2,1)S(1)}, bf16[520,128]{1,0:T(8,128)(2,1)S(1)}, u32[]{:S(2)}, u32[]{:S(2)}) collective-permute-start(bf16[520,128]{1,0:T(8,128)(2,1)S(1)} %get-tuple-element.13.refs_0_), channel_id=1, source_target_pairs={{0,4},{1,7},{2,0},{3,5},{4,6},{5,1},{6,2},{7,3},{8,12},{9,15},{10,... | collective-permute-start | bytes 399368 | tf_op jit(solution)/shard_map/ppermute | solution.py:224
  5.0 0.0 collective-permute-start.1
  5.0 3.0 %collective-permute-start.3 = (bf16[520,128]{1,0:T(8,128)(2,1)S(1)}, bf16[520,128]{1,0:T(8,128)(2,1)S(1)}, u32[]{:S(2)}, u32[]{:S(2)}) collective-permute-start(bf16[520,128]{1,0:T(8,128)(2,1)S(1)} %get-tuple-element.13.refs_0_), channel_id=1, source_target_pairs={{0,6},{1,3},{2,4},{3,1},{4,2},{5,7},{6,0},{7,5},{8,14},{9,11},{10,... | collective-permute-start | bytes 399368 | tf_op jit(solution)/shard_map/ppermute | solution.py:224
  8.1 0.0 collective-permute-start.5
  8.1 1.0 %fetch.1.queries_ref = bf16[64,2048]{1,0:T(8,128)(2,1)S(1)} custom-call(bf16[64,2048]{1,0:T(8,128)(2,1)} %queries_ref.1), custom_call_target="tpu_custom_call" | custom-call | bytes 2097152 | tf_op jit(solution)/shard_map/fetch/pallas_call | solution.py:89
  9.0 0.0 collective-permute-done.refs_2_
  9.0 1.6 %collective-permute-start.6 = (bf16[520,128]{1,0:T(8,128)(2,1)S(1)}, bf16[520,128]{1,0:T(8,128)(2,1)S(1)}, u32[]{:S(2)}, u32[]{:S(2)}) collective-permute-start(bf16[520,128]{1,0:T(8,128)(2,1)S(1)} %collective-permute-done.refs_2_), channel_id=1, source_target_pairs={{0,1},{1,0},{2,3},{3,2},{4,5},{5,4},{6,7},{7,6},{8,9},{9,8},{10,11... | collective-permute-start | bytes 399368 | tf_op jit(solution)/shard_map/ppermute | solution.py:227
  10.6 4.9 %collective-permute-done.1.refs_3_ = bf16[520,128]{1,0:T(8,128)(2,1)S(1)} collective-permute-done((bf16[520,128]{1,0:T(8,128)(2,1)S(1)}, bf16[520,128]{1,0:T(8,128)(2,1)S(1)}, u32[]{:S(2)}, u32[]{:S(2)}) %collective-permute-start.1) | collective-permute-done | bytes 133152 | tf_op jit(solution)/shard_map/ppermute | solution.py:224
  15.5 0.0 collective-permute-start.2
  15.5 0.0 collective-permute-done.3.refs_4_
  15.5 0.5 %collective-permute-start.4 = (bf16[520,128]{1,0:T(8,128)(2,1)S(1)}, bf16[520,128]{1,0:T(8,128)(2,1)S(1)}, u32[]{:S(2)}, u32[]{:S(2)}) collective-permute-start(bf16[520,128]{1,0:T(8,128)(2,1)S(1)} %collective-permute-done.3.refs_4_), channel_id=1, source_target_pairs={{0,1},{1,0},{2,3},{3,2},{4,5},{5,4},{6,7},{7,6},{8,9},{9,8},{10,11... | collective-permute-start | bytes 399368 | tf_op jit(solution)/shard_map/ppermute | solution.py:227
  16.0 0.0 collective-permute-done.5.refs_1_
  16.0 0.0 collective-permute-done.6.refs_5_
  16.0 0.7 %begin.1 = (f32[4,256,128]{2,1,0:T(8,128)S(1)}, f32[4,256,128]{2,1,0:T(8,128)S(1)}, f32[4,256,128]{2,1,0:T(8,128)S(1)}) custom-call(s32[2,64,128]{2,1,0:T(8,128)S(1)} %get-tuple-element.12.span_ref, bf16[64,2048]{1,0:T(8,128)(2,1)S(1)} %fetch.1.queries_ref, bf16[520,128]{1,0:T(8,128)(2,1)S(1)} %get-tuple-element.13.refs_0_, ...), custom_call_target="tpu_custom_call" | custom-call | flops 201326592 | bytes 1572864 | tf_op jit(solution)/shard_map/begin/pallas_call | solution.py:192
  16.7 0.1 collective-permute-done.2.refs_0_
  16.8 0.2 %collective-permute-done.4.refs_1_ = bf16[520,128]{1,0:T(8,128)(2,1)S(1)} collective-permute-done((bf16[520,128]{1,0:T(8,128)(2,1)S(1)}, bf16[520,128]{1,0:T(8,128)(2,1)S(1)}, u32[]{:S(2)}, u32[]{:S(2)}) %collective-permute-start.4) | collective-permute-done | bytes 133152 | tf_op jit(solution)/shard_map/ppermute | solution.py:227
  17.0 1.3 %finish.1 = bf16[64,2048]{1,0:T(8,128)(2,1)} custom-call(s32[2,64,128]{2,1,0:T(8,128)S(1)} %get-tuple-element.12.span_ref, bf16[64,2048]{1,0:T(8,128)(2,1)S(1)} %fetch.1.queries_ref, bf16[520,128]{1,0:T(8,128)(2,1)S(1)} %collective-permute-done.2.refs_0_, bf16[520,128]{1,0:T(8,128)(2,1)S(1)} %collective-permute-done.4.refs_1_, ...), custom_call_target="tpu_custom_call" | custom-call | flops 67108864 | bytes 524288 | tf_op jit(solution)/shard_map/finish/pallas_call | solution.py:192
Async XLA Ops:
  0.9 8.1 %collective-permute-start = (bf16[520,128]{1,0:T(8,128)(2,1)S(1)}, bf16[520,128]{1,0:T(8,128)(2,1)S(1)}, u32[]{:S(2)}, u32[]{:S(2)}) collective-permute-start(bf16[520,128]{1,0:T(8,128)(2,1)S(1)} %get-tuple-element.13.refs_0_), channel_id=1, source_target_pairs={{0,4},{1,7},{2,0},{3,5},{4,6},{5,1},{6,2},{7,3},{8,12},{9,15},{10,... | collective-permute-start | bytes 399368 | tf_op jit(solution)/shard_map/ppermute | solution.py:224
  5.0 10.5 %collective-permute-start.1 = (bf16[520,128]{1,0:T(8,128)(2,1)S(1)}, bf16[520,128]{1,0:T(8,128)(2,1)S(1)}, u32[]{:S(2)}, u32[]{:S(2)}) collective-permute-start(bf16[520,128]{1,0:T(8,128)(2,1)S(1)} %get-tuple-element.13.refs_0_), channel_id=1, source_target_pairs={{0,2},{1,5},{2,6},{3,7},{4,0},{5,3},{6,4},{7,1},{8,10},{9,13},{10,... | collective-permute-start | bytes 399368 | tf_op jit(solution)/shard_map/ppermute | solution.py:224
  5.0 10.5 %collective-permute-start.3 = (bf16[520,128]{1,0:T(8,128)(2,1)S(1)}, bf16[520,128]{1,0:T(8,128)(2,1)S(1)}, u32[]{:S(2)}, u32[]{:S(2)}) collective-permute-start(bf16[520,128]{1,0:T(8,128)(2,1)S(1)} %get-tuple-element.13.refs_0_), channel_id=1, source_target_pairs={{0,6},{1,3},{2,4},{3,1},{4,2},{5,7},{6,0},{7,5},{8,14},{9,11},{10,... | collective-permute-start | bytes 399368 | tf_op jit(solution)/shard_map/ppermute | solution.py:224
  8.1 7.9 %collective-permute-start.5 = (bf16[520,128]{1,0:T(8,128)(2,1)S(1)}, bf16[520,128]{1,0:T(8,128)(2,1)S(1)}, u32[]{:S(2)}, u32[]{:S(2)}) collective-permute-start(bf16[520,128]{1,0:T(8,128)(2,1)S(1)} %get-tuple-element.13.refs_0_), channel_id=1, source_target_pairs={{0,1},{1,0},{2,3},{3,2},{4,5},{5,4},{6,7},{7,6},{8,9},{9,8},{10,11... | collective-permute-start | bytes 399368 | tf_op jit(solution)/shard_map/ppermute | solution.py:227
  9.0 7.0 %collective-permute-start.6 = (bf16[520,128]{1,0:T(8,128)(2,1)S(1)}, bf16[520,128]{1,0:T(8,128)(2,1)S(1)}, u32[]{:S(2)}, u32[]{:S(2)}) collective-permute-start(bf16[520,128]{1,0:T(8,128)(2,1)S(1)} %collective-permute-done.refs_2_), channel_id=1, source_target_pairs={{0,1},{1,0},{2,3},{3,2},{4,5},{5,4},{6,7},{7,6},{8,9},{9,8},{10,11... | collective-permute-start | bytes 399368 | tf_op jit(solution)/shard_map/ppermute | solution.py:227
  15.5 1.4 %collective-permute-start.2 = (bf16[520,128]{1,0:T(8,128)(2,1)S(1)}, bf16[520,128]{1,0:T(8,128)(2,1)S(1)}, u32[]{:S(2)}, u32[]{:S(2)}) collective-permute-start(bf16[520,128]{1,0:T(8,128)(2,1)S(1)} %collective-permute-done.1.refs_3_), channel_id=1, source_target_pairs={{0,1},{1,0},{2,3},{3,2},{4,5},{5,4},{6,7},{7,6},{8,9},{9,8},{10,11... | collective-permute-start | bytes 399368 | tf_op jit(solution)/shard_map/ppermute | solution.py:227
  15.5 1.5 %collective-permute-start.4 = (bf16[520,128]{1,0:T(8,128)(2,1)S(1)}, bf16[520,128]{1,0:T(8,128)(2,1)S(1)}, u32[]{:S(2)}, u32[]{:S(2)}) collective-permute-start(bf16[520,128]{1,0:T(8,128)(2,1)S(1)} %collective-permute-done.3.refs_4_), channel_id=1, source_target_pairs={{0,1},{1,0},{2,3},{3,2},{4,5},{5,4},{6,7},{7,6},{8,9},{9,8},{10,11... | collective-permute-start | bytes 399368 | tf_op jit(solution)/shard_map/ppermute | solution.py:227

commit v8 on v7

--- a/solution.py
+++ b/solution.py
@@ -240,7 +240,7 @@
     return attend(span, rows, late[len(late) % 2 :], state, True)
 
 
-ROUTES = (((2, 0, 3, 1), (3, 2, 0, 1)), ((1, 3, 0, 2), (2, 3, 1, 0)), ((3, 2, 1, 0), (1, 0, 3, 2)))
+ROUTES = (((2, 3, 0, 1), (3, 2, 0, 1)), ((1, 0, 3, 2), (1, 0, 3, 2)), ((3, 2, 1, 0), (2, 3, 1, 0)))
 
 
 def solution(mesh):

time: 18.5 us -> 18.6 us (level)
  waiting for transfers between devices: 5.18 us -> 8.3 us
  starting transfers between devices: 9.22 us -> 6.18 us
    ppermute x3, waiting for transfers between devices: 4.88 us -> 8.01 us  [along(): return lax.ppermute(array, 'ctx', pairs)]
    ppermute x4, starting transfers between devices: 2.09 us -> 0.52 us  [across(): return lax.ppermute(array, 'ctx', other_core)]
    ppermute x3, starting transfers between devices: 7.13 us -> 5.67 us  [along(): return lax.ppermute(array, 'ctx', pairs)]
  transfers between devices with their start and end apart: 7 -> 7, of which waited for: 3 -> 4; matrix products, arithmetic and copies ran while one was open for 0% -> 0% of each run, Pallas kernels for 9% -> 9%
where the time goes in v8:
time: 18.6 us; the launch traced here: 18.4 us
  waiting for transfers between devices  8.3 us (45%)
  starting transfers between devices  6.18 us (33%)
  Pallas kernels  3.87 us (21%)
    ppermute x3, waiting for transfers between devices, along(): return lax.ppermute(array, 'ctx', pairs)  8.01 us
    ppermute x3, starting transfers between devices, along(): return lax.ppermute(array, 'ctx', pairs)  5.67 us
    pallas_call x2, Pallas kernels, attend(): pl.pallas_call(partial(attend_kernel, len(parts), not state, last), out_s...  1.99 us
    pallas_call x1, Pallas kernels, fetch(): pl.pallas_call(fetch_kernel, out_shape=pltpu.VMEM(queries.shape, queries....  0.96 us
    pallas_call x1, Pallas kernels, pack(): pl.pallas_call(pack_kernel, out_shape=(pltpu.VMEM((2 * half + TAG, HD), k...  0.92 us
    ppermute x4, starting transfers between devices, across(): return lax.ppermute(array, 'ctx', other_core)  0.52 us
  transfers between devices with their start and end apart: 7, of which 4 were waited for; matrix products, arithmetic and copies ran while one was open for 0% of the time, Pallas kernels for 9%

profile of v8, /device:TPU:0, one launch (start us, length us, event | category | flops | bytes accessed | tf_op | source)
XLA Modules:
  0.0 18.4 jit_solution(12605040753380198891)
XLA Ops:
  0.0 0.9 %pack.1 = (bf16[520,128]{1,0:T(8,128)(2,1)S(1)}, s32[2,64,128]{2,1,0:T(8,128)S(1)}) custom-call(s32[2]{0:T(128)} %order_ref.1, s32[4]{0:T(128)} %lengths_ref.1, bf16[64,512]{1,0:T(8,128)(2,1)} %keys_ref.1, bf16[64,512]{1,0:T(8,128)(2,1)} %values_ref.1), custom_call_target="tpu_custom_call" | custom-call | tf_op jit(solution)/shard_map/pack/pallas_call | solution.py:65
  0.9 4.1 %collective-permute-start = (bf16[520,128]{1,0:T(8,128)(2,1)S(1)}, bf16[520,128]{1,0:T(8,128)(2,1)S(1)}, u32[]{:S(2)}, u32[]{:S(2)}) collective-permute-start(bf16[520,128]{1,0:T(8,128)(2,1)S(1)} %get-tuple-element.13.refs_0_), channel_id=1, source_target_pairs={{0,4},{1,7},{2,6},{3,5},{4,0},{5,1},{6,2},{7,3},{8,12},{9,15},{10,... | collective-permute-start | bytes 399368 | tf_op jit(solution)/shard_map/ppermute | solution.py:224
  5.0 1.6 %collective-permute-start.1 = (bf16[520,128]{1,0:T(8,128)(2,1)S(1)}, bf16[520,128]{1,0:T(8,128)(2,1)S(1)}, u32[]{:S(2)}, u32[]{:S(2)}) collective-permute-start(bf16[520,128]{1,0:T(8,128)(2,1)S(1)} %get-tuple-element.13.refs_0_), channel_id=1, source_target_pairs={{0,2},{1,3},{2,0},{3,1},{4,6},{5,7},{6,4},{7,5},{8,10},{9,11},{10,... | collective-permute-start | bytes 399368 | tf_op jit(solution)/shard_map/ppermute | solution.py:224
  6.6 0.0 collective-permute-start.3
  6.6 0.0 collective-permute-start.5
  6.6 1.0 %fetch.1.queries_ref = bf16[64,2048]{1,0:T(8,128)(2,1)S(1)} custom-call(bf16[64,2048]{1,0:T(8,128)(2,1)} %queries_ref.1), custom_call_target="tpu_custom_call" | custom-call | bytes 2097152 | tf_op jit(solution)/shard_map/fetch/pallas_call | solution.py:89
  7.6 5.5 %collective-permute-done.refs_2_ = bf16[520,128]{1,0:T(8,128)(2,1)S(1)} collective-permute-done((bf16[520,128]{1,0:T(8,128)(2,1)S(1)}, bf16[520,128]{1,0:T(8,128)(2,1)S(1)}, u32[]{:S(2)}, u32[]{:S(2)}) %collective-permute-start) | collective-permute-done | bytes 133152 | tf_op jit(solution)/shard_map/ppermute | solution.py:224
  13.1 0.0 collective-permute-start.6
  13.1 2.5 %collective-permute-done.1.refs_3_ = bf16[520,128]{1,0:T(8,128)(2,1)S(1)} collective-permute-done((bf16[520,128]{1,0:T(8,128)(2,1)S(1)}, bf16[520,128]{1,0:T(8,128)(2,1)S(1)}, u32[]{:S(2)}, u32[]{:S(2)}) %collective-permute-start.1) | collective-permute-done | bytes 133152 | tf_op jit(solution)/shard_map/ppermute | solution.py:224
  15.6 0.0 collective-permute-start.2
  15.6 0.0 collective-permute-done.3.refs_4_
  15.6 0.5 %collective-permute-start.4 = (bf16[520,128]{1,0:T(8,128)(2,1)S(1)}, bf16[520,128]{1,0:T(8,128)(2,1)S(1)}, u32[]{:S(2)}, u32[]{:S(2)}) collective-permute-start(bf16[520,128]{1,0:T(8,128)(2,1)S(1)} %collective-permute-done.3.refs_4_), channel_id=1, source_target_pairs={{0,1},{1,0},{2,3},{3,2},{4,5},{5,4},{6,7},{7,6},{8,9},{9,8},{10,11... | collective-permute-start | bytes 399368 | tf_op jit(solution)/shard_map/ppermute | solution.py:227
  16.1 0.0 collective-permute-done.5.refs_1_
  16.1 0.0 collective-permute-done.6.refs_5_
  16.1 0.7 %begin.1 = (f32[4,256,128]{2,1,0:T(8,128)S(1)}, f32[4,256,128]{2,1,0:T(8,128)S(1)}, f32[4,256,128]{2,1,0:T(8,128)S(1)}) custom-call(s32[2,64,128]{2,1,0:T(8,128)S(1)} %get-tuple-element.12.span_ref, bf16[64,2048]{1,0:T(8,128)(2,1)S(1)} %fetch.1.queries_ref, bf16[520,128]{1,0:T(8,128)(2,1)S(1)} %get-tuple-element.13.refs_0_, ...), custom_call_target="tpu_custom_call" | custom-call | flops 201326592 | bytes 1572864 | tf_op jit(solution)/shard_map/begin/pallas_call | solution.py:192
  16.8 0.1 collective-permute-done.2.refs_0_
  16.9 0.2 %collective-permute-done.4.refs_1_ = bf16[520,128]{1,0:T(8,128)(2,1)S(1)} collective-permute-done((bf16[520,128]{1,0:T(8,128)(2,1)S(1)}, bf16[520,128]{1,0:T(8,128)(2,1)S(1)}, u32[]{:S(2)}, u32[]{:S(2)}) %collective-permute-start.4) | collective-permute-done | bytes 133152 | tf_op jit(solution)/shard_map/ppermute | solution.py:227
  17.1 1.3 %finish.1 = bf16[64,2048]{1,0:T(8,128)(2,1)} custom-call(s32[2,64,128]{2,1,0:T(8,128)S(1)} %get-tuple-element.12.span_ref, bf16[64,2048]{1,0:T(8,128)(2,1)S(1)} %fetch.1.queries_ref, bf16[520,128]{1,0:T(8,128)(2,1)S(1)} %collective-permute-done.2.refs_0_, bf16[520,128]{1,0:T(8,128)(2,1)S(1)} %collective-permute-done.4.refs_1_, ...), custom_call_target="tpu_custom_call" | custom-call | flops 67108864 | bytes 524288 | tf_op jit(solution)/shard_map/finish/pallas_call | solution.py:192
Async XLA Ops:
  0.9 12.1 %collective-permute-start = (bf16[520,128]{1,0:T(8,128)(2,1)S(1)}, bf16[520,128]{1,0:T(8,128)(2,1)S(1)}, u32[]{:S(2)}, u32[]{:S(2)}) collective-permute-start(bf16[520,128]{1,0:T(8,128)(2,1)S(1)} %get-tuple-element.13.refs_0_), channel_id=1, source_target_pairs={{0,4},{1,7},{2,6},{3,5},{4,0},{5,1},{6,2},{7,3},{8,12},{9,15},{10,... | collective-permute-start | bytes 399368 | tf_op jit(solution)/shard_map/ppermute | solution.py:224
  5.0 10.6 %collective-permute-start.1 = (bf16[520,128]{1,0:T(8,128)(2,1)S(1)}, bf16[520,128]{1,0:T(8,128)(2,1)S(1)}, u32[]{:S(2)}, u32[]{:S(2)}) collective-permute-start(bf16[520,128]{1,0:T(8,128)(2,1)S(1)} %get-tuple-element.13.refs_0_), channel_id=1, source_target_pairs={{0,2},{1,3},{2,0},{3,1},{4,6},{5,7},{6,4},{7,5},{8,10},{9,11},{10,... | collective-permute-start | bytes 399368 | tf_op jit(solution)/shard_map/ppermute | solution.py:224
  6.6 9.0 %collective-permute-start.3 = (bf16[520,128]{1,0:T(8,128)(2,1)S(1)}, bf16[520,128]{1,0:T(8,128)(2,1)S(1)}, u32[]{:S(2)}, u32[]{:S(2)}) collective-permute-start(bf16[520,128]{1,0:T(8,128)(2,1)S(1)} %get-tuple-element.13.refs_0_), channel_id=1, source_target_pairs={{0,6},{1,5},{2,4},{3,7},{4,2},{5,3},{6,0},{7,1},{8,14},{9,13},{10,... | collective-permute-start | bytes 399368 | tf_op jit(solution)/shard_map/ppermute | solution.py:224
  6.6 9.5 %collective-permute-start.5 = (bf16[520,128]{1,0:T(8,128)(2,1)S(1)}, bf16[520,128]{1,0:T(8,128)(2,1)S(1)}, u32[]{:S(2)}, u32[]{:S(2)}) collective-permute-start(bf16[520,128]{1,0:T(8,128)(2,1)S(1)} %get-tuple-element.13.refs_0_), channel_id=1, source_target_pairs={{0,1},{1,0},{2,3},{3,2},{4,5},{5,4},{6,7},{7,6},{8,9},{9,8},{10,11... | collective-permute-start | bytes 399368 | tf_op jit(solution)/shard_map/ppermute | solution.py:227
  13.1 3.0 %collective-permute-start.6 = (bf16[520,128]{1,0:T(8,128)(2,1)S(1)}, bf16[520,128]{1,0:T(8,128)(2,1)S(1)}, u32[]{:S(2)}, u32[]{:S(2)}) collective-permute-start(bf16[520,128]{1,0:T(8,128)(2,1)S(1)} %collective-permute-done.refs_2_), channel_id=1, source_target_pairs={{0,1},{1,0},{2,3},{3,2},{4,5},{5,4},{6,7},{7,6},{8,9},{9,8},{10,11... | collective-permute-start | bytes 399368 | tf_op jit(solution)/shard_map/ppermute | solution.py:227
  15.6 1.4 %collective-permute-start.2 = (bf16[520,128]{1,0:T(8,128)(2,1)S(1)}, bf16[520,128]{1,0:T(8,128)(2,1)S(1)}, u32[]{:S(2)}, u32[]{:S(2)}) collective-permute-start(bf16[520,128]{1,0:T(8,128)(2,1)S(1)} %collective-permute-done.1.refs_3_), channel_id=1, source_target_pairs={{0,1},{1,0},{2,3},{3,2},{4,5},{5,4},{6,7},{7,6},{8,9},{9,8},{10,11... | collective-permute-start | bytes 399368 | tf_op jit(solution)/shard_map/ppermute | solution.py:227
  15.6 1.5 %collective-permute-start.4 = (bf16[520,128]{1,0:T(8,128)(2,1)S(1)}, bf16[520,128]{1,0:T(8,128)(2,1)S(1)}, u32[]{:S(2)}, u32[]{:S(2)}) collective-permute-start(bf16[520,128]{1,0:T(8,128)(2,1)S(1)} %collective-permute-done.3.refs_4_), channel_id=1, source_target_pairs={{0,1},{1,0},{2,3},{3,2},{4,5},{5,4},{6,7},{7,6},{8,9},{9,8},{10,11... | collective-permute-start | bytes 399368 | tf_op jit(solution)/shard_map/ppermute | solution.py:227

commit v9 on v8

--- a/solution.py
+++ b/solution.py
@@ -240,7 +240,7 @@
     return attend(span, rows, late[len(late) % 2 :], state, True)
 
 
-ROUTES = (((2, 3, 0, 1), (3, 2, 0, 1)), ((1, 0, 3, 2), (1, 0, 3, 2)), ((3, 2, 1, 0), (2, 3, 1, 0)))
+ROUTES = (((1, 3, 0, 2), (3, 2, 0, 1)), ((2, 0, 3, 1), (2, 3, 1, 0)), ((3, 2, 1, 0), (1, 0, 3, 2)))
 
 
 def solution(mesh):

time: 18.6 us -> 18.6 us (level)
  starting transfers between devices: 6.18 us -> 8.04 us
  waiting for transfers between devices: 8.3 us -> 6.45 us
    ppermute x3, starting transfers between devices: 5.67 us -> 8.03 us  [along(): return lax.ppermute(array, 'ctx', pairs)]
    ppermute x3, waiting for transfers between devices: 8.01 us -> 5.85 us  [along(): return lax.ppermute(array, 'ctx', pairs)]
    ppermute x4, starting transfers between devices: 0.52 us -> 0.01 us  [across(): return lax.ppermute(array, 'ctx', other_core)]
    ppermute x4, waiting for transfers between devices: 0.29 us -> 0.61 us  [across(): return lax.ppermute(array, 'ctx', other_core)]
where the time goes in v9:
time: 18.6 us; the launch traced here: 18.4 us
  starting transfers between devices  8.04 us (43%)
  waiting for transfers between devices  6.45 us (35%)
  Pallas kernels  3.87 us (21%)
    ppermute x3, starting transfers between devices, along(): return lax.ppermute(array, 'ctx', pairs)  8.03 us
    ppermute x3, waiting for transfers between devices, along(): return lax.ppermute(array, 'ctx', pairs)  5.85 us
    pallas_call x2, Pallas kernels, attend(): pl.pallas_call(partial(attend_kernel, len(parts), not state, last), out_s...  1.99 us
    pallas_call x1, Pallas kernels, fetch(): pl.pallas_call(fetch_kernel, out_shape=pltpu.VMEM(queries.shape, queries....  0.96 us
    pallas_call x1, Pallas kernels, pack(): pl.pallas_call(pack_kernel, out_shape=(pltpu.VMEM((2 * half + TAG, HD), k...  0.92 us
    ppermute x4, waiting for transfers between devices, across(): return lax.ppermute(array, 'ctx', other_core)  0.61 us
  transfers between devices with their start and end apart: 7, of which 4 were waited for; matrix products, arithmetic and copies ran while one was open for 0% of the time, Pallas kernels for 9%

profile of v9, /device:TPU:0, one launch (start us, length us, event | category | flops | bytes accessed | tf_op | source)
XLA Modules:
  0.0 18.4 jit_solution(13062516051561380786)
XLA Ops:
  0.0 0.9 %pack.1 = (bf16[520,128]{1,0:T(8,128)(2,1)S(1)}, s32[2,64,128]{2,1,0:T(8,128)S(1)}) custom-call(s32[2]{0:T(128)} %order_ref.1, s32[4]{0:T(128)} %lengths_ref.1, bf16[64,512]{1,0:T(8,128)(2,1)} %keys_ref.1, bf16[64,512]{1,0:T(8,128)(2,1)} %values_ref.1), custom_call_target="tpu_custom_call" | custom-call | tf_op jit(solution)/shard_map/pack/pallas_call | solution.py:65
  0.9 3.1 %collective-permute-start = (bf16[520,128]{1,0:T(8,128)(2,1)S(1)}, bf16[520,128]{1,0:T(8,128)(2,1)S(1)}, u32[]{:S(2)}, u32[]{:S(2)}) collective-permute-start(bf16[520,128]{1,0:T(8,128)(2,1)S(1)} %get-tuple-element.13.refs_0_), channel_id=1, source_target_pairs={{0,2},{1,7},{2,6},{3,5},{4,0},{5,1},{6,4},{7,3},{8,10},{9,15},{10,... | collective-permute-start | bytes 399368 | tf_op jit(solution)/shard_map/ppermute | solution.py:224
  4.0 1.1 %collective-permute-start.1 = (bf16[520,128]{1,0:T(8,128)(2,1)S(1)}, bf16[520,128]{1,0:T(8,128)(2,1)S(1)}, u32[]{:S(2)}, u32[]{:S(2)}) collective-permute-start(bf16[520,128]{1,0:T(8,128)(2,1)S(1)} %get-tuple-element.13.refs_0_), channel_id=1, source_target_pairs={{0,4},{1,5},{2,0},{3,7},{4,6},{5,3},{6,2},{7,1},{8,12},{9,13},{10,... | collective-permute-start | bytes 399368 | tf_op jit(solution)/shard_map/ppermute | solution.py:224
  5.1 3.9 %collective-permute-start.3 = (bf16[520,128]{1,0:T(8,128)(2,1)S(1)}, bf16[520,128]{1,0:T(8,128)(2,1)S(1)}, u32[]{:S(2)}, u32[]{:S(2)}) collective-permute-start(bf16[520,128]{1,0:T(8,128)(2,1)S(1)} %get-tuple-element.13.refs_0_), channel_id=1, source_target_pairs={{0,6},{1,3},{2,4},{3,1},{4,2},{5,7},{6,0},{7,5},{8,14},{9,11},{10,... | collective-permute-start | bytes 399368 | tf_op jit(solution)/shard_map/ppermute | solution.py:224
  9.0 0.0 collective-permute-start.5
  9.0 1.0 %fetch.1.queries_ref = bf16[64,2048]{1,0:T(8,128)(2,1)S(1)} custom-call(bf16[64,2048]{1,0:T(8,128)(2,1)} %queries_ref.1), custom_call_target="tpu_custom_call" | custom-call | bytes 2097152 | tf_op jit(solution)/shard_map/fetch/pallas_call | solution.py:89
  9.9 4.1 %collective-permute-done.refs_2_ = bf16[520,128]{1,0:T(8,128)(2,1)S(1)} collective-permute-done((bf16[520,128]{1,0:T(8,128)(2,1)S(1)}, bf16[520,128]{1,0:T(8,128)(2,1)S(1)}, u32[]{:S(2)}, u32[]{:S(2)}) %collective-permute-start) | collective-permute-done | bytes 133152 | tf_op jit(solution)/shard_map/ppermute | solution.py:224
  14.0 0.0 collective-permute-start.6
  14.0 0.8 %collective-permute-done.1.refs_3_ = bf16[520,128]{1,0:T(8,128)(2,1)S(1)} collective-permute-done((bf16[520,128]{1,0:T(8,128)(2,1)S(1)}, bf16[520,128]{1,0:T(8,128)(2,1)S(1)}, u32[]{:S(2)}, u32[]{:S(2)}) %collective-permute-start.1) | collective-permute-done | bytes 133152 | tf_op jit(solution)/shard_map/ppermute | solution.py:224
  14.8 0.0 collective-permute-start.2
  14.8 1.0 %collective-permute-done.3.refs_4_ = bf16[520,128]{1,0:T(8,128)(2,1)S(1)} collective-permute-done((bf16[520,128]{1,0:T(8,128)(2,1)S(1)}, bf16[520,128]{1,0:T(8,128)(2,1)S(1)}, u32[]{:S(2)}, u32[]{:S(2)}) %collective-permute-start.3) | collective-permute-done | bytes 133152 | tf_op jit(solution)/shard_map/ppermute | solution.py:224
  15.8 0.0 collective-permute-start.4
  15.8 0.0 collective-permute-done.5.refs_1_
  15.8 0.0 collective-permute-done.6.refs_5_
  15.8 0.7 %begin.1 = (f32[4,256,128]{2,1,0:T(8,128)S(1)}, f32[4,256,128]{2,1,0:T(8,128)S(1)}, f32[4,256,128]{2,1,0:T(8,128)S(1)}) custom-call(s32[2,64,128]{2,1,0:T(8,128)S(1)} %get-tuple-element.12.span_ref, bf16[64,2048]{1,0:T(8,128)(2,1)S(1)} %fetch.1.queries_ref, bf16[520,128]{1,0:T(8,128)(2,1)S(1)} %get-tuple-element.13.refs_0_, ...), custom_call_target="tpu_custom_call" | custom-call | flops 201326592 | bytes 1572864 | tf_op jit(solution)/shard_map/begin/pallas_call | solution.py:192
  16.5 0.0 collective-permute-done.2.refs_0_
  16.5 0.6 %collective-permute-done.4.refs_1_ = bf16[520,128]{1,0:T(8,128)(2,1)S(1)} collective-permute-done((bf16[520,128]{1,0:T(8,128)(2,1)S(1)}, bf16[520,128]{1,0:T(8,128)(2,1)S(1)}, u32[]{:S(2)}, u32[]{:S(2)}) %collective-permute-start.4) | collective-permute-done | bytes 133152 | tf_op jit(solution)/shard_map/ppermute | solution.py:227
  17.1 1.3 %finish.1 = bf16[64,2048]{1,0:T(8,128)(2,1)} custom-call(s32[2,64,128]{2,1,0:T(8,128)S(1)} %get-tuple-element.12.span_ref, bf16[64,2048]{1,0:T(8,128)(2,1)S(1)} %fetch.1.queries_ref, bf16[520,128]{1,0:T(8,128)(2,1)S(1)} %collective-permute-done.2.refs_0_, bf16[520,128]{1,0:T(8,128)(2,1)S(1)} %collective-permute-done.4.refs_1_, ...), custom_call_target="tpu_custom_call" | custom-call | flops 67108864 | bytes 524288 | tf_op jit(solution)/shard_map/finish/pallas_call | solution.py:192
Async XLA Ops:
  0.9 13.1 %collective-permute-start = (bf16[520,128]{1,0:T(8,128)(2,1)S(1)}, bf16[520,128]{1,0:T(8,128)(2,1)S(1)}, u32[]{:S(2)}, u32[]{:S(2)}) collective-permute-start(bf16[520,128]{1,0:T(8,128)(2,1)S(1)} %get-tuple-element.13.refs_0_), channel_id=1, source_target_pairs={{0,2},{1,7},{2,6},{3,5},{4,0},{5,1},{6,4},{7,3},{8,10},{9,15},{10,... | collective-permute-start | bytes 399368 | tf_op jit(solution)/shard_map/ppermute | solution.py:224
  4.0 10.8 %collective-permute-start.1 = (bf16[520,128]{1,0:T(8,128)(2,1)S(1)}, bf16[520,128]{1,0:T(8,128)(2,1)S(1)}, u32[]{:S(2)}, u32[]{:S(2)}) collective-permute-start(bf16[520,128]{1,0:T(8,128)(2,1)S(1)} %get-tuple-element.13.refs_0_), channel_id=1, source_target_pairs={{0,4},{1,5},{2,0},{3,7},{4,6},{5,3},{6,2},{7,1},{8,12},{9,13},{10,... | collective-permute-start | bytes 399368 | tf_op jit(solution)/shard_map/ppermute | solution.py:224
  5.1 10.7 %collective-permute-start.3 = (bf16[520,128]{1,0:T(8,128)(2,1)S(1)}, bf16[520,128]{1,0:T(8,128)(2,1)S(1)}, u32[]{:S(2)}, u32[]{:S(2)}) collective-permute-start(bf16[520,128]{1,0:T(8,128)(2,1)S(1)} %get-tuple-element.13.refs_0_), channel_id=1, source_target_pairs={{0,6},{1,3},{2,4},{3,1},{4,2},{5,7},{6,0},{7,5},{8,14},{9,11},{10,... | collective-permute-start | bytes 399368 | tf_op jit(solution)/shard_map/ppermute | solution.py:224
  9.0 6.8 %collective-permute-start.5 = (bf16[520,128]{1,0:T(8,128)(2,1)S(1)}, bf16[520,128]{1,0:T(8,128)(2,1)S(1)}, u32[]{:S(2)}, u32[]{:S(2)}) collective-permute-start(bf16[520,128]{1,0:T(8,128)(2,1)S(1)} %get-tuple-element.13.refs_0_), channel_id=1, source_target_pairs={{0,1},{1,0},{2,3},{3,2},{4,5},{5,4},{6,7},{7,6},{8,9},{9,8},{10,11... | collective-permute-start | bytes 399368 | tf_op jit(solution)/shard_map/ppermute | solution.py:227
  14.0 1.8 %collective-permute-start.6 = (bf16[520,128]{1,0:T(8,128)(2,1)S(1)}, bf16[520,128]{1,0:T(8,128)(2,1)S(1)}, u32[]{:S(2)}, u32[]{:S(2)}) collective-permute-start(bf16[520,128]{1,0:T(8,128)(2,1)S(1)} %collective-permute-done.refs_2_), channel_id=1, source_target_pairs={{0,1},{1,0},{2,3},{3,2},{4,5},{5,4},{6,7},{7,6},{8,9},{9,8},{10,11... | collective-permute-start | bytes 399368 | tf_op jit(solution)/shard_map/ppermute | solution.py:227
  14.8 1.7 %collective-permute-start.2 = (bf16[520,128]{1,0:T(8,128)(2,1)S(1)}, bf16[520,128]{1,0:T(8,128)(2,1)S(1)}, u32[]{:S(2)}, u32[]{:S(2)}) collective-permute-start(bf16[520,128]{1,0:T(8,128)(2,1)S(1)} %collective-permute-done.1.refs_3_), channel_id=1, source_target_pairs={{0,1},{1,0},{2,3},{3,2},{4,5},{5,4},{6,7},{7,6},{8,9},{9,8},{10,11... | collective-permute-start | bytes 399368 | tf_op jit(solution)/shard_map/ppermute | solution.py:227
  15.8 1.4 %collective-permute-start.4 = (bf16[520,128]{1,0:T(8,128)(2,1)S(1)}, bf16[520,128]{1,0:T(8,128)(2,1)S(1)}, u32[]{:S(2)}, u32[]{:S(2)}) collective-permute-start(bf16[520,128]{1,0:T(8,128)(2,1)S(1)} %collective-permute-done.3.refs_4_), channel_id=1, source_target_pairs={{0,1},{1,0},{2,3},{3,2},{4,5},{5,4},{6,7},{7,6},{8,9},{9,8},{10,11... | collective-permute-start | bytes 399368 | tf_op jit(solution)/shard_map/ppermute | solution.py:227

commit v10 on v9

--- a/solution.py
+++ b/solution.py
@@ -240,7 +240,7 @@
     return attend(span, rows, late[len(late) % 2 :], state, True)
 
 
-ROUTES = (((1, 3, 0, 2), (3, 2, 0, 1)), ((2, 0, 3, 1), (2, 3, 1, 0)), ((3, 2, 1, 0), (1, 0, 3, 2)))
+ROUTES = (((2, 3, 0, 1), (3, 2, 0, 1)), ((1, 2, 3, 0), (2, 3, 1, 0)), ((3, 0, 1, 2), (1, 0, 3, 2)))
 
 
 def solution(mesh):

time: 18.6 us -> 18.7 us (level)
  starting transfers between devices: 8.04 us -> 8.46 us
  waiting for transfers between devices: 6.45 us -> 6.13 us
    ppermute x4, starting transfers between devices: 0.01 us -> 0.55 us  [across(): return lax.ppermute(array, 'ctx', other_core)]
    ppermute x3, waiting for transfers between devices: 5.85 us -> 5.37 us  [along(): return lax.ppermute(array, 'ctx', pairs)]
  transfers between devices with their start and end apart: 7 -> 7, of which waited for: 4 -> 2; matrix products, arithmetic and copies ran while one was open for 0% -> 0% of each run, Pallas kernels for 9% -> 9%
where the time goes in v10:
time: 18.7 us; the launch traced here: 18.5 us
  starting transfers between devices  8.46 us (45%)
  waiting for transfers between devices  6.13 us (33%)
  Pallas kernels  3.87 us (21%)
    ppermute x3, starting transfers between devices, along(): return lax.ppermute(array, 'ctx', pairs)  7.91 us
    ppermute x3, waiting for transfers between devices, along(): return lax.ppermute(array, 'ctx', pairs)  5.37 us
    pallas_call x2, Pallas kernels, attend(): pl.pallas_call(partial(attend_kernel, len(parts), not state, last), out_s...  1.99 us
    pallas_call x1, Pallas kernels, fetch(): pl.pallas_call(fetch_kernel, out_shape=pltpu.VMEM(queries.shape, queries....  0.96 us
    pallas_call x1, Pallas kernels, pack(): pl.pallas_call(pack_kernel, out_shape=(pltpu.VMEM((2 * half + TAG, HD), k...  0.92 us
    ppermute x4, waiting for transfers between devices, across(): return lax.ppermute(array, 'ctx', other_core)  0.77 us
    ppermute x4, starting transfers between devices, across(): return lax.ppermute(array, 'ctx', other_core)  0.55 us
  transfers between devices with their start and end apart: 7, of which 2 were waited for; matrix products, arithmetic and copies ran while one was open for 0% of the time, Pallas kernels for 9%

profile of v10, /device:TPU:0, one launch (start us, length us, event | category | flops | bytes accessed | tf_op | source)
XLA Modules:
  0.0 18.5 jit_solution(17692527981616419149)
XLA Ops:
  0.0 0.9 %pack.1 = (bf16[520,128]{1,0:T(8,128)(2,1)S(1)}, s32[2,64,128]{2,1,0:T(8,128)S(1)}) custom-call(s32[2]{0:T(128)} %order_ref.1, s32[4]{0:T(128)} %lengths_ref.1, bf16[64,512]{1,0:T(8,128)(2,1)} %keys_ref.1, bf16[64,512]{1,0:T(8,128)(2,1)} %values_ref.1), custom_call_target="tpu_custom_call" | custom-call | tf_op jit(solution)/shard_map/pack/pallas_call | solution.py:65
  0.9 4.1 %collective-permute-start = (bf16[520,128]{1,0:T(8,128)(2,1)S(1)}, bf16[520,128]{1,0:T(8,128)(2,1)S(1)}, u32[]{:S(2)}, u32[]{:S(2)}) collective-permute-start(bf16[520,128]{1,0:T(8,128)(2,1)S(1)} %get-tuple-element.13.refs_0_), channel_id=1, source_target_pairs={{0,4},{1,7},{2,6},{3,5},{4,0},{5,1},{6,2},{7,3},{8,12},{9,15},{10,... | collective-permute-start | bytes 399368 | tf_op jit(solution)/shard_map/ppermute | solution.py:224
  5.0 1.6 %collective-permute-start.1 = (bf16[520,128]{1,0:T(8,128)(2,1)S(1)}, bf16[520,128]{1,0:T(8,128)(2,1)S(1)}, u32[]{:S(2)}, u32[]{:S(2)}) collective-permute-start(bf16[520,128]{1,0:T(8,128)(2,1)S(1)} %get-tuple-element.13.refs_0_), channel_id=1, source_target_pairs={{0,2},{1,5},{2,4},{3,7},{4,6},{5,3},{6,0},{7,1},{8,10},{9,13},{10,... | collective-permute-start | bytes 399368 | tf_op jit(solution)/shard_map/ppermute | solution.py:224
  6.6 2.2 %collective-permute-start.3 = (bf16[520,128]{1,0:T(8,128)(2,1)S(1)}, bf16[520,128]{1,0:T(8,128)(2,1)S(1)}, u32[]{:S(2)}, u32[]{:S(2)}) collective-permute-start(bf16[520,128]{1,0:T(8,128)(2,1)S(1)} %get-tuple-element.13.refs_0_), channel_id=1, source_target_pairs={{0,6},{1,3},{2,0},{3,1},{4,2},{5,7},{6,4},{7,5},{8,14},{9,11},{10,... | collective-permute-start | bytes 399368 | tf_op jit(solution)/shard_map/ppermute | solution.py:224
  8.8 0.0 collective-permute-start.5
  8.8 1.0 %fetch.1.queries_ref = bf16[64,2048]{1,0:T(8,128)(2,1)S(1)} custom-call(bf16[64,2048]{1,0:T(8,128)(2,1)} %queries_ref.1), custom_call_target="tpu_custom_call" | custom-call | bytes 2097152 | tf_op jit(solution)/shard_map/fetch/pallas_call | solution.py:89
  9.8 5.3 %collective-permute-done.refs_2_ = bf16[520,128]{1,0:T(8,128)(2,1)S(1)} collective-permute-done((bf16[520,128]{1,0:T(8,128)(2,1)S(1)}, bf16[520,128]{1,0:T(8,128)(2,1)S(1)}, u32[]{:S(2)}, u32[]{:S(2)}) %collective-permute-start) | collective-permute-done | bytes 133152 | tf_op jit(solution)/shard_map/ppermute | solution.py:224
  15.1 0.0 collective-permute-start.6
  15.1 0.0 collective-permute-done.1.refs_3_
  15.1 0.5 %collective-permute-start.2 = (bf16[520,128]{1,0:T(8,128)(2,1)S(1)}, bf16[520,128]{1,0:T(8,128)(2,1)S(1)}, u32[]{:S(2)}, u32[]{:S(2)}) collective-permute-start(bf16[520,128]{1,0:T(8,128)(2,1)S(1)} %collective-permute-done.1.refs_3_), channel_id=1, source_target_pairs={{0,1},{1,0},{2,3},{3,2},{4,5},{5,4},{6,7},{7,6},{8,9},{9,8},{10,11... | collective-permute-start | bytes 399368 | tf_op jit(solution)/shard_map/ppermute | solution.py:227
  15.7 0.0 collective-permute-done.3.refs_4_
  15.7 0.0 collective-permute-start.4
  15.7 0.0 collective-permute-done.5.refs_1_
  15.7 0.8 %collective-permute-done.6.refs_5_ = bf16[520,128]{1,0:T(8,128)(2,1)S(1)} collective-permute-done((bf16[520,128]{1,0:T(8,128)(2,1)S(1)}, bf16[520,128]{1,0:T(8,128)(2,1)S(1)}, u32[]{:S(2)}, u32[]{:S(2)}) %collective-permute-start.6) | collective-permute-done | bytes 133152 | tf_op jit(solution)/shard_map/ppermute | solution.py:227
  16.5 0.7 %begin.1 = (f32[4,256,128]{2,1,0:T(8,128)S(1)}, f32[4,256,128]{2,1,0:T(8,128)S(1)}, f32[4,256,128]{2,1,0:T(8,128)S(1)}) custom-call(s32[2,64,128]{2,1,0:T(8,128)S(1)} %get-tuple-element.12.span_ref, bf16[64,2048]{1,0:T(8,128)(2,1)S(1)} %fetch.1.queries_ref, bf16[520,128]{1,0:T(8,128)(2,1)S(1)} %get-tuple-element.13.refs_0_, ...), custom_call_target="tpu_custom_call" | custom-call | flops 201326592 | bytes 1572864 | tf_op jit(solution)/shard_map/begin/pallas_call | solution.py:192
  17.2 0.0 collective-permute-done.2.refs_0_
  17.2 0.0 collective-permute-done.4.refs_1_
  17.2 1.3 %finish.1 = bf16[64,2048]{1,0:T(8,128)(2,1)} custom-call(s32[2,64,128]{2,1,0:T(8,128)S(1)} %get-tuple-element.12.span_ref, bf16[64,2048]{1,0:T(8,128)(2,1)S(1)} %fetch.1.queries_ref, bf16[520,128]{1,0:T(8,128)(2,1)S(1)} %collective-permute-done.2.refs_0_, bf16[520,128]{1,0:T(8,128)(2,1)S(1)} %collective-permute-done.4.refs_1_, ...), custom_call_target="tpu_custom_call" | custom-call | flops 67108864 | bytes 524288 | tf_op jit(solution)/shard_map/finish/pallas_call | solution.py:192
Async XLA Ops:
  0.9 14.2 %collective-permute-start = (bf16[520,128]{1,0:T(8,128)(2,1)S(1)}, bf16[520,128]{1,0:T(8,128)(2,1)S(1)}, u32[]{:S(2)}, u32[]{:S(2)}) collective-permute-start(bf16[520,128]{1,0:T(8,128)(2,1)S(1)} %get-tuple-element.13.refs_0_), channel_id=1, source_target_pairs={{0,4},{1,7},{2,6},{3,5},{4,0},{5,1},{6,2},{7,3},{8,12},{9,15},{10,... | collective-permute-start | bytes 399368 | tf_op jit(solution)/shard_map/ppermute | solution.py:224
  5.0 10.1 %collective-permute-start.1 = (bf16[520,128]{1,0:T(8,128)(2,1)S(1)}, bf16[520,128]{1,0:T(8,128)(2,1)S(1)}, u32[]{:S(2)}, u32[]{:S(2)}) collective-permute-start(bf16[520,128]{1,0:T(8,128)(2,1)S(1)} %get-tuple-element.13.refs_0_), channel_id=1, source_target_pairs={{0,2},{1,5},{2,4},{3,7},{4,6},{5,3},{6,0},{7,1},{8,10},{9,13},{10,... | collective-permute-start | bytes 399368 | tf_op jit(solution)/shard_map/ppermute | solution.py:224
  6.6 9.1 %collective-permute-start.3 = (bf16[520,128]{1,0:T(8,128)(2,1)S(1)}, bf16[520,128]{1,0:T(8,128)(2,1)S(1)}, u32[]{:S(2)}, u32[]{:S(2)}) collective-permute-start(bf16[520,128]{1,0:T(8,128)(2,1)S(1)} %get-tuple-element.13.refs_0_), channel_id=1, source_target_pairs={{0,6},{1,3},{2,0},{3,1},{4,2},{5,7},{6,4},{7,5},{8,14},{9,11},{10,... | collective-permute-start | bytes 399368 | tf_op jit(solution)/shard_map/ppermute | solution.py:224
  8.8 6.9 %collective-permute-start.5 = (bf16[520,128]{1,0:T(8,128)(2,1)S(1)}, bf16[520,128]{1,0:T(8,128)(2,1)S(1)}, u32[]{:S(2)}, u32[]{:S(2)}) collective-permute-start(bf16[520,128]{1,0:T(8,128)(2,1)S(1)} %get-tuple-element.13.refs_0_), channel_id=1, source_target_pairs={{0,1},{1,0},{2,3},{3,2},{4,5},{5,4},{6,7},{7,6},{8,9},{9,8},{10,11... | collective-permute-start | bytes 399368 | tf_op jit(solution)/shard_map/ppermute | solution.py:227
  15.1 1.4 %collective-permute-start.6 = (bf16[520,128]{1,0:T(8,128)(2,1)S(1)}, bf16[520,128]{1,0:T(8,128)(2,1)S(1)}, u32[]{:S(2)}, u32[]{:S(2)}) collective-permute-start(bf16[520,128]{1,0:T(8,128)(2,1)S(1)} %collective-permute-done.refs_2_), channel_id=1, source_target_pairs={{0,1},{1,0},{2,3},{3,2},{4,5},{5,4},{6,7},{7,6},{8,9},{9,8},{10,11... | collective-permute-start | bytes 399368 | tf_op jit(solution)/shard_map/ppermute | solution.py:227
  15.1 2.1 %collective-permute-start.2 = (bf16[520,128]{1,0:T(8,128)(2,1)S(1)}, bf16[520,128]{1,0:T(8,128)(2,1)S(1)}, u32[]{:S(2)}, u32[]{:S(2)}) collective-permute-start(bf16[520,128]{1,0:T(8,128)(2,1)S(1)} %collective-permute-done.1.refs_3_), channel_id=1, source_target_pairs={{0,1},{1,0},{2,3},{3,2},{4,5},{5,4},{6,7},{7,6},{8,9},{9,8},{10,11... | collective-permute-start | bytes 399368 | tf_op jit(solution)/shard_map/ppermute | solution.py:227
  15.7 1.5 %collective-permute-start.4 = (bf16[520,128]{1,0:T(8,128)(2,1)S(1)}, bf16[520,128]{1,0:T(8,128)(2,1)S(1)}, u32[]{:S(2)}, u32[]{:S(2)}) collective-permute-start(bf16[520,128]{1,0:T(8,128)(2,1)S(1)} %collective-permute-done.3.refs_4_), channel_id=1, source_target_pairs={{0,1},{1,0},{2,3},{3,2},{4,5},{5,4},{6,7},{7,6},{8,9},{9,8},{10,11... | collective-permute-start | bytes 399368 | tf_op jit(solution)/shard_map/ppermute | solution.py:227

commit v11 on v10

--- a/solution.py
+++ b/solution.py
@@ -240,7 +240,7 @@
     return attend(span, rows, late[len(late) % 2 :], state, True)
 
 
-ROUTES = (((2, 3, 0, 1), (3, 2, 0, 1)), ((1, 2, 3, 0), (2, 3, 1, 0)), ((3, 0, 1, 2), (1, 0, 3, 2)))
+ROUTES = (((1, 2, 3, 0), (3, 2, 0, 1)), ((2, 3, 0, 1), (1, 0, 3, 2)), ((3, 0, 1, 2), (2, 3, 1, 0)))
 
 
 def solution(mesh):

time: 18.7 us -> 18.5 us (0.989)
  starting transfers between devices: 8.46 us -> 7.53 us
  waiting for transfers between devices: 6.13 us -> 6.91 us
    ppermute x3, waiting for transfers between devices: 5.37 us -> 6.62 us  [along(): return lax.ppermute(array, 'ctx', pairs)]
    ppermute x3, starting transfers between devices: 7.91 us -> 7.01 us  [along(): return lax.ppermute(array, 'ctx', pairs)]
    ppermute x4, waiting for transfers between devices: 0.77 us -> 0.3 us  [across(): return lax.ppermute(array, 'ctx', other_core)]
  transfers between devices with their start and end apart: 7 -> 7, of which waited for: 2 -> 4; matrix products, arithmetic and copies ran while one was open for 0% -> 0% of each run, Pallas kernels for 9% -> 9%
where the time goes in v11:
time: 18.5 us; the launch traced here: 18.3 us
  starting transfers between devices  7.53 us (41%)
  waiting for transfers between devices  6.91 us (37%)
  Pallas kernels  3.87 us (21%)
    ppermute x3, starting transfers between devices, along(): return lax.ppermute(array, 'ctx', pairs)  7.01 us
    ppermute x3, waiting for transfers between devices, along(): return lax.ppermute(array, 'ctx', pairs)  6.62 us
    pallas_call x2, Pallas kernels, attend(): pl.pallas_call(partial(attend_kernel, len(parts), not state, last), out_s...  1.99 us
    pallas_call x1, Pallas kernels, fetch(): pl.pallas_call(fetch_kernel, out_shape=pltpu.VMEM(queries.shape, queries....  0.96 us
    pallas_call x1, Pallas kernels, pack(): pl.pallas_call(pack_kernel, out_shape=(pltpu.VMEM((2 * half + TAG, HD), k...  0.92 us
    ppermute x4, starting transfers between devices, across(): return lax.ppermute(array, 'ctx', other_core)  0.52 us
  transfers between devices with their start and end apart: 7, of which 4 were waited for; matrix products, arithmetic and copies ran while one was open for 0% of the time, Pallas kernels for 9%

profile of v11, /device:TPU:0, one launch (start us, length us, event | category | flops | bytes accessed | tf_op | source)
XLA Modules:
  0.0 18.3 jit_solution(72508023174703148)
XLA Ops:
  0.0 0.9 %pack.1 = (bf16[520,128]{1,0:T(8,128)(2,1)S(1)}, s32[2,64,128]{2,1,0:T(8,128)S(1)}) custom-call(s32[2]{0:T(128)} %order_ref.1, s32[4]{0:T(128)} %lengths_ref.1, bf16[64,512]{1,0:T(8,128)(2,1)} %keys_ref.1, bf16[64,512]{1,0:T(8,128)(2,1)} %values_ref.1), custom_call_target="tpu_custom_call" | custom-call | tf_op jit(solution)/shard_map/pack/pallas_call | solution.py:65
  0.9 3.1 %collective-permute-start = (bf16[520,128]{1,0:T(8,128)(2,1)S(1)}, bf16[520,128]{1,0:T(8,128)(2,1)S(1)}, u32[]{:S(2)}, u32[]{:S(2)}) collective-permute-start(bf16[520,128]{1,0:T(8,128)(2,1)S(1)} %get-tuple-element.13.refs_0_), channel_id=1, source_target_pairs={{0,2},{1,7},{2,4},{3,5},{4,6},{5,1},{6,0},{7,3},{8,10},{9,15},{10,... | collective-permute-start | bytes 399368 | tf_op jit(solution)/shard_map/ppermute | solution.py:224
  4.0 2.6 %collective-permute-start.1 = (bf16[520,128]{1,0:T(8,128)(2,1)S(1)}, bf16[520,128]{1,0:T(8,128)(2,1)S(1)}, u32[]{:S(2)}, u32[]{:S(2)}) collective-permute-start(bf16[520,128]{1,0:T(8,128)(2,1)S(1)} %get-tuple-element.13.refs_0_), channel_id=1, source_target_pairs={{0,4},{1,3},{2,6},{3,1},{4,0},{5,7},{6,2},{7,5},{8,12},{9,11},{10,... | collective-permute-start | bytes 399368 | tf_op jit(solution)/shard_map/ppermute | solution.py:224
  6.6 1.3 %collective-permute-start.3 = (bf16[520,128]{1,0:T(8,128)(2,1)S(1)}, bf16[520,128]{1,0:T(8,128)(2,1)S(1)}, u32[]{:S(2)}, u32[]{:S(2)}) collective-permute-start(bf16[520,128]{1,0:T(8,128)(2,1)S(1)} %get-tuple-element.13.refs_0_), channel_id=1, source_target_pairs={{0,6},{1,5},{2,0},{3,7},{4,2},{5,3},{6,4},{7,1},{8,14},{9,13},{10,... | collective-permute-start | bytes 399368 | tf_op jit(solution)/shard_map/ppermute | solution.py:224
  7.9 0.0 collective-permute-start.5
  8.0 1.0 %fetch.1.queries_ref = bf16[64,2048]{1,0:T(8,128)(2,1)S(1)} custom-call(bf16[64,2048]{1,0:T(8,128)(2,1)} %queries_ref.1), custom_call_target="tpu_custom_call" | custom-call | bytes 2097152 | tf_op jit(solution)/shard_map/fetch/pallas_call | solution.py:89
  8.9 1.5 %collective-permute-done.refs_2_ = bf16[520,128]{1,0:T(8,128)(2,1)S(1)} collective-permute-done((bf16[520,128]{1,0:T(8,128)(2,1)S(1)}, bf16[520,128]{1,0:T(8,128)(2,1)S(1)}, u32[]{:S(2)}, u32[]{:S(2)}) %collective-permute-start) | collective-permute-done | bytes 133152 | tf_op jit(solution)/shard_map/ppermute | solution.py:224
  10.4 0.0 collective-permute-start.6
  10.4 5.1 %collective-permute-done.1.refs_3_ = bf16[520,128]{1,0:T(8,128)(2,1)S(1)} collective-permute-done((bf16[520,128]{1,0:T(8,128)(2,1)S(1)}, bf16[520,128]{1,0:T(8,128)(2,1)S(1)}, u32[]{:S(2)}, u32[]{:S(2)}) %collective-permute-start.1) | collective-permute-done | bytes 133152 | tf_op jit(solution)/shard_map/ppermute | solution.py:224
  15.5 0.0 collective-permute-start.2
  15.5 0.0 collective-permute-done.3.refs_4_
  15.5 0.5 %collective-permute-start.4 = (bf16[520,128]{1,0:T(8,128)(2,1)S(1)}, bf16[520,128]{1,0:T(8,128)(2,1)S(1)}, u32[]{:S(2)}, u32[]{:S(2)}) collective-permute-start(bf16[520,128]{1,0:T(8,128)(2,1)S(1)} %collective-permute-done.3.refs_4_), channel_id=1, source_target_pairs={{0,1},{1,0},{2,3},{3,2},{4,5},{5,4},{6,7},{7,6},{8,9},{9,8},{10,11... | collective-permute-start | bytes 399368 | tf_op jit(solution)/shard_map/ppermute | solution.py:227
  16.0 0.0 collective-permute-done.5.refs_1_
  16.1 0.0 collective-permute-done.6.refs_5_
  16.1 0.7 %begin.1 = (f32[4,256,128]{2,1,0:T(8,128)S(1)}, f32[4,256,128]{2,1,0:T(8,128)S(1)}, f32[4,256,128]{2,1,0:T(8,128)S(1)}) custom-call(s32[2,64,128]{2,1,0:T(8,128)S(1)} %get-tuple-element.12.span_ref, bf16[64,2048]{1,0:T(8,128)(2,1)S(1)} %fetch.1.queries_ref, bf16[520,128]{1,0:T(8,128)(2,1)S(1)} %get-tuple-element.13.refs_0_, ...), custom_call_target="tpu_custom_call" | custom-call | flops 201326592 | bytes 1572864 | tf_op jit(solution)/shard_map/begin/pallas_call | solution.py:192
  16.8 0.1 collective-permute-done.2.refs_0_
  16.9 0.2 %collective-permute-done.4.refs_1_ = bf16[520,128]{1,0:T(8,128)(2,1)S(1)} collective-permute-done((bf16[520,128]{1,0:T(8,128)(2,1)S(1)}, bf16[520,128]{1,0:T(8,128)(2,1)S(1)}, u32[]{:S(2)}, u32[]{:S(2)}) %collective-permute-start.4) | collective-permute-done | bytes 133152 | tf_op jit(solution)/shard_map/ppermute | solution.py:227
  17.1 1.3 %finish.1 = bf16[64,2048]{1,0:T(8,128)(2,1)} custom-call(s32[2,64,128]{2,1,0:T(8,128)S(1)} %get-tuple-element.12.span_ref, bf16[64,2048]{1,0:T(8,128)(2,1)S(1)} %fetch.1.queries_ref, bf16[520,128]{1,0:T(8,128)(2,1)S(1)} %collective-permute-done.2.refs_0_, bf16[520,128]{1,0:T(8,128)(2,1)S(1)} %collective-permute-done.4.refs_1_, ...), custom_call_target="tpu_custom_call" | custom-call | flops 67108864 | bytes 524288 | tf_op jit(solution)/shard_map/finish/pallas_call | solution.py:192
Async XLA Ops:
  0.9 9.5 %collective-permute-start = (bf16[520,128]{1,0:T(8,128)(2,1)S(1)}, bf16[520,128]{1,0:T(8,128)(2,1)S(1)}, u32[]{:S(2)}, u32[]{:S(2)}) collective-permute-start(bf16[520,128]{1,0:T(8,128)(2,1)S(1)} %get-tuple-element.13.refs_0_), channel_id=1, source_target_pairs={{0,2},{1,7},{2,4},{3,5},{4,6},{5,1},{6,0},{7,3},{8,10},{9,15},{10,... | collective-permute-start | bytes 399368 | tf_op jit(solution)/shard_map/ppermute | solution.py:224
  4.0 11.5 %collective-permute-start.1 = (bf16[520,128]{1,0:T(8,128)(2,1)S(1)}, bf16[520,128]{1,0:T(8,128)(2,1)S(1)}, u32[]{:S(2)}, u32[]{:S(2)}) collective-permute-start(bf16[520,128]{1,0:T(8,128)(2,1)S(1)} %get-tuple-element.13.refs_0_), channel_id=1, source_target_pairs={{0,4},{1,3},{2,6},{3,1},{4,0},{5,7},{6,2},{7,5},{8,12},{9,11},{10,... | collective-permute-start | bytes 399368 | tf_op jit(solution)/shard_map/ppermute | solution.py:224
  6.6 8.9 %collective-permute-start.3 = (bf16[520,128]{1,0:T(8,128)(2,1)S(1)}, bf16[520,128]{1,0:T(8,128)(2,1)S(1)}, u32[]{:S(2)}, u32[]{:S(2)}) collective-permute-start(bf16[520,128]{1,0:T(8,128)(2,1)S(1)} %get-tuple-element.13.refs_0_), channel_id=1, source_target_pairs={{0,6},{1,5},{2,0},{3,7},{4,2},{5,3},{6,4},{7,1},{8,14},{9,13},{10,... | collective-permute-start | bytes 399368 | tf_op jit(solution)/shard_map/ppermute | solution.py:224
  7.9 8.1 %collective-permute-start.5 = (bf16[520,128]{1,0:T(8,128)(2,1)S(1)}, bf16[520,128]{1,0:T(8,128)(2,1)S(1)}, u32[]{:S(2)}, u32[]{:S(2)}) collective-permute-start(bf16[520,128]{1,0:T(8,128)(2,1)S(1)} %get-tuple-element.13.refs_0_), channel_id=1, source_target_pairs={{0,1},{1,0},{2,3},{3,2},{4,5},{5,4},{6,7},{7,6},{8,9},{9,8},{10,11... | collective-permute-start | bytes 399368 | tf_op jit(solution)/shard_map/ppermute | solution.py:227
  10.4 5.6 %collective-permute-start.6 = (bf16[520,128]{1,0:T(8,128)(2,1)S(1)}, bf16[520,128]{1,0:T(8,128)(2,1)S(1)}, u32[]{:S(2)}, u32[]{:S(2)}) collective-permute-start(bf16[520,128]{1,0:T(8,128)(2,1)S(1)} %collective-permute-done.refs_2_), channel_id=1, source_target_pairs={{0,1},{1,0},{2,3},{3,2},{4,5},{5,4},{6,7},{7,6},{8,9},{9,8},{10,11... | collective-permute-start | bytes 399368 | tf_op jit(solution)/shard_map/ppermute | solution.py:227
  15.5 1.4 %collective-permute-start.2 = (bf16[520,128]{1,0:T(8,128)(2,1)S(1)}, bf16[520,128]{1,0:T(8,128)(2,1)S(1)}, u32[]{:S(2)}, u32[]{:S(2)}) collective-permute-start(bf16[520,128]{1,0:T(8,128)(2,1)S(1)} %collective-permute-done.1.refs_3_), channel_id=1, source_target_pairs={{0,1},{1,0},{2,3},{3,2},{4,5},{5,4},{6,7},{7,6},{8,9},{9,8},{10,11... | collective-permute-start | bytes 399368 | tf_op jit(solution)/shard_map/ppermute | solution.py:227
  15.5 1.5 %collective-permute-start.4 = (bf16[520,128]{1,0:T(8,128)(2,1)S(1)}, bf16[520,128]{1,0:T(8,128)(2,1)S(1)}, u32[]{:S(2)}, u32[]{:S(2)}) collective-permute-start(bf16[520,128]{1,0:T(8,128)(2,1)S(1)} %collective-permute-done.3.refs_4_), channel_id=1, source_target_pairs={{0,1},{1,0},{2,3},{3,2},{4,5},{5,4},{6,7},{7,6},{8,9},{9,8},{10,11... | collective-permute-start | bytes 399368 | tf_op jit(solution)/shard_map/ppermute | solution.py:227
